TPU v7x, 32 devices: a whole 2x2x4 slice. The times are simulated.
32 devices in a mesh: row: 16 (over z, y, x), col: 2 (over core).
Axes of the slice: x: 2, y: 2, z: 4, core: 2. Of those that a mesh axis runs over, the one named last changes fastest.
Arguments:
- features: bfloat16 [128, 32, 16, 128], P('row', None, 'col'), may hold values from -6 to 6
- down_weight: bfloat16 [4, 4, 4, 32, 512], replicated, may hold values from -0.25 to 0.25
- bott_weight: bfloat16 [3, 3, 3, 512, 512], P(None, None, None, 'row'), may hold values from -0.078125 to 0.078125
- up_weight: bfloat16 [4, 4, 4, 32, 512], replicated, may hold values from -0.375 to 0.375
- dec_weight: bfloat16 [3, 3, 3, 32, 32], replicated, may hold values from -0.21875 to 0.21875
Outputs:
- decoded: bfloat16 [128, 32, 16, 128], P('row', None, 'col')
All inputs are finite; a program needn't handle non-finite values.
Results may differ from a plain program's by a relative error of at most 0.015.
Values may be sent and summed in bfloat16 or wider, within the bound.
No kernel may reach another device: no remote copies, remote signals or barrier semaphores. Data moves between devices by JAX's collectives and lax.ppermute only.
A program may use at most 128 MiB of HBM per device.

v0:
```python
import jax
import jax.numpy as jnp
from jax import lax
from jax.sharding import PartitionSpec as P


def with_halo(block, sides, width):
    for axis, dim in sides:
        count = lax.axis_size(axis)
        forward = [(i, i + 1) for i in range(count - 1)]
        backward = [(target, source) for source, target in forward]
        low = lax.ppermute(
            lax.slice_in_dim(block, block.shape[dim] - width, None, axis=dim), axis, forward
        )
        high = lax.ppermute(lax.slice_in_dim(block, 0, width, axis=dim), axis, backward)
        block = jnp.concatenate([low, block, high], axis=dim)
    return block


def convolve(padded, kernel):
    return lax.conv_general_dilated(
        padded[None],
        kernel,
        (1, 1, 1),
        ((0, 0), (0, 0), (1, 1)),
        dimension_numbers=("NDCHW", "DHWIO", "NDCHW"),
        preferred_element_type=jnp.float32,
    )[0]


def body(features, down_weight, bott_weight, up_weight, dec_weight):
    depth, chans, height, width = features.shape
    pooled = (
        features.astype(jnp.float32)
        .reshape(depth // 2, 2, chans, height // 2, 2, width // 2, 2)
        .mean(axis=(1, 4, 6))
        .astype(jnp.bfloat16)
    )
    blocks = pooled.reshape(depth // 8, 4, chans, height // 8, 4, width // 8, 4)
    lowered = jax.nn.silu(
        jnp.einsum("daihbwc,abcio->dohw", blocks, down_weight, preferred_element_type=jnp.float32)
    ).astype(jnp.bfloat16)
    regrouped = lax.all_to_all(lowered, "row", split_axis=1, concat_axis=0, tiled=True)
    rimmed = with_halo(regrouped, (("col", 2),), 1)
    deeper = jnp.pad(rimmed, ((1, 1), (0, 0), (0, 0), (0, 0)))
    summed = lax.psum_scatter(
        convolve(deeper, bott_weight).astype(jnp.bfloat16), "row", scatter_dimension=0, tiled=True
    ).astype(jnp.float32)
    middle = jax.nn.silu(summed).astype(jnp.bfloat16)
    raised = jnp.einsum(
        "dihw,abcoi->daohbwc", middle, up_weight, preferred_element_type=jnp.float32
    )
    raised = raised.reshape(depth // 2, chans, height // 2, width // 2)
    raised = jnp.repeat(jnp.repeat(jnp.repeat(raised, 2, axis=0), 2, axis=2), 2, axis=3)
    joined = (features.astype(jnp.float32) + raised).astype(jnp.bfloat16)
    rimmed_joined = with_halo(joined, (("row", 0), ("col", 2)), 1)
    return jax.nn.silu(convolve(rimmed_joined, dec_weight)).astype(jnp.bfloat16)


def solution(mesh):
    placed = (P("row", None, "col", None), P(), P(None, None, None, "row", None), P(), P())
    return jax.shard_map(
        body, mesh=mesh, in_specs=placed, out_specs=P("row", None, "col", None), check_vma=False
    )
```

profile of v0, /device:TPU:0, one launch (start us, length us, event | category | flops | bytes accessed | tf_op | source)
XLA Modules:
  0.0 193.9 jit_solution(16733433186388117384)
XLA Ops:
  6.5 0.0 copy-start
  6.5 0.0 reduce-scatter.2.cloned.1.call-start
  6.5 3.5 %copy.102 = bf16[8,32,8,128]{1,2,3,0:T(8,128)(2,1)} copy(bf16[8,32,8,128]{3,2,1,0:T(8,128)(2,1)} %param.5) | data formatting | bytes 1048576 | tf_op args[0]
  10.0 4.1 %copy.103 = f32[8,32,8,128]{1,3,2,0:T(8,128)} copy(bf16[8,32,8,128]{1,2,3,0:T(8,128)(2,1)} %copy.102) | data formatting | bytes 1572864 | tf_op jit(solution)/shard_map/convert_element_type | solution.py:55
  14.1 4.8 %reduce_sum.9 = f32[4,32,4,64]{1,3,2,0:T(8,128)S(1)} reduce(f32[4,2,32,4,2,64,2]{2,6,5,4,3,1,0:T(2,128)} %bitcast.80, f32[]{:T(128)} %constant.10.clone.1), dimensions={1,4,6}, to_apply=%region_0.0 | reduce | flops 229376 | bytes 1179652 | tf_op jit(solution)/shard_map/reduce_sum | solution.py:36
  19.0 0.1 multiply_convert_fusion
  19.0 0.0 copy-start.3
  19.0 0.0 copy-start.6
  19.0 2.4 %fusion.38 = bf16[1,512,1,16]{1,3,2,0:T(8,128)(2,1)S(1)} fusion(bf16[4,4,4,32,512]{4,3,2,1,0:T(8,128)(2,1)} %param.6, bf16[4,32,4,16,4]{1,4,3,2,0:T(4,128)(2,1)S(1)} %bitcast.87), kind=kOutput, calls=%fused_computation.50 | convolution fusion | flops 33595392 | bytes 2179072 | tf_op jit(solution)/shard_map/daihbwc,abcio->dohw/dot_general | solution.py:41
  21.5 0.2 copy.105
  21.6 0.5 broadcast.55
  22.2 1.4 reduce
  23.6 0.2 reshape.82
  23.8 15.5 %all_to_all.12 = bf16[16,2,256]{2,1,0:T(2,128)(2,1)S(1)} all-to-all(bf16[16,2,256]{2,1,0:T(2,128)(2,1)S(1)} %reshape.82), channel_id=1, replica_groups=mesh['row'=16,'col'=2] {'row'}, dimensions={0} | all-to-all | bytes 32768 | tf_op jit(solution)/shard_map/all_to_all | solution.py:43
  39.2 0.2 reshape.83
  39.5 0.1 copy.106
  39.6 0.1 all_to_all.10
  39.7 1.3 collective-permute-start.1
  41.0 3.0 %collective-permute-start = (bf16[16,32,1,16]{1,0,3,2:T(8,128)(2,1)S(1)}, bf16[16,32,1,16]{1,0,3,2:T(8,128)(2,1)S(1)}, u32[]{:S(2)}, u32[]{:S(2)}) collective-permute-start(bf16[16,32,1,16]{1,0,3,2:T(8,128)(2,1)S(1)} %all_to_all.10), channel_id=1, source_target_pairs={{0,1},{2,3},{4,5},{6,7},{8,9},{10,11},{12,13},{14,15},{16,17},{18,... | collective-permute-start | bytes 49160 | tf_op jit(solution)/shard_map/ppermute | solution.py:12
  44.0 0.0 collective-permute-done.1
  44.0 0.9 collective-permute-done
  44.9 0.1 fusion.29
  45.0 0.1 pad.5
  45.2 0.1 slice.20
  45.2 0.0 copy-done.3
  45.2 0.0 copy-done.6
  45.2 1.3 fusion.11
  46.5 0.1 copy.110
  46.7 0.9 copy.111
  47.5 0.0 reduce-scatter.2.cloned.1.call-update
  47.5 73.9 %reduce-scatter.2.cloned.1.call-done = bf16[1,512,1,16]{1,3,2,0:T(8,128)(2,1)} async-done(((bf16[16,512,1,16]{1,3,2,0:T(8,128)(2,1)}), bf16[1,512,1,16]{1,3,2,0:T(8,128)(2,1)}) %reduce-scatter.2.cloned.1.call-update) | async-done | bytes 16400 | tf_op jit(solution)/shard_map/reduce_scatter | solution.py:46
  121.4 0.0 copy-done
  121.4 2.2 %convolution_bitcast_fusion = f32[1,4,32,1,4,16,4]{2,5,6,4,1,3,0:T(8,128)S(1)} fusion(bf16[4,4,4,32,512]{4,3,2,1,0:T(8,128)(2,1)S(1)} %copy-done, bf16[1,512,1,16]{1,3,2,0:T(8,128)(2,1)} %reduce-scatter.2.cloned.1.call-done), kind=kOutput, calls=%fused_computation.14 | convolution fusion | flops 33603584 | bytes 2244608 | tf_op jit(solution)/shard_map/dihw,abcoi->daohbwc/dot_general | solution.py:50
  123.6 0.2 copy.112
  123.8 0.3 copy.113
  124.2 0.1 broadcast_in_dim.16
  124.3 0.7 broadcast_in_dim.17
  125.0 0.3 broadcast_in_dim.18
  125.3 1.3 copy-done.1
  126.6 0.4 add_convert_fusion
  127.1 1.3 collective-permute-start.2
  128.4 1.3 collective-permute-start.3
  129.7 5.4 %collective-permute-done.2 = bf16[1,32,8,128]{1,2,3,0:T(8,128)(2,1)S(1)} collective-permute-done((bf16[1,32,8,128]{1,2,3,0:T(8,128)(2,1)S(1)}, bf16[1,32,8,128]{1,2,3,0:T(8,128)(2,1)S(1)}, u32[]{:S(2)}, u32[]{:S(2)}) %collective-permute-start.2) | collective-permute-done | bytes 65568 | tf_op jit(solution)/shard_map/ppermute | solution.py:12
  135.1 1.6 collective-permute-done.3
  136.7 0.6 pad_maximum_fusion
  137.3 1.5 copy-done.2
  138.8 1.2 fusion.51
  140.0 0.4 copy.114
  140.4 0.4 copy.115
  140.7 1.3 collective-permute-start.5
  142.0 3.2 %collective-permute-start.4 = (bf16[10,32,1,128]{3,1,2,0:T(8,128)(2,1)S(1)}, bf16[10,32,1,128]{3,1,2,0:T(8,128)(2,1)S(1)}, u32[]{:S(2)}, u32[]{:S(2)}) collective-permute-start(bf16[10,32,1,128]{3,1,2,0:T(8,128)(2,1)S(1)} %copy.114), channel_id=1, source_target_pairs={{0,1},{2,3},{4,5},{6,7},{8,9},{10,11},{12,13},{14,15},{16,17},{18,... | collective-permute-start | bytes 245768 | tf_op jit(solution)/shard_map/ppermute | solution.py:12
  145.3 3.3 %copy.116 = bf16[10,32,8,128]{3,1,2,0:T(8,128)(2,1)S(1)} copy(bf16[10,32,8,128]{1,2,3,0:T(8,128)(2,1)} %copy-done.2) | data formatting | bytes 1310720 | tf_op jit(solution)/shard_map/concatenate | solution.py:16
  148.6 0.0 collective-permute-done.5
  148.6 0.0 collective-permute-done.4
  148.6 0.1 maximum_bitcast_fusion
  148.7 1.8 pad.7
  150.5 8.7 %reshape.65 = bf16[10,32,10,1,8,17]{5,4,1,2,0,3:T(8,128)(2,1)} reshape(bf16[10,32,10,1,136]{4,1,2,0,3:T(8,128)(2,1)} %pad.7) | data formatting | bytes 1740800 | tf_op jit(solution)/shard_map/conv_general_dilated | solution.py:21
  159.2 10.2 %copy.118 = bf16[10,32,10,1,8,17]{1,4,5,2,0,3:T(8,128)(2,1)} copy(bf16[10,32,10,1,8,17]{5,4,1,2,0,3:T(8,128)(2,1)} %reshape.65) | data formatting | bytes 1740800 | tf_op jit(solution)/shard_map/conv_general_dilated | solution.py:21
  169.4 1.1 slice.26
  170.5 9.6 %broadcast_select_fusion = f32[8,8,8,17,32]{4,2,3,1,0:T(8,128)S(1)} fusion(pred[8,17]{0,1:T(8,128)(4,1)S(1)} %copy-done.5, bf16[3,3,3,32,32]{4,3,2,1,0:T(8,128)(2,1)S(1)} %copy-done.4, bf16[10,32,10,1,7,2]{1,4,5,2,0,3:T(8,128)(2,1)S(1)} %slice.26, bf16[10,32,10,1,8,17]{1,4,5,2,0,3:T(8,128)(2,1)} %copy.118), kind=kOutput, calls=%fused_computation.10 | convolution fusion | flops 484493312 | bytes 2129544 | tf_op jit(solution)/shard_map/conv_general_dilated | solution.py:21
  180.1 0.8 copy.119
  180.9 2.2 %slice.27 = f32[8,8,1,128,32]{4,1,3,0,2:T(8,128)} slice(f32[8,8,1,136,32]{4,1,3,0,2:T(8,128)S(1)} %bitcast.79), slice={[0:8], [0:8], [0:1], [0:128], [0:32]} | slice | bytes 2097152 | tf_op jit(solution)/shard_map/conv_general_dilated | solution.py:21
  183.1 2.8 %copy.126 = f32[8,8,1,128,32]{3,1,4,0,2:T(8,128)S(1)} copy(f32[8,8,1,128,32]{4,1,3,0,2:T(8,128)} %slice.27) | data formatting | bytes 2097152
  186.0 1.1 fusion.16
  (9 shorter events, 0.1 us)
Async XLA Ops:
  6.5 114.9 %copy-start = (bf16[4,4,4,32,512]{4,3,2,1,0:T(8,128)(2,1)S(1)}, bf16[4,4,4,32,512]{4,3,2,1,0:T(8,128)(2,1)}, u32[]{:S(2)}) copy-start(bf16[4,4,4,32,512]{4,3,2,1,0:T(8,128)(2,1)} %param.8) | copy-start | bytes 6291460
  6.5 114.9 %reduce-scatter.2.cloned.1.call-start = ((), (), s32[]{:S(2)}) async-start(), calls=%async_computation.2 | async-start | bytes 278528 | tf_op jit(solution)/shard_map/reduce_scatter | solution.py:46
  19.0 26.2 %copy-start.3 = (bf16[3,3,3,32,512]{4,3,2,1,0:T(8,128)(2,1)S(1)}, bf16[3,3,3,32,512]{4,3,2,1,0:T(8,128)(2,1)}, u32[]{:S(2)}) copy-start(bf16[3,3,3,32,512]{4,3,2,1,0:T(8,128)(2,1)} %param.7) | copy-start | bytes 2654212
  19.0 26.2 %copy-start.6 = (pred[8,3]{0,1:T(4,128)(4,1)S(1)}, pred[8,3]{0,1:T(4,128)(4,1)}, u32[]{:S(2)}) copy-start(pred[8,3]{0,1:T(4,128)(4,1)} %constant.26) | copy-start | bytes 76
  39.7 4.3 %collective-permute-start.1 = (bf16[16,32,1,16]{1,0,3,2:T(8,128)(2,1)S(1)}, bf16[16,32,1,16]{1,0,3,2:T(8,128)(2,1)S(1)}, u32[]{:S(2)}, u32[]{:S(2)}) collective-permute-start(bf16[16,32,1,16]{1,0,3,2:T(8,128)(2,1)S(1)} %all_to_all.10), channel_id=1, source_target_pairs={{1,0},{3,2},{5,4},{7,6},{9,8},{11,10},{13,12},{15,14},{17,16},{19,... | collective-permute-start | bytes 49160 | tf_op jit(solution)/shard_map/ppermute | solution.py:15
  41.0 3.9 %collective-permute-start = (bf16[16,32,1,16]{1,0,3,2:T(8,128)(2,1)S(1)}, bf16[16,32,1,16]{1,0,3,2:T(8,128)(2,1)S(1)}, u32[]{:S(2)}, u32[]{:S(2)}) collective-permute-start(bf16[16,32,1,16]{1,0,3,2:T(8,128)(2,1)S(1)} %all_to_all.10), channel_id=1, source_target_pairs={{0,1},{2,3},{4,5},{6,7},{8,9},{10,11},{12,13},{14,15},{16,17},{18,... | collective-permute-start | bytes 49160 | tf_op jit(solution)/shard_map/ppermute | solution.py:12
  125.0 1.6 copy-start.1
  127.1 8.0 %collective-permute-start.2 = (bf16[1,32,8,128]{1,2,3,0:T(8,128)(2,1)S(1)}, bf16[1,32,8,128]{1,2,3,0:T(8,128)(2,1)S(1)}, u32[]{:S(2)}, u32[]{:S(2)}) collective-permute-start(bf16[1,32,8,128]{1,2,3,0:T(8,128)(2,1)S(1)} %get-tuple-element.7), channel_id=1, source_target_pairs={{0,2},{2,4},{4,6},{6,8},{8,10},{10,12},{12,14},{14,16},{16,18},{18... | collective-permute-start | bytes 196616 | tf_op jit(solution)/shard_map/ppermute | solution.py:12
  128.4 8.3 %collective-permute-start.3 = (bf16[1,32,8,128]{1,2,3,0:T(8,128)(2,1)S(1)}, bf16[1,32,8,128]{1,2,3,0:T(8,128)(2,1)S(1)}, u32[]{:S(2)}, u32[]{:S(2)}) collective-permute-start(bf16[1,32,8,128]{1,2,3,0:T(8,128)(2,1)S(1)} %get-tuple-element.8), channel_id=1, source_target_pairs={{2,0},{4,2},{6,4},{8,6},{10,8},{12,10},{14,12},{16,14},{18,16},{20... | collective-permute-start | bytes 196616 | tf_op jit(solution)/shard_map/ppermute | solution.py:15
  137.3 1.5 copy-start.2
  140.7 7.8 %collective-permute-start.5 = (bf16[10,32,1,128]{3,1,2,0:T(8,128)(2,1)S(1)}, bf16[10,32,1,128]{3,1,2,0:T(8,128)(2,1)S(1)}, u32[]{:S(2)}, u32[]{:S(2)}) collective-permute-start(bf16[10,32,1,128]{3,1,2,0:T(8,128)(2,1)S(1)} %copy.115), channel_id=1, source_target_pairs={{1,0},{3,2},{5,4},{7,6},{9,8},{11,10},{13,12},{15,14},{17,16},{19,... | collective-permute-start | bytes 245768 | tf_op jit(solution)/shard_map/ppermute | solution.py:15
  142.0 6.6 %collective-permute-start.4 = (bf16[10,32,1,128]{3,1,2,0:T(8,128)(2,1)S(1)}, bf16[10,32,1,128]{3,1,2,0:T(8,128)(2,1)S(1)}, u32[]{:S(2)}, u32[]{:S(2)}) collective-permute-start(bf16[10,32,1,128]{3,1,2,0:T(8,128)(2,1)S(1)} %copy.114), channel_id=1, source_target_pairs={{0,1},{2,3},{4,5},{6,7},{8,9},{10,11},{12,13},{14,15},{16,17},{18,... | collective-permute-start | bytes 245768 | tf_op jit(solution)/shard_map/ppermute | solution.py:12
  159.2 11.3 %copy-start.4 = (bf16[3,3,3,32,32]{4,3,2,1,0:T(8,128)(2,1)S(1)}, bf16[3,3,3,32,32]{4,3,2,1,0:T(8,128)(2,1)}, u32[]{:S(2)}) copy-start(bf16[3,3,3,32,32]{4,3,2,1,0:T(8,128)(2,1)} %param.9) | copy-start | bytes 165892
  159.2 11.3 %copy-start.5 = (pred[8,17]{0,1:T(8,128)(4,1)S(1)}, pred[8,17]{0,1:T(8,128)(4,1)}, u32[]{:S(2)}) copy-start(pred[8,17]{0,1:T(8,128)(4,1)} %constant.25) | copy-start | bytes 412
Sparse Core Ops, SparseCore 0:
  47.7 73.6 reduce-scatter.1
where the time goes:
time: 195 us; the launch traced here: 194 us
  waiting for transfers between devices  81.7 us (42%)
  local copies, waits for them, and re-layouts  47.5 us (24%)
  blocking collectives  15.5 us (8%)
  matrix products  15.4 us (8%)
  between operations  13.7 us (7%)
  starting transfers between devices  11.4 us (6%)
  other arithmetic  8.64 us (4%)
    reduce_scatter x1, waiting for transfers between devices, body(): lax.psum_scatter(convolve(deeper, bott_weight).astype(jnp.bfloat16), 'row...  73.9 us
    conv_general_dilated x7, local copies, waits for them, and re-layouts, convolve(): lax.conv_general_dilated(padded[None], kernel, (1, 1, 1), ((0, 0), (0, 0)...  23.1 us
    all_to_all x1, blocking collectives, body(): lax.all_to_all(lowered, 'row', split_axis=1, concat_axis=0, tiled=True)  15.5 us
    conv_general_dilated x2, matrix products, convolve(): lax.conv_general_dilated(padded[None], kernel, (1, 1, 1), ((0, 0), (0, 0)...  10.9 us
    unnamed x19, local copies, waits for them, and re-layouts  10 us
    ppermute x3, starting transfers between devices, with_halo(): lax.ppermute(lax.slice_in_dim(block, block.shape[dim] - width, None, axis...  7.55 us
    ppermute x3, waiting for transfers between devices, with_halo(): lax.ppermute(lax.slice_in_dim(block, block.shape[dim] - width, None, axis...  6.24 us
    reduce_sum x1, other arithmetic, body(): pooled = features.astype(jnp.float32).reshape(depth // 2, 2, chans, heigh...  4.83 us
  transfers between devices with their start and end apart: 7, of which 4 were waited for; matrix products, arithmetic and copies ran while one was open for 2% of the time, Pallas kernels for 0%

commit v1 on v0

v1 whole, which is shorter than its diff:
```python
import functools

import jax
import jax.numpy as jnp
from jax import lax
from jax.experimental import pallas as pl
from jax.experimental.pallas import tpu as pltpu
from jax.sharding import PartitionSpec as P

F32, BF16 = jnp.float32, jnp.bfloat16
NT = (((1,), (1,)), ((), ()))


def iota(shape, dim):
    return lax.broadcasted_iota(jnp.int32, shape, dim)


def dot(a, b):
    return jnp.dot(a, b, preferred_element_type=F32)


def dot_nt(a, b):
    return lax.dot_general(a, b, NT, preferred_element_type=F32)


def silu(v):
    return v / (1.0 + jnp.exp(-v))


def lower_kernel(count, chans, height, feat, down, out):
    planes, rows, width = feat.shape
    coarse = width // 8
    half = height // 2
    each = down.shape[4] // count
    shape = (half * chans, rows)
    r, c = iota(shape, 0), iota(shape, 1)
    pick = ((r % chans == c // height) & (r // chans == (c % height) // 2)).astype(F32).astype(BF16)
    sums = []
    for a in range(planes // 2):
        sums.append((dot(pick, feat[2 * a]) + dot(pick, feat[2 * a + 1])).astype(BF16))
    table = jnp.concatenate(sums, axis=0)
    shape = (4 * coarse, width)
    r, c = iota(shape, 0), iota(shape, 1)
    cols = ((r % coarse == c // 8) & (r // coarse == (c % 8) // 2)).astype(F32).astype(BF16)
    pooled = (dot_nt(cols, table) * 0.125).astype(BF16)
    low = jnp.zeros((coarse, down.shape[4]), F32)
    for c in range(4):
        weight = down[:, :, c].reshape(-1, down.shape[4])
        low = low + dot(pooled[c * coarse : (c + 1) * coarse], weight)
    low = silu(low)
    place = iota(low.shape, 0)
    before = jnp.where(place == 0, 0.0, pltpu.roll(low, 1, 0))
    after = jnp.where(place == coarse - 1, 0.0, pltpu.roll(low, coarse - 1, 0))
    for k in range(count):
        part = slice(k * each, (k + 1) * each)
        out[k] = jnp.concatenate([before[:, part], low[:, part], after[:, part]], axis=1).astype(BF16)


def bottleneck_kernel(sides, taps_of, *refs):
    blocks, weight, out, pads = refs[:sides], refs[sides], refs[sides + 1], refs[sides + 2 :]
    depth, coarse, lanes = blocks[0].shape
    rows = depth * coarse
    total = jnp.zeros((rows, weight.shape[4]), F32)
    taps = taps_of()
    for block, tap, pad in zip(blocks, taps, pads):
        zero = jnp.zeros((coarse, lanes), BF16)
        pad[:coarse] = zero
        pad[coarse + rows :] = zero
        pad[coarse : coarse + rows] = block[...].reshape(rows, lanes)
        for a in range(3):
            kernel = weight[a, tap].reshape(lanes, weight.shape[4])
            total = total + dot(pad[a * coarse : a * coarse + rows], kernel)
    out[...] = total.astype(BF16).reshape(out.shape)


def raise_kernel(chans, height, parts, feat, up, joined, spread):
    planes, rows, width = feat.shape
    coarse = width // 8
    total = parts[0].astype(F32)
    for k in range(1, parts.shape[0]):
        total = total + parts[k].astype(F32)
    middle = silu(total).astype(BF16)
    shape = (4 * width, coarse)
    r, c = iota(shape, 0), iota(shape, 1)
    pick = (((r % width) // 8 == c) & ((r % 8) // 2 == r // width)).astype(F32).astype(BF16)
    wide = dot(pick, middle).astype(BF16)
    raised = None
    for c in range(4):
        weight = up[:, :, c].reshape(-1, up.shape[4])
        term = dot_nt(weight, wide[c * width : (c + 1) * width])
        raised = term if raised is None else raised + term
    per = chans * (height // 2)
    for d in range(planes):
        spread[...] = feat[d].astype(F32)
        for h in range(height):
            start = (d // 2) * per + (h // 2) * chans
            value = spread[pl.ds(h, chans, stride=height), :] + raised[start : start + chans]
            joined[d, h * chans : (h + 1) * chans] = value.astype(BF16)


def band_kernel(chans, height, dec, out):
    eye = (iota((chans, chans), 0) == iota((chans, chans), 1)).astype(F32).astype(BF16)
    span = (height + 2) * chans
    total = 3 * span
    wide = -(-total // 128) * 128
    for c in range(3):
        taps = dot_nt(eye, dec[:, :, c].reshape(9 * chans, chans))
        pieces = []
        for a in range(3):
            pieces.append(taps[:, a * 3 * chans : (a + 1) * 3 * chans])
            pieces.append(jnp.zeros((chans, span - 3 * chans), F32))
        pieces.append(jnp.zeros((chans, wide - total), F32))
        base = jnp.concatenate(pieces, axis=1)
        for h in range(height):
            row = (c * height + h) * chans
            moved = base if h == 0 else pltpu.roll(base, h * chans, 1)
            out[row : row + chans] = moved[:, :total].astype(BF16)


def decode_kernel(chans, height, band, joined, low_h, high_h, low_d, high_d, out, field, spread):
    planes, rows, width = joined.shape
    span = rows + 2 * chans
    field[:span] = low_d[...]
    for d in range(planes):
        at = (d + 1) * span
        field[at : at + chans] = low_h[d]
        field[at + chans : at + chans + rows] = joined[d]
        field[at + chans + rows : at + span] = high_h[d]
    field[(planes + 1) * span :] = high_d[...]
    lane = iota((rows, width), 1)

    def pair(step, carry):
        at = pl.multiple_of(step * 2 * span, 16)
        window = jnp.concatenate(
            [field[pl.ds(at, 3 * span)], field[pl.ds(at + span, 3 * span)]], axis=1
        )
        sums = dot(band[...], window)
        for e in range(2):
            part = sums[:, e * width : (e + 1) * width]
            before = jnp.where(lane == 0, 0.0, pltpu.roll(part[:rows], 1, 1))
            after = jnp.where(lane == width - 1, 0.0, pltpu.roll(part[2 * rows :], width - 1, 1))
            value = silu(part[rows : 2 * rows] + before + after)
            for h in range(height):
                spread[pl.ds(h, chans, stride=height), :] = value[h * chans : (h + 1) * chans]
            out[step * 2 + e] = spread[...].astype(BF16)
        return carry

    lax.fori_loop(0, planes // 2, pair, 0)


def call(kernel, shape, scratch=(), name=None, flops=0, nbytes=0):
    return pl.pallas_call(
        kernel,
        out_shape=shape,
        scratch_shapes=list(scratch),
        name=name,
        cost_estimate=pl.CostEstimate(flops=flops, bytes_accessed=nbytes, transcendentals=0),
        compiler_params=pltpu.CompilerParams(vmem_limit_bytes=40 << 20),
    )


def bf16(*shape):
    return jax.ShapeDtypeStruct(shape, BF16)


def swap_pairs(count):
    first = [(i, i ^ 1) for i in range(count)]
    second = [(i, (i + 1 if i % 2 else i - 1) % count) for i in range(count)]
    return first, second


def body(features, down_weight, bott_weight, up_weight, dec_weight):
    depth, chans, height, width = features.shape
    count, cols = lax.axis_size("row"), lax.axis_size("col")
    top = down_weight.shape[4]
    coarse, rows, each = width // 8, chans * height, bott_weight.shape[3]
    feat = features.reshape(depth, rows, width)
    row, col = lax.axis_index("row"), lax.axis_index("col")

    lowered = call(
        functools.partial(lower_kernel, count, chans, height), bf16(count, coarse, 3 * each), name="lower"
    )(feat, down_weight)
    own = lax.all_to_all(lowered, "row", split_axis=0, concat_axis=0, tiled=True)

    up_one = [(i, i + 1) for i in range(cols - 1)]
    down_one = [(i + 1, i) for i in range(cols - 1)]
    if cols == 2:
        blocks = [own, lax.ppermute(own, "col", up_one + down_one)]
        taps_of = lambda: (1, 2 - 2 * lax.axis_index("col"))
    else:
        blocks = [lax.ppermute(own, "col", up_one), own, lax.ppermute(own, "col", down_one)]
        taps_of = lambda: (0, 1, 2)
    shares = call(
        functools.partial(bottleneck_kernel, len(blocks), taps_of),
        bf16(count, coarse, top),
        scratch=[pltpu.VMEM(((count + 2) * coarse, 3 * each), BF16) for _ in blocks],
        name="bottleneck",
    )(*blocks, bott_weight)
    parts = lax.all_to_all(shares, "row", split_axis=0, concat_axis=0, tiled=True)

    joined = call(
        functools.partial(raise_kernel, chans, height),
        bf16(depth, rows, width),
        scratch=[pltpu.VMEM((rows, width), F32)],
        name="raise",
    )(parts, feat, up_weight)

    span = 3 * (rows + 2 * chans)
    band = call(
        functools.partial(band_kernel, chans, height), bf16(3 * rows, span), name="band"
    )(dec_weight)

    bottom, top_rows = joined[:, :chans], joined[:, rows - chans :]
    none = jnp.zeros_like(bottom)
    if cols == 2:
        other = lax.ppermute(jnp.where(col == 0, top_rows, bottom), "col", up_one + down_one)
        low_h = jnp.where(col == 0, none, other)
        high_h = jnp.where(col == 0, other, none)
    else:
        low_h = lax.ppermute(top_rows, "col", up_one)
        high_h = lax.ppermute(bottom, "col", down_one)
    first = jnp.concatenate([low_h[0], joined[0], high_h[0]], axis=0)
    last = jnp.concatenate([low_h[-1], joined[-1], high_h[-1]], axis=0)
    if count % 2 == 0:
        even = row % 2 == 0
        pairs, others = swap_pairs(count)
        near = lax.ppermute(jnp.where(even, last, first), "row", pairs)
        far = lax.ppermute(jnp.where(even, first, last), "row", others)
        low_d = jnp.where(row == 0, jnp.zeros_like(first), jnp.where(even, far, near))
        high_d = jnp.where(row == count - 1, jnp.zeros_like(first), jnp.where(even, near, far))
    else:
        low_d = lax.ppermute(last, "row", [(i, i + 1) for i in range(count - 1)])
        high_d = lax.ppermute(first, "row", [(i + 1, i) for i in range(count - 1)])

    decoded = call(
        functools.partial(decode_kernel, chans, height),
        bf16(depth, rows, width),
        scratch=[
            pltpu.VMEM(((depth + 2) * (rows + 2 * chans), width), BF16),
            pltpu.VMEM((rows, width), F32),
        ],
        name="decode",
    )(band, joined, low_h, high_h, low_d, high_d)
    return decoded.reshape(depth, chans, height, width)


def solution(mesh):
    placed = (P("row", None, "col", None), P(), P(None, None, None, "row", None), P(), P())
    return jax.shard_map(
        body, mesh=mesh, in_specs=placed, out_specs=P("row", None, "col", None), check_vma=False
    )
```

time: 195 us -> 52.2 us (0.27)
  waiting for transfers between devices: 81.7 us -> 16.7 us
  local copies, waits for them, and re-layouts: 47.5 us -> 4.76 us
  matrix products: 15.4 us -> 0 us
  between operations: 13.7 us -> 0.11 us
  other arithmetic: 8.64 us -> 0.08 us
  Pallas kernels: 0 us -> 7.32 us
  starting transfers between devices: 11.4 us -> 7.26 us
    reduce_scatter x1 -> x0, waiting for transfers between devices: 73.9 us -> none  [body(): lax.psum_scatter(convolve(deeper, bott_weight).astype(jnp.bfloat16), 'row...]
    conv_general_dilated x7 -> x0, local copies, waits for them, and re-layouts: 23.1 us -> none  [convolve(): lax.conv_general_dilated(padded[None], kernel, (1, 1, 1), ((0, 0), (0, 0)...]
    conv_general_dilated x2 -> x0, matrix products: 10.9 us -> none  [convolve(): lax.conv_general_dilated(padded[None], kernel, (1, 1, 1), ((0, 0), (0, 0)...]
    all_to_all x0 -> x1, waiting for transfers between devices: none -> 10.4 us  [body(): lax.all_to_all(shares, 'row', split_axis=0, concat_axis=0, tiled=True)]
    ppermute x6 -> x4, starting transfers between devices: 11.4 us -> 3.72 us  [the longest x1 2.8 us: body(): far = lax.ppermute(jnp.where(even, first, last), 'row', others)]
    pallas_call x0 -> x5, Pallas kernels: none -> 7.32 us  [the longest x1 3.63 us: body(): call(functools.partial(decode_kernel, chans, height), bf16(depth, rows, w...]
    unnamed x19 -> x12, local copies, waits for them, and re-layouts: 10 us -> 4.74 us
    convert_element_type x5 -> x0, local copies, waits for them, and re-layouts: 5.24 us -> none  [the longest x1 4.09 us: body(): joined = (features.astype(jnp.float32) + raised).astype(jnp.bfloat16)]
  transfers between devices with their start and end apart: 7 -> 5, of which waited for: 4 -> 5; matrix products, arithmetic and copies ran while one was open for 2% -> 0% of each run, Pallas kernels for 0% -> 1%
where the time goes in v1:
time: 52.2 us; the launch traced here: 51.8 us
  waiting for transfers between devices  16.7 us (32%)
  blocking collectives  15.7 us (30%)
  Pallas kernels  7.32 us (14%)
  starting transfers between devices  7.26 us (14%)
  local copies, waits for them, and re-layouts  4.76 us (9%)
    all_to_all x1, blocking collectives, body(): lax.all_to_all(lowered, 'row', split_axis=0, concat_axis=0, tiled=True)  15.7 us
    all_to_all x1, waiting for transfers between devices, body(): lax.all_to_all(shares, 'row', split_axis=0, concat_axis=0, tiled=True)  10.4 us
    unnamed x12, local copies, waits for them, and re-layouts  4.74 us
    pallas_call x1, Pallas kernels, body(): call(functools.partial(decode_kernel, chans, height), bf16(depth, rows, w...  3.63 us
    all_to_all x1, starting transfers between devices, body(): lax.all_to_all(shares, 'row', split_axis=0, concat_axis=0, tiled=True)  3.53 us
    ppermute x1, waiting for transfers between devices, body(): far = lax.ppermute(jnp.where(even, first, last), 'row', others)  3.51 us
    ppermute x1, starting transfers between devices, body(): far = lax.ppermute(jnp.where(even, first, last), 'row', others)  2.8 us
    pallas_call x1, Pallas kernels, body(): call(functools.partial(bottleneck_kernel, len(blocks), taps_of), bf16(cou...  1.28 us
  transfers between devices with their start and end apart: 5, of which 5 were waited for; matrix products, arithmetic and copies ran while one was open for 0% of the time, Pallas kernels for 1%

profile of v1, /device:TPU:0, one launch (start us, length us, event | category | flops | bytes accessed | tf_op | source)
XLA Modules:
  0.0 51.8 jit_solution(6898767775628403682)
XLA Ops:
  0.0 0.0 copy-start
  0.0 1.6 %copy-done = bf16[4,4,4,32,512]{4,3,2,1,0:T(8,128)(2,1)S(1)} copy-done((bf16[4,4,4,32,512]{4,3,2,1,0:T(8,128)(2,1)S(1)}, bf16[4,4,4,32,512]{4,3,2,1,0:T(8,128)(2,1)}, u32[]{:S(2)}) %copy-start) | copy-done | bytes 2097176
  1.6 0.0 copy-start.2
  1.6 1.0 %copy-done.2 = bf16[8,32,8,128]{3,2,1,0:T(8,128)(2,1)S(1)} copy-done((bf16[8,32,8,128]{3,2,1,0:T(8,128)(2,1)S(1)}, bf16[8,32,8,128]{3,2,1,0:T(8,128)(2,1)}, u32[]{:S(2)}) %copy-start.2) | copy-done | bytes 524312
  2.6 0.0 copy-start.1
  2.6 0.0 copy-start.3
  2.6 0.8 %lower.1 = bf16[16,16,96]{2,1,0:T(8,128)(2,1)S(1)} custom-call(bf16[8,256,128]{2,1,0:T(8,128)(2,1)S(1)} %bitcast.14, bf16[4,4,4,32,512]{4,3,2,1,0:T(8,128)(2,1)S(1)} %copy-done), custom_call_target="tpu_custom_call" | custom-call | tf_op jit(solution)/shard_map/lower/pallas_call | solution.py:180
  3.5 15.7 %all_to_all.10.refs_0_ = bf16[16,16,96]{2,1,0:T(8,128)(2,1)S(1)} all-to-all(bf16[16,16,96]{2,1,0:T(8,128)(2,1)S(1)} %lower.1), channel_id=1, replica_groups=mesh['row'=16,'col'=2] {'row'}, dimensions={0} | all-to-all | bytes 98304 | tf_op jit(solution)/shard_map/all_to_all | solution.py:183
  19.2 0.0 collective-permute-start
  19.2 1.3 %collective-permute-done.refs_1_ = bf16[16,16,96]{2,1,0:T(8,128)(2,1)S(1)} collective-permute-done((bf16[16,16,96]{2,1,0:T(8,128)(2,1)S(1)}, bf16[16,16,96]{2,1,0:T(8,128)(2,1)S(1)}, u32[]{:S(2)}, u32[]{:S(2)}) %collective-permute-start) | collective-permute-done | bytes 49184 | tf_op jit(solution)/shard_map/ppermute | solution.py:188
  20.4 0.0 copy-start.4
  20.4 1.2 %copy-done.4 = bf16[3,3,3,32,512]{4,3,2,1,0:T(8,128)(2,1)S(1)} copy-done((bf16[3,3,3,32,512]{4,3,2,1,0:T(8,128)(2,1)S(1)}, bf16[3,3,3,32,512]{4,3,2,1,0:T(8,128)(2,1)}, u32[]{:S(2)}) %copy-start.4) | copy-done | bytes 884760
  21.6 1.3 %bottleneck.1 = bf16[16,16,512]{2,1,0:T(8,128)(2,1)} custom-call(bf16[16,16,96]{2,1,0:T(8,128)(2,1)S(1)} %all_to_all.10.refs_0_, bf16[16,16,96]{2,1,0:T(8,128)(2,1)S(1)} %collective-permute-done.refs_1_, bf16[3,3,3,32,512]{4,3,2,1,0:T(8,128)(2,1)S(1)} %copy-done.4), custom_call_target="tpu_custom_call" | custom-call | tf_op jit(solution)/shard_map/bottleneck/pallas_call | solution.py:193
  22.9 3.5 %all-to-all-start.1 = ((bf16[16,16,512]{2,1,0:T(8,128)(2,1)}), bf16[16,16,512]{2,1,0:T(8,128)(2,1)S(1)}, u32[]{:S(2)}, u32[]{:S(2)}) async-start(bf16[16,16,512]{2,1,0:T(8,128)(2,1)} %bottleneck.1), calls=%async_computation.1 | async-start | bytes 524288 | tf_op jit(solution)/shard_map/all_to_all | solution.py:199
  26.4 10.4 %all-to-all-done.1.parts = bf16[16,16,512]{2,1,0:T(8,128)(2,1)S(1)} async-done(((bf16[16,16,512]{2,1,0:T(8,128)(2,1)}), bf16[16,16,512]{2,1,0:T(8,128)(2,1)S(1)}, u32[]{:S(2)}, u32[]{:S(2)}) %all-to-all-start.1) | async-done | bytes 262176 | tf_op jit(solution)/shard_map/all_to_all | solution.py:199
  36.8 0.0 copy-done.1
  36.8 0.0 copy-done.3
  36.8 1.0 %raise.1.joined = bf16[8,256,128]{2,1,0:T(8,128)(2,1)S(1)} custom-call(bf16[16,16,512]{2,1,0:T(8,128)(2,1)S(1)} %all-to-all-done.1.parts, bf16[8,256,128]{2,1,0:T(8,128)(2,1)S(1)} %bitcast.15, bf16[4,4,4,32,512]{4,3,2,1,0:T(8,128)(2,1)S(1)} %copy-done.1), custom_call_target="tpu_custom_call" | custom-call | tf_op jit(solution)/shard_map/raise/pallas_call | solution.py:201
  37.9 0.1 collective-permute-start.1
  38.0 1.2 %collective-permute-done.1 = bf16[8,32,128]{2,1,0:T(8,128)(2,1)S(1)} collective-permute-done((bf16[8,32,128]{2,1,0:T(8,128)(2,1)S(1)}, bf16[8,32,128]{2,1,0:T(8,128)(2,1)S(1)}, u32[]{:S(2)}, u32[]{:S(2)}) %collective-permute-start.1) | collective-permute-done | bytes 65568 | tf_op jit(solution)/shard_map/ppermute | solution.py:216
  39.3 0.9 %collective-permute-start.3 = (bf16[320,128]{1,0:T(8,128)(2,1)S(1)}, bf16[320,128]{1,0:T(8,128)(2,1)S(1)}, u32[]{:S(2)}, u32[]{:S(2)}) collective-permute-start(bf16[320,128]{1,0:T(8,128)(2,1)S(1)} %get-tuple-element.9), channel_id=1, source_target_pairs={{0,2},{2,0},{4,6},{6,4},{8,10},{10,8},{12,14},{14,12},{16,18},{18,... | collective-permute-start | bytes 245768 | tf_op jit(solution)/shard_map/ppermute | solution.py:227
  40.2 2.8 %collective-permute-start.2 = (bf16[320,128]{1,0:T(8,128)(2,1)S(1)}, bf16[320,128]{1,0:T(8,128)(2,1)S(1)}, u32[]{:S(2)}, u32[]{:S(2)}) collective-permute-start(bf16[320,128]{1,0:T(8,128)(2,1)S(1)} %get-tuple-element.10), channel_id=1, source_target_pairs={{0,30},{2,4},{4,2},{6,8},{8,6},{10,12},{12,10},{14,16},{16,14},{18... | collective-permute-start | bytes 245768 | tf_op jit(solution)/shard_map/ppermute | solution.py:228
  43.0 0.0 copy-start.5
  43.0 0.9 %copy-done.5 = bf16[3,3,3,32,32]{4,3,2,1,0:T(8,128)(2,1)S(1)} copy-done((bf16[3,3,3,32,32]{4,3,2,1,0:T(8,128)(2,1)S(1)}, bf16[3,3,3,32,32]{4,3,2,1,0:T(8,128)(2,1)}, u32[]{:S(2)}) %copy-start.5) | copy-done | bytes 55320
  43.9 0.5 band.1
  44.4 0.3 collective-permute-done.3
  44.7 3.5 %collective-permute-done.2 = bf16[320,128]{1,0:T(8,128)(2,1)S(1)} collective-permute-done((bf16[320,128]{1,0:T(8,128)(2,1)S(1)}, bf16[320,128]{1,0:T(8,128)(2,1)S(1)}, u32[]{:S(2)}, u32[]{:S(2)}) %collective-permute-start.2) | collective-permute-done | bytes 81952 | tf_op jit(solution)/shard_map/ppermute | solution.py:228
  48.2 3.6 %decode.1 = bf16[8,256,128]{2,1,0:T(8,128)(2,1)} custom-call(bf16[768,960]{1,0:T(8,128)(2,1)S(1)} %band.1, bf16[8,256,128]{2,1,0:T(8,128)(2,1)S(1)} %raise.1.joined, bf16[8,32,128]{2,1,0:T(8,128)(2,1)S(1)} %get-tuple-element.16.low_h, bf16[8,32,128]{2,1,0:T(8,128)(2,1)S(1)} %get-tuple-element.15.high_h, bf16[320,128]{1,0:T(8,128)(2,1)S(1)} %get-tuple-element.8.low_d, ...), custom_call_target="tpu_custom_call" | custom-call | tf_op jit(solution)/shard_map/decode/pallas_call | solution.py:235
  (6 shorter events, 0.1 us)
Async XLA Ops:
  0.0 1.6 %copy-start = (bf16[4,4,4,32,512]{4,3,2,1,0:T(8,128)(2,1)S(1)}, bf16[4,4,4,32,512]{4,3,2,1,0:T(8,128)(2,1)}, u32[]{:S(2)}) copy-start(bf16[4,4,4,32,512]{4,3,2,1,0:T(8,128)(2,1)} %down.1) | copy-start | bytes 6291460
  1.6 1.0 %copy-start.2 = (bf16[8,32,8,128]{3,2,1,0:T(8,128)(2,1)S(1)}, bf16[8,32,8,128]{3,2,1,0:T(8,128)(2,1)}, u32[]{:S(2)}) copy-start(bf16[8,32,8,128]{3,2,1,0:T(8,128)(2,1)} %param.5) | copy-start | bytes 1572868
  2.6 34.2 %copy-start.1 = (bf16[4,4,4,32,512]{4,3,2,1,0:T(8,128)(2,1)S(1)}, bf16[4,4,4,32,512]{4,3,2,1,0:T(8,128)(2,1)}, u32[]{:S(2)}) copy-start(bf16[4,4,4,32,512]{4,3,2,1,0:T(8,128)(2,1)} %up.1) | copy-start | bytes 6291460
  2.6 34.2 %copy-start.3 = (bf16[8,32,8,128]{3,2,1,0:T(8,128)(2,1)S(1)}, bf16[8,32,8,128]{3,2,1,0:T(8,128)(2,1)}, u32[]{:S(2)}) copy-start(bf16[8,32,8,128]{3,2,1,0:T(8,128)(2,1)} %param.5) | copy-start | bytes 1572868
  19.2 1.3 %collective-permute-start = (bf16[16,16,96]{2,1,0:T(8,128)(2,1)S(1)}, bf16[16,16,96]{2,1,0:T(8,128)(2,1)S(1)}, u32[]{:S(2)}, u32[]{:S(2)}) collective-permute-start(bf16[16,16,96]{2,1,0:T(8,128)(2,1)S(1)} %all_to_all.10.refs_0_), channel_id=1, source_target_pairs={{0,1},{1,0},{2,3},{3,2},{4,5},{5,4},{6,7},{7,6},{8,9},{9,8},{10,11... | collective-permute-start | bytes 147464 | tf_op jit(solution)/shard_map/ppermute | solution.py:188
  20.4 1.2 %copy-start.4 = (bf16[3,3,3,32,512]{4,3,2,1,0:T(8,128)(2,1)S(1)}, bf16[3,3,3,32,512]{4,3,2,1,0:T(8,128)(2,1)}, u32[]{:S(2)}) copy-start(bf16[3,3,3,32,512]{4,3,2,1,0:T(8,128)(2,1)} %refs_2_.1) | copy-start | bytes 2654212
  22.9 14.0 %all-to-all-start.1 = ((bf16[16,16,512]{2,1,0:T(8,128)(2,1)}), bf16[16,16,512]{2,1,0:T(8,128)(2,1)S(1)}, u32[]{:S(2)}, u32[]{:S(2)}) async-start(bf16[16,16,512]{2,1,0:T(8,128)(2,1)} %bottleneck.1), calls=%async_computation.1 | async-start | bytes 524288 | tf_op jit(solution)/shard_map/all_to_all | solution.py:199
  37.9 1.3 %collective-permute-start.1 = (bf16[8,32,128]{2,1,0:T(8,128)(2,1)S(1)}, bf16[8,32,128]{2,1,0:T(8,128)(2,1)S(1)}, u32[]{:S(2)}, u32[]{:S(2)}) collective-permute-start(bf16[8,32,128]{2,1,0:T(8,128)(2,1)S(1)} %slice_select_fusion), channel_id=1, source_target_pairs={{0,1},{1,0},{2,3},{3,2},{4,5},{5,4},{6,7},{7,6},{8,9},{9,8},{10,11... | collective-permute-start | bytes 196616 | tf_op jit(solution)/shard_map/ppermute | solution.py:216
  39.3 5.4 %collective-permute-start.3 = (bf16[320,128]{1,0:T(8,128)(2,1)S(1)}, bf16[320,128]{1,0:T(8,128)(2,1)S(1)}, u32[]{:S(2)}, u32[]{:S(2)}) collective-permute-start(bf16[320,128]{1,0:T(8,128)(2,1)S(1)} %get-tuple-element.9), channel_id=1, source_target_pairs={{0,2},{2,0},{4,6},{6,4},{8,10},{10,8},{12,14},{14,12},{16,18},{18,... | collective-permute-start | bytes 245768 | tf_op jit(solution)/shard_map/ppermute | solution.py:227
  40.2 8.0 %collective-permute-start.2 = (bf16[320,128]{1,0:T(8,128)(2,1)S(1)}, bf16[320,128]{1,0:T(8,128)(2,1)S(1)}, u32[]{:S(2)}, u32[]{:S(2)}) collective-permute-start(bf16[320,128]{1,0:T(8,128)(2,1)S(1)} %get-tuple-element.10), channel_id=1, source_target_pairs={{0,30},{2,4},{4,2},{6,8},{8,6},{10,12},{12,10},{14,16},{16,14},{18... | collective-permute-start | bytes 245768 | tf_op jit(solution)/shard_map/ppermute | solution.py:228
  43.0 0.9 %copy-start.5 = (bf16[3,3,3,32,32]{4,3,2,1,0:T(8,128)(2,1)S(1)}, bf16[3,3,3,32,32]{4,3,2,1,0:T(8,128)(2,1)}, u32[]{:S(2)}) copy-start(bf16[3,3,3,32,32]{4,3,2,1,0:T(8,128)(2,1)} %dec.1) | copy-start | bytes 165892

commit v2 on v1

v2 whole, which is shorter than its diff:
```python
import functools

import jax
import jax.numpy as jnp
from jax import lax
from jax.experimental import pallas as pl
from jax.experimental.pallas import tpu as pltpu
from jax.sharding import PartitionSpec as P

F32, BF16 = jnp.float32, jnp.bfloat16
NT = (((1,), (1,)), ((), ()))


def iota(shape, dim):
    return lax.broadcasted_iota(jnp.int32, shape, dim)


def dot(a, b):
    return jnp.dot(a, b, preferred_element_type=F32)


def dot_nt(a, b):
    return lax.dot_general(a, b, NT, preferred_element_type=F32)


def silu(v):
    half = 0.5 * v
    return half + half * jnp.tanh(half)


def lower_kernel(count, repeat, chans, height, feat_hbm, down_hbm, out, feat, down, sems):
    planes, rows, width = feat.shape
    quarters = planes // 2
    loads = [
        pltpu.make_async_copy(feat_hbm.at[2 * a : 2 * a + 2], feat.at[2 * a : 2 * a + 2], sems.at[a])
        for a in range(quarters)
    ] + [
        pltpu.make_async_copy(down_hbm.at[a], down.at[a], sems.at[quarters + a]) for a in range(quarters)
    ]
    for load in loads:
        load.start()
    coarse = width // 8
    half = height // 2
    top = down.shape[4]
    each = top // count
    shape = (half * chans, rows)
    r, c = iota(shape, 0), iota(shape, 1)
    pick = ((r % chans == c // height) & (r // chans == (c % height) // 2)).astype(F32).astype(BF16)
    shape = (4 * coarse, width)
    r, c = iota(shape, 0), iota(shape, 1)
    cols = ((r % coarse == c // 8) & (r // coarse == (c % 8) // 2)).astype(F32).astype(BF16)
    for a in range(quarters):
        loads[a].wait()
    tables = [(dot(pick, feat[2 * a]) + dot(pick, feat[2 * a + 1])).astype(BF16) for a in range(quarters)]
    pooled = [(dot_nt(cols, table) * 0.125).astype(BF16) for table in tables]
    low = jnp.zeros((coarse, top), F32)
    for a in range(quarters):
        loads[quarters + a].wait()
        for c in range(4):
            low = low + dot(pooled[a][c * coarse : (c + 1) * coarse], down[a, :, c].reshape(-1, top))
    low = silu(low)
    place = iota(low.shape, 0)
    before = jnp.where(place == 0, 0.0, pltpu.roll(low, 1, 0))
    after = jnp.where(place == coarse - 1, 0.0, pltpu.roll(low, coarse - 1, 0))
    for k in range(count):
        part = slice(k * each, (k + 1) * each)
        block = jnp.concatenate([before[:, part], low[:, part], after[:, part]], axis=1).astype(BF16)
        for e in range(repeat):
            out[repeat * k + e] = block


def bottleneck_kernel(joint, blocks, *refs):
    if joint:
        got, weight, out = refs[:3]
        pads = refs[3:]
        col = lax.axis_index("col")
        sources = [(got[:, col], 1), (got[:, 1 - col], 2 - 2 * col)]
    else:
        weight, out = refs[blocks : blocks + 2]
        pads = refs[blocks + 2 :]
        sources = [(refs[k][...], k) for k in range(blocks)]
    depth, coarse, top = out.shape
    rows = depth * coarse
    lanes = 3 * weight.shape[3]
    total = jnp.zeros((rows, top), F32)
    for (block, tap), pad in zip(sources, pads):
        zero = jnp.zeros((coarse, lanes), BF16)
        pad[:coarse] = zero
        pad[coarse + rows :] = zero
        pad[coarse : coarse + rows] = block.reshape(rows, lanes)
        for a in range(3):
            kernel = weight[a, tap].reshape(lanes, top)
            total = total + dot(pad[a * coarse : a * coarse + rows], kernel)
    out[...] = total.astype(BF16).reshape(out.shape)


def raise_kernel(chans, height, parts, feat, up, joined, ends, *rest):
    sides, spread = rest[:-1], rest[-1]
    planes, rows, width = feat.shape
    coarse = width // 8
    total = parts[0].astype(F32)
    for k in range(1, parts.shape[0]):
        total = total + parts[k].astype(F32)
    middle = silu(total).astype(BF16)
    shape = (4 * width, coarse)
    r, c = iota(shape, 0), iota(shape, 1)
    pick = (((r % width) // 8 == c) & ((r % 8) // 2 == r // width)).astype(F32).astype(BF16)
    wide = dot(pick, middle).astype(BF16)
    raised = None
    for c in range(4):
        weight = up[:, :, c].reshape(-1, up.shape[4])
        term = dot_nt(weight, wide[c * width : (c + 1) * width])
        raised = term if raised is None else raised + term
    per = chans * (height // 2)
    for d in range(planes):
        spread[d] = feat[d].astype(F32)
        for h in range(height):
            start = (d // 2) * per + (h // 2) * chans
            value = spread[d, pl.ds(h, chans, stride=height), :] + raised[start : start + chans]
            joined[d, h * chans : (h + 1) * chans] = value.astype(BF16)
    odd = lax.axis_index("row") % 2
    near, far = (planes - 1) * (1 - odd), (planes - 1) * odd
    ends[0] = joined[near]
    ends[1] = joined[far]
    if len(sides) == 1:
        starts = [pl.multiple_of((rows - chans) * (1 - lax.axis_index("col")), chans)]
    else:
        starts = [0, rows - chans]
    for side, start in zip(sides, starts):
        for d in range(planes):
            side[d] = joined[d, pl.ds(start, chans)]
        side[planes] = joined[near, pl.ds(start, chans)]
        side[planes + 1] = joined[far, pl.ds(start, chans)]


def band_kernel(chans, height, dec, after, out):
    eye = (iota((chans, chans), 0) == iota((chans, chans), 1)).astype(F32).astype(BF16)
    step = 3 * chans
    wide = out.shape[1]
    for c in range(3):
        taps = [dot_nt(eye, dec[:, b, c].reshape(step, chans)) for b in range(3)]
        base = jnp.concatenate(taps + [jnp.zeros((chans, wide - 3 * step), F32)], axis=1)
        for h in range(height):
            row = h * step + c * chans
            moved = base if h == 0 else pltpu.roll(base, h * step, 1)
            out[row : row + chans] = moved.astype(BF16)


def decode_pair(chans, height, band, planes, spread, store):
    step = 3 * chans
    blocks = [jnp.concatenate([plane(h) for plane in planes], axis=1) for h in range(height + 2)]
    window = jnp.concatenate(blocks, axis=0)
    width = window.shape[1] // 2
    sums = [None] * height
    for at in range(0, window.shape[0], 256):
        stop = min(at + 256, window.shape[0])
        first = max(0, at // step - 2)
        last = min(height - 1, (stop - 1) // step)
        part = dot(band[first * step : (last + 1) * step, at:stop], window[at:stop])
        for h in range(first, last + 1):
            piece = part[(h - first) * step : (h - first + 1) * step]
            sums[h] = piece if sums[h] is None else sums[h] + piece
    lane = iota((chans, width), 1)
    for e in range(2):
        for h in range(height):
            part = sums[h][:, e * width : (e + 1) * width]
            before = jnp.where(lane == 0, 0.0, pltpu.roll(part[:chans], 1, 1))
            after = jnp.where(lane == width - 1, 0.0, pltpu.roll(part[2 * chans :], width - 1, 1))
            spread[e, pl.ds(h, chans, stride=height), :] = silu(part[chans : 2 * chans] + before + after)
        store(e, spread[e].astype(BF16))


def fill(field, slot, chans, plane, borders):
    height = field.shape[0]
    at = slice(slot * chans, (slot + 1) * chans)
    for h in range(1, height - 1):
        field[h, at] = plane[(h - 1) * chans : h * chans]
    if len(borders) == 1:
        col = lax.axis_index("col")
        field[(height - 1) * col, at] = jnp.zeros_like(borders[0])
        field[(height - 1) * (1 - col), at] = borders[0]
    else:
        field[0, at] = borders[0]
        field[height - 1, at] = borders[1]


def interior_kernel(chans, height, band, joined, *rest):
    sides, (out_hbm, field, spread, held, sems) = rest[:-5], rest[-5:]
    planes = joined.shape[0]
    for d in range(planes):
        fill(field, d, chans, joined[d], [side[d] for side in sides])
    copies = []
    for step in range(planes // 2 - 1):
        views = [
            lambda h, at=(2 * step + e) * chans: field[h, at : at + 3 * chans] for e in range(2)
        ]

        def store(e, value):
            held[2 * step + e] = value

        decode_pair(chans, height, band, views, spread.at[step], store)
        copies.append(
            pltpu.make_async_copy(
                held.at[2 * step : 2 * step + 2], out_hbm.at[2 * step + 1 : 2 * step + 3], sems.at[step]
            )
        )
        copies[-1].start()
    for copy in copies:
        copy.wait()


def edge_kernel(chans, height, band, joined, near, far, *rest):
    sides, (mid_hbm, out_hbm, field, spread, held, sems) = rest[:-6], rest[-6:]
    planes, rows, width = joined.shape
    for slot, d in ((1, 0), (2, 1), (3, planes - 2), (4, planes - 1)):
        fill(field, slot, chans, joined[d], [side[d] for side in sides])
    row, last = lax.axis_index("row"), lax.axis_size("row") - 1

    def outer(slot, got):
        borders = [got[rows + k * chans : rows + (k + 1) * chans] for k in range(len(sides))]
        fill(field, slot, chans, got[:rows], borders)

    @pl.when(row % 2 == 0)
    def _():
        outer(0, far[...])
        outer(5, near[...])

    @pl.when(row % 2 == 1)
    def _():
        outer(0, near[...])
        outer(5, far[...])

    @pl.when(row == 0)
    def _():
        field[:, :chans] = jnp.zeros((height + 2, chans, width), BF16)

    @pl.when(row == last)
    def _():
        field[:, 5 * chans :] = jnp.zeros((height + 2, chans, width), BF16)

    copies = [
        pltpu.make_async_copy(held.at[e], out_hbm.at[d], sems.at[e]) for e, d in ((0, 0), (1, planes - 1))
    ]

    def store(e, value):
        held[e] = value
        copies[e].start()

    views = [lambda h, at=3 * e * chans: field[h, at : at + 3 * chans] for e in range(2)]
    decode_pair(chans, height, band, views, spread, store)
    for copy in copies:
        copy.wait()


VMEM = pl.BlockSpec(memory_space=pltpu.MemorySpace.VMEM)
HBM = pl.BlockSpec(memory_space=pltpu.MemorySpace.HBM)


def fixed(x):
    return pltpu.with_memory_space_constraint(x, pltpu.MemorySpace.HBM)


def call(kernel, name, shape, ins, out, scratch=(), aliases=None, cost=0, limit=24):
    return pl.pallas_call(
        kernel,
        out_shape=shape,
        in_specs=ins,
        out_specs=out,
        scratch_shapes=list(scratch),
        input_output_aliases=aliases or {},
        name=name,
        cost_estimate=pl.CostEstimate(flops=cost, bytes_accessed=cost // 100, transcendentals=0),
        compiler_params=pltpu.CompilerParams(vmem_limit_bytes=limit << 20),
    )


def bf16(*shape):
    return jax.ShapeDtypeStruct(shape, BF16)


def neighbour_swaps(count, cols):
    ids = lambda row, col: row * cols + col
    first = [(ids(r, c), ids(r ^ 1, c)) for r in range(count) for c in range(cols)]
    second = []
    for r in range(count):
        for c in range(cols):
            other = r + 1 if r % 2 else r - 1
            inside = 0 <= other < count
            second.append((ids(r, c), ids(other, c) if inside else ids(r, c ^ 1)))
    return first, second


def body(features, down_weight, bott_weight, up_weight, dec_weight):
    depth, chans, height, width = features.shape
    count, cols = lax.axis_size("row"), lax.axis_size("col")
    top = down_weight.shape[4]
    coarse, rows, each = width // 8, chans * height, bott_weight.shape[3]
    feat = features.reshape(depth, rows, width)

    sems = lambda n: pltpu.SemaphoreType.DMA((n,))
    lower = functools.partial(lower_kernel, count, 2 if cols == 2 else 1, chans, height)
    lowered = call(
        lower,
        "lower",
        bf16((2 if cols == 2 else 1) * count, coarse, 3 * each),
        [HBM, HBM],
        VMEM,
        [pltpu.VMEM(feat.shape, BF16), pltpu.VMEM(down_weight.shape, BF16), sems(depth)],
        limit=24, cost=1_000_000_000,
    )(fixed(feat), fixed(down_weight))
    up_one = [(i, i + 1) for i in range(cols - 1)]
    down_one = [(i + 1, i) for i in range(cols - 1)]
    if cols == 2:
        got = lax.all_to_all(lowered, ("row", "col"), split_axis=0, concat_axis=0, tiled=True)
        blocks = [got.reshape(count, cols, coarse, 3 * each)]
        sides = 2
    else:
        own = lax.all_to_all(lowered, "row", split_axis=0, concat_axis=0, tiled=True)
        blocks = [lax.ppermute(own, "col", up_one), own, lax.ppermute(own, "col", down_one)]
        sides = 3
    shares = call(
        functools.partial(bottleneck_kernel, cols == 2, sides),
        "bottleneck",
        bf16(count, coarse, top),
        [VMEM] * (len(blocks) + 1),
        VMEM,
        [pltpu.VMEM(((count + 2) * coarse, 3 * each), BF16) for _ in range(sides)],
        cost=2_000_000_000,
    )(*blocks, bott_weight)
    parts = lax.all_to_all(shares, "row", split_axis=0, concat_axis=0, tiled=True)

    side = bf16(depth + 2, chans, width)
    sides = 1 if cols == 2 else 2
    joined, ends, *sides = call(
        functools.partial(raise_kernel, chans, height),
        "raise",
        (bf16(depth, rows, width), bf16(2, rows, width)) + (side,) * sides,
        [VMEM] * 3,
        (VMEM,) * (2 + sides),
        [pltpu.VMEM(feat.shape, F32)],
    )(parts, feat, up_weight)
    if cols == 2:
        sides = [lax.ppermute(sides[0], "col", up_one + down_one)]
    else:
        sides = [lax.ppermute(sides[1], "col", up_one), lax.ppermute(sides[0], "col", down_one)]

    span = rows + 2 * chans
    band = call(
        functools.partial(band_kernel, chans, height),
        "band",
        bf16(3 * rows, -(-3 * span // 128) * 128),
        [VMEM, HBM],
        VMEM,
        cost=500_000_000,
    )(dec_weight, joined)

    got = []
    for k, pairs in enumerate(neighbour_swaps(count, cols)):
        sent = jnp.concatenate([ends[k]] + [side[depth + k] for side in sides], axis=0)
        got.append(lax.ppermute(sent, ("row", "col"), pairs))

    shape = bf16(depth, rows, width)
    inner = call(
        functools.partial(interior_kernel, chans, height),
        "interior",
        shape,
        [VMEM] * (2 + len(sides)),
        HBM,
        [
            pltpu.VMEM((height + 2, depth * chans, width), BF16),
            pltpu.VMEM((depth // 2 - 1, 2, rows, width), F32),
            pltpu.VMEM((depth - 2, rows, width), BF16),
            sems(depth // 2 - 1),
        ],
        cost=3_000_000_000,
    )(band, joined, *sides)
    decoded = call(
        functools.partial(edge_kernel, chans, height),
        "edge",
        shape,
        [VMEM] * (4 + len(sides)) + [HBM],
        HBM,
        [
            pltpu.VMEM((height + 2, 6 * chans, width), BF16),
            pltpu.VMEM((2, rows, width), F32),
            pltpu.VMEM((2, rows, width), BF16),
            sems(2),
        ],
        aliases={4 + len(sides): 0},
        cost=1_000_000_000,
    )(band, joined, *got, *sides, inner)
    return decoded.reshape(depth, chans, height, width)


def solution(mesh):
    placed = (P("row", None, "col", None), P(), P(None, None, None, "row", None), P(), P())
    return jax.shard_map(
        body, mesh=mesh, in_specs=placed, out_specs=P("row", None, "col", None), check_vma=False
    )
```

time: 52.2 us -> 40.3 us (0.77)
  waiting for transfers between devices: 16.7 us -> 3.31 us
  blocking collectives: 15.7 us -> 28.6 us
  starting transfers between devices: 7.26 us -> 0.92 us
  local copies, waits for them, and re-layouts: 4.76 us -> 0.03 us
    all_to_all x1 -> x2, blocking collectives: 15.7 us -> 28.6 us  [the longest x1 15.3 us: body(): lax.all_to_all(lowered, ('row', 'col'), split_axis=0, concat_axis=0, tile...]
    all_to_all x1 -> x0, waiting for transfers between devices: 10.4 us -> none  [body(): lax.all_to_all(shares, 'row', split_axis=0, concat_axis=0, tiled=True)]
    unnamed x12 -> x8, local copies, waits for them, and re-layouts: 4.74 us -> 0.02 us
    all_to_all x1 -> x0, starting transfers between devices: 3.53 us -> none  [body(): lax.all_to_all(shares, 'row', split_axis=0, concat_axis=0, tiled=True)]
    ppermute x4 -> x3, waiting for transfers between devices: 6.25 us -> 3.31 us  [the longest x2 2.65 us: body(): got.append(lax.ppermute(sent, ('row', 'col'), pairs))]
    ppermute x4 -> x3, starting transfers between devices: 3.72 us -> 0.92 us  [the longest x2 0.85 us: body(): got.append(lax.ppermute(sent, ('row', 'col'), pairs))]
    pallas_call x5 -> x6, Pallas kernels: 7.32 us -> 7.23 us  [the longest x1 2.21 us: body(): call(lower, 'lower', bf16((2 if cols == 2 else 1) * count, coarse, 3 * ea...]
  transfers between devices with their start and end apart: 5 -> 3, of which waited for: 5 -> 2; matrix products, arithmetic and copies ran while one was open for 0% -> 0% of each run, Pallas kernels for 1% -> 6%
where the time goes in v2:
time: 40.3 us; the launch traced here: 40.2 us
  blocking collectives  28.6 us (71%)
  Pallas kernels  7.23 us (18%)
  waiting for transfers between devices  3.31 us (8%)
  starting transfers between devices  0.92 us (2%)
    all_to_all x1, blocking collectives, body(): lax.all_to_all(lowered, ('row', 'col'), split_axis=0, concat_axis=0, tile...  15.3 us
    all_to_all x1, blocking collectives, body(): lax.all_to_all(shares, 'row', split_axis=0, concat_axis=0, tiled=True)  13.2 us
    ppermute x2, waiting for transfers between devices, body(): got.append(lax.ppermute(sent, ('row', 'col'), pairs))  2.65 us
    pallas_call x1, Pallas kernels, body(): call(lower, 'lower', bf16((2 if cols == 2 else 1) * count, coarse, 3 * ea...  2.21 us
    pallas_call x1, Pallas kernels, body(): call(functools.partial(interior_kernel, chans, height), 'interior', shape...  1.66 us
    pallas_call x1, Pallas kernels, body(): call(functools.partial(edge_kernel, chans, height), 'edge', shape, [VMEM]...  1.18 us
    pallas_call x1, Pallas kernels, body(): call(functools.partial(raise_kernel, chans, height), 'raise', (bf16(depth...  1.03 us
    ppermute x2, starting transfers between devices, body(): got.append(lax.ppermute(sent, ('row', 'col'), pairs))  0.85 us
  transfers between devices with their start and end apart: 3, of which 2 were waited for; matrix products, arithmetic and copies ran while one was open for 0% of the time, Pallas kernels for 6%

profile of v2, /device:TPU:0, one launch (start us, length us, event | category | flops | bytes accessed | tf_op | source)
XLA Modules:
  0.0 40.2 jit_solution(8554117213692063010)
XLA Ops:
  0.0 0.0 copy-start.3
  0.0 2.2 %lower.1 = bf16[32,16,96]{2,1,0:T(8,128)(2,1)S(1)} custom-call(bf16[8,256,128]{2,1,0:T(8,128)(2,1)} %bitcast.11, bf16[4,4,4,32,512]{4,3,2,1,0:T(8,128)(2,1)} %down_hbm.1), custom_call_target="tpu_custom_call" | custom-call | flops 1000000000 | bytes 10000000 | tf_op jit(solution)/shard_map/lower/pallas_call | solution.py:302
  2.2 15.3 %all_to_all.10 = bf16[32,16,96]{2,1,0:T(8,128)(2,1)S(1)} all-to-all(bf16[32,16,96]{2,1,0:T(8,128)(2,1)S(1)} %lower.1), channel_id=1, replica_groups=mesh['row'=16,'col'=2] {'row','col'}, dimensions={0} | all-to-all | bytes 196608 | tf_op jit(solution)/shard_map/all_to_all | solution.py:314
  17.6 0.0 copy-done.3
  17.6 0.0 copy-start
  17.6 0.0 copy-start.1
  17.6 0.6 %bottleneck.1 = bf16[16,16,512]{2,1,0:T(8,128)(2,1)S(1)} custom-call(bf16[16,2,16,96]{3,2,1,0:T(8,128)(2,1)S(1)} %bitcast.13, bf16[3,3,3,32,512]{4,3,2,1,0:T(8,128)(2,1)S(1)} %copy-done.3), custom_call_target="tpu_custom_call" | custom-call | flops 2000000000 | bytes 20000000 | tf_op jit(solution)/shard_map/bottleneck/pallas_call | solution.py:321
  18.1 0.0 copy-start.2
  18.2 13.2 %all_to_all.11.parts = bf16[16,16,512]{2,1,0:T(8,128)(2,1)S(1)} all-to-all(bf16[16,16,512]{2,1,0:T(8,128)(2,1)S(1)} %bottleneck.1), channel_id=1, replica_groups=mesh['row'=16,'col'=2] {'row'}, dimensions={0} | all-to-all | bytes 524288 | tf_op jit(solution)/shard_map/all_to_all | solution.py:330
  31.4 0.0 copy-done
  31.4 0.0 copy-done.1
  31.4 1.0 %raise.1 = (bf16[8,256,128]{2,1,0:T(8,128)(2,1)S(1)}, bf16[2,256,128]{2,1,0:T(8,128)(2,1)S(1)}, bf16[10,32,128]{2,1,0:T(8,128)(2,1)S(1)}) custom-call(bf16[16,16,512]{2,1,0:T(8,128)(2,1)S(1)} %all_to_all.11.parts, bf16[8,256,128]{2,1,0:T(8,128)(2,1)S(1)} %bitcast.12, bf16[4,4,4,32,512]{4,3,2,1,0:T(8,128)(2,1)S(1)} %copy-done), custom_call_target="tpu_custom_call" | custom-call | tf_op jit(solution)/shard_map/raise/pallas_call | solution.py:334
  32.4 0.1 collective-permute-start
  32.5 0.0 copy-done.2
  32.5 0.6 %band.1 = bf16[768,1024]{1,0:T(8,128)(2,1)S(1)} custom-call(bf16[3,3,3,32,32]{4,3,2,1,0:T(8,128)(2,1)S(1)} %copy-done.2, bf16[8,256,128]{2,1,0:T(8,128)(2,1)S(1)} %get-tuple-element.8.after.joined), custom_call_target="tpu_custom_call" | custom-call | flops 500000000 | bytes 5000000 | tf_op jit(solution)/shard_map/band/pallas_call | solution.py:348
  33.1 0.7 %collective-permute-done.rest_0_ = bf16[10,32,128]{2,1,0:T(8,128)(2,1)S(1)} collective-permute-done((bf16[10,32,128]{2,1,0:T(8,128)(2,1)S(1)}, bf16[10,32,128]{2,1,0:T(8,128)(2,1)S(1)}, u32[]{:S(2)}, u32[]{:S(2)}) %collective-permute-start) | collective-permute-done | bytes 81952 | tf_op jit(solution)/shard_map/ppermute | solution.py:343
  33.8 0.8 %collective-permute-start.1 = (bf16[288,128]{1,0:T(8,128)(2,1)S(1)}, bf16[288,128]{1,0:T(8,128)(2,1)S(1)}, u32[]{:S(2)}, u32[]{:S(2)}) collective-permute-start(bf16[288,128]{1,0:T(8,128)(2,1)S(1)} %pad_maximum_fusion), channel_id=1, source_target_pairs={{0,2},{1,3},{2,0},{3,1},{4,6},{5,7},{6,4},{7,5},{8,10},{9,11},{10,... | collective-permute-start | bytes 221192 | tf_op jit(solution)/shard_map/ppermute | solution.py:360
  34.6 0.0 collective-permute-start.2
  34.7 1.7 %interior.1.rest_1_ = bf16[8,256,128]{2,1,0:T(8,128)(2,1)} custom-call(bf16[768,1024]{1,0:T(8,128)(2,1)S(1)} %band.1, bf16[8,256,128]{2,1,0:T(8,128)(2,1)S(1)} %get-tuple-element.8.after.joined, bf16[10,32,128]{2,1,0:T(8,128)(2,1)S(1)} %collective-permute-done.rest_0_), custom_call_target="tpu_custom_call" | custom-call | flops 3000000000 | bytes 30000000 | tf_op jit(solution)/shard_map/interior/pallas_call | solution.py:363
  36.3 2.7 %collective-permute-done.1.near = bf16[288,128]{1,0:T(8,128)(2,1)S(1)} collective-permute-done((bf16[288,128]{1,0:T(8,128)(2,1)S(1)}, bf16[288,128]{1,0:T(8,128)(2,1)S(1)}, u32[]{:S(2)}, u32[]{:S(2)}) %collective-permute-start.1) | collective-permute-done | bytes 73760 | tf_op jit(solution)/shard_map/ppermute | solution.py:360
  39.0 0.0 collective-permute-done.2.far
  39.0 1.2 %edge.1 = bf16[8,256,128]{2,1,0:T(8,128)(2,1)} custom-call(bf16[768,1024]{1,0:T(8,128)(2,1)S(1)} %band.1, bf16[8,256,128]{2,1,0:T(8,128)(2,1)S(1)} %get-tuple-element.8.after.joined, bf16[288,128]{1,0:T(8,128)(2,1)S(1)} %collective-permute-done.1.near, bf16[288,128]{1,0:T(8,128)(2,1)S(1)} %collective-permute-done.2.far, ...), custom_call_target="tpu_custom_call", output_to_operand_aliasing={{}: (5, {})} | custom-call | flops 1000000000 | bytes 10000000 | tf_op jit(solution)/shard_map/edge/pallas_call | solution.py:377
  (4 shorter events, 0.0 us)
Async XLA Ops:
  0.0 17.6 %copy-start.3 = (bf16[3,3,3,32,512]{4,3,2,1,0:T(8,128)(2,1)S(1)}, bf16[3,3,3,32,512]{4,3,2,1,0:T(8,128)(2,1)}, u32[]{:S(2)}) copy-start(bf16[3,3,3,32,512]{4,3,2,1,0:T(8,128)(2,1)} %refs_1_.1) | copy-start | bytes 2654212
  17.6 13.8 %copy-start = (bf16[4,4,4,32,512]{4,3,2,1,0:T(8,128)(2,1)S(1)}, bf16[4,4,4,32,512]{4,3,2,1,0:T(8,128)(2,1)}, u32[]{:S(2)}) copy-start(bf16[4,4,4,32,512]{4,3,2,1,0:T(8,128)(2,1)} %up.1) | copy-start | bytes 6291460
  17.6 13.8 %copy-start.1 = (bf16[8,32,8,128]{3,2,1,0:T(8,128)(2,1)S(1)}, bf16[8,32,8,128]{3,2,1,0:T(8,128)(2,1)}, u32[]{:S(2)}) copy-start(bf16[8,32,8,128]{3,2,1,0:T(8,128)(2,1)} %param.5) | copy-start | bytes 1572868
  18.1 14.4 %copy-start.2 = (bf16[3,3,3,32,32]{4,3,2,1,0:T(8,128)(2,1)S(1)}, bf16[3,3,3,32,32]{4,3,2,1,0:T(8,128)(2,1)}, u32[]{:S(2)}) copy-start(bf16[3,3,3,32,32]{4,3,2,1,0:T(8,128)(2,1)} %dec.1) | copy-start | bytes 165892
  32.4 1.3 %collective-permute-start = (bf16[10,32,128]{2,1,0:T(8,128)(2,1)S(1)}, bf16[10,32,128]{2,1,0:T(8,128)(2,1)S(1)}, u32[]{:S(2)}, u32[]{:S(2)}) collective-permute-start(bf16[10,32,128]{2,1,0:T(8,128)(2,1)S(1)} %get-tuple-element.10), channel_id=1, source_target_pairs={{0,1},{1,0},{2,3},{3,2},{4,5},{5,4},{6,7},{7,6},{8,9},{9,8},{10,11... | collective-permute-start | bytes 245768 | tf_op jit(solution)/shard_map/ppermute | solution.py:343
  33.8 5.2 %collective-permute-start.1 = (bf16[288,128]{1,0:T(8,128)(2,1)S(1)}, bf16[288,128]{1,0:T(8,128)(2,1)S(1)}, u32[]{:S(2)}, u32[]{:S(2)}) collective-permute-start(bf16[288,128]{1,0:T(8,128)(2,1)S(1)} %pad_maximum_fusion), channel_id=1, source_target_pairs={{0,2},{1,3},{2,0},{3,1},{4,6},{5,7},{6,4},{7,5},{8,10},{9,11},{10,... | collective-permute-start | bytes 221192 | tf_op jit(solution)/shard_map/ppermute | solution.py:360
  34.6 4.3 %collective-permute-start.2 = (bf16[288,128]{1,0:T(8,128)(2,1)S(1)}, bf16[288,128]{1,0:T(8,128)(2,1)S(1)}, u32[]{:S(2)}, u32[]{:S(2)}) collective-permute-start(bf16[288,128]{1,0:T(8,128)(2,1)S(1)} %pad_maximum_fusion.1), channel_id=1, source_target_pairs={{0,1},{1,0},{2,4},{3,5},{4,2},{5,3},{6,8},{7,9},{8,6},{9,7},{10,12... | collective-permute-start | bytes 221192 | tf_op jit(solution)/shard_map/ppermute | solution.py:360

commit v3 on v2

--- a/solution.py
+++ b/solution.py
@@ -28,22 +28,12 @@
     return half + half * jnp.tanh(half)
 
 
-def lower_kernel(count, repeat, chans, height, feat_hbm, down_hbm, out, feat, down, sems):
+def lowered_rows(height, chans, loads, feat, down):
     planes, rows, width = feat.shape
     quarters = planes // 2
-    loads = [
-        pltpu.make_async_copy(feat_hbm.at[2 * a : 2 * a + 2], feat.at[2 * a : 2 * a + 2], sems.at[a])
-        for a in range(quarters)
-    ] + [
-        pltpu.make_async_copy(down_hbm.at[a], down.at[a], sems.at[quarters + a]) for a in range(quarters)
-    ]
-    for load in loads:
-        load.start()
     coarse = width // 8
-    half = height // 2
     top = down.shape[4]
-    each = top // count
-    shape = (half * chans, rows)
+    shape = (height // 2 * chans, rows)
     r, c = iota(shape, 0), iota(shape, 1)
     pick = ((r % chans == c // height) & (r // chans == (c % height) // 2)).astype(F32).astype(BF16)
     shape = (4 * coarse, width)
@@ -58,50 +48,129 @@
         loads[quarters + a].wait()
         for c in range(4):
             low = low + dot(pooled[a][c * coarse : (c + 1) * coarse], down[a, :, c].reshape(-1, top))
-    low = silu(low)
+    return silu(low)
+
+
+def input_loads(feat_hbm, down_hbm, feat, down, sems):
+    quarters = feat.shape[0] // 2
+    return [
+        pltpu.make_async_copy(feat_hbm.at[2 * a : 2 * a + 2], feat.at[2 * a : 2 * a + 2], sems.at[a])
+        for a in range(quarters)
+    ] + [
+        pltpu.make_async_copy(down_hbm.at[a], down.at[a], sems.at[quarters + a]) for a in range(quarters)
+    ]
+
+
+def lower_kernel(count, chans, height, feat_hbm, down_hbm, out, feat, down, sems):
+    loads = input_loads(feat_hbm, down_hbm, feat, down, sems)
+    for load in loads:
+        load.start()
+    low = lowered_rows(height, chans, loads, feat, down)
+    coarse = low.shape[0]
+    each = low.shape[1] // count
     place = iota(low.shape, 0)
     before = jnp.where(place == 0, 0.0, pltpu.roll(low, 1, 0))
     after = jnp.where(place == coarse - 1, 0.0, pltpu.roll(low, coarse - 1, 0))
     for k in range(count):
         part = slice(k * each, (k + 1) * each)
-        block = jnp.concatenate([before[:, part], low[:, part], after[:, part]], axis=1).astype(BF16)
-        for e in range(repeat):
-            out[repeat * k + e] = block
-
-
-def bottleneck_kernel(joint, blocks, *refs):
-    if joint:
-        got, weight, out = refs[:3]
-        pads = refs[3:]
-        col = lax.axis_index("col")
-        sources = [(got[:, col], 1), (got[:, 1 - col], 2 - 2 * col)]
-    else:
-        weight, out = refs[blocks : blocks + 2]
-        pads = refs[blocks + 2 :]
-        sources = [(refs[k][...], k) for k in range(blocks)]
+        out[k] = jnp.concatenate([before[:, part], low[:, part], after[:, part]], axis=1).astype(BF16)
+
+
+def quarter(row, col, size):
+    return pl.multiple_of((2 * (row % 2) + col) * size, size)
+
+
+def lower_pair_kernel(count, chans, height, feat_hbm, down_hbm, bott_hbm, out, keep, give, feat, down, sems):
+    loads = input_loads(feat_hbm, down_hbm, feat, down, sems)
+    row, col = lax.axis_index("row"), lax.axis_index("col")
+    size = keep.shape[4]
+    quarters = [
+        pltpu.make_async_copy(
+            bott_hbm.at[:, :, :, :, pl.ds(quarter(owner, col, size), size)], held, sems.at[len(loads) + k]
+        )
+        for k, (owner, held) in enumerate(((row + 1, give), (row, keep)))
+    ]
+    for load in loads + quarters:
+        load.start()
+    low = lowered_rows(height, chans, loads, feat, down)
+    half = low.shape[0] // 2
+    each = low.shape[1] // count
+    for k in range(count):
+        pieces = []
+        for rows in (slice(0, half), slice(half, 2 * half)):
+            for owner in (k, k ^ 1):
+                pieces.append(low[rows, owner * each : (owner + 1) * each])
+        block = jnp.concatenate(pieces, axis=1).astype(BF16)
+        out[2 * k] = block
+        out[2 * k + 1] = block
+    for load in quarters:
+        load.wait()
+
+
+def bottleneck_kernel(*refs):
+    blocks, weight, out, pads = refs[:3], refs[3], refs[4], refs[5:]
     depth, coarse, top = out.shape
     rows = depth * coarse
     lanes = 3 * weight.shape[3]
     total = jnp.zeros((rows, top), F32)
-    for (block, tap), pad in zip(sources, pads):
+    for tap, (block, pad) in enumerate(zip(blocks, pads)):
         zero = jnp.zeros((coarse, lanes), BF16)
         pad[:coarse] = zero
         pad[coarse + rows :] = zero
-        pad[coarse : coarse + rows] = block.reshape(rows, lanes)
+        pad[coarse : coarse + rows] = block[...].reshape(rows, lanes)
         for a in range(3):
             kernel = weight[a, tap].reshape(lanes, top)
             total = total + dot(pad[a * coarse : a * coarse + rows], kernel)
     out[...] = total.astype(BF16).reshape(out.shape)
 
 
+def bottleneck_pair_kernel(got, keep, took, out, pad):
+    depth, _, half, lanes = got.shape
+    group = lanes // 2
+    coarse = 2 * half
+    rows = depth * coarse
+    lane = iota((half, lanes), 1)
+    blocks = []
+    for d in range(depth):
+        low, high = got[d, 0].astype(F32), got[d, 1].astype(F32)
+        blocks.append(jnp.where(lane < group, low, pltpu.roll(high, group, 1)))
+        blocks.append(jnp.where(lane < group, pltpu.roll(low, group, 1), high))
+    here = jnp.concatenate(blocks, axis=0)
+    place = iota((rows, lanes), 0) % coarse
+    before = jnp.where(place == 0, 0.0, pltpu.roll(here, 1, 0))
+    after = jnp.where(place == coarse - 1, 0.0, pltpu.roll(here, rows - 1, 0))
+    zero = jnp.zeros((coarse, 3 * lanes), BF16)
+    pad[:coarse] = zero
+    pad[coarse + rows :] = zero
+    for c, value in enumerate((before, here, after)):
+        pad[coarse : coarse + rows, c * lanes : (c + 1) * lanes] = value.astype(BF16)
+    total = None
+    for a in range(3):
+        bands = []
+        for c in range(3):
+            for source in range(2):
+                for held in (keep, took):
+                    bands.append(jnp.concatenate([held[a, source - h + 1, c] for h in range(2)], axis=1))
+        term = dot(pad[a * coarse : a * coarse + rows], jnp.concatenate(bands, axis=0))
+        total = term if total is None else total + term
+    size = out.shape[2]
+    for h in range(2):
+        for d in range(depth):
+            out[2 * d + h] = total[d * coarse : (d + 1) * coarse, h * size : (h + 1) * size].astype(BF16)
+
+
 def raise_kernel(chans, height, parts, feat, up, joined, ends, *rest):
     sides, spread = rest[:-1], rest[-1]
     planes, rows, width = feat.shape
     coarse = width // 8
-    total = parts[0].astype(F32)
-    for k in range(1, parts.shape[0]):
-        total = total + parts[k].astype(F32)
-    middle = silu(total).astype(BF16)
+    groups = up.shape[4] // parts.shape[2]
+    sums = []
+    for q in range(groups):
+        total = parts[q].astype(F32)
+        for k in range(q + groups, parts.shape[0], groups):
+            total = total + parts[k].astype(F32)
+        sums.append(total)
+    middle = silu(sums[0] if groups == 1 else jnp.concatenate(sums, axis=1)).astype(BF16)
     shape = (4 * width, coarse)
     r, c = iota(shape, 0), iota(shape, 1)
     pick = (((r % width) // 8 == c) & ((r % 8) // 2 == r // width)).astype(F32).astype(BF16)
@@ -298,36 +367,54 @@
     feat = features.reshape(depth, rows, width)
 
     sems = lambda n: pltpu.SemaphoreType.DMA((n,))
-    lower = functools.partial(lower_kernel, count, 2 if cols == 2 else 1, chans, height)
-    lowered = call(
-        lower,
-        "lower",
-        bf16((2 if cols == 2 else 1) * count, coarse, 3 * each),
-        [HBM, HBM],
-        VMEM,
-        [pltpu.VMEM(feat.shape, BF16), pltpu.VMEM(down_weight.shape, BF16), sems(depth)],
-        limit=24, cost=1_000_000_000,
-    )(fixed(feat), fixed(down_weight))
+    scratch = [pltpu.VMEM(feat.shape, BF16), pltpu.VMEM(down_weight.shape, BF16)]
     up_one = [(i, i + 1) for i in range(cols - 1)]
     down_one = [(i + 1, i) for i in range(cols - 1)]
     if cols == 2:
+        size = top // 4
+        held = bf16(3, 3, 3, each, size)
+        lowered, keep, give = call(
+            functools.partial(lower_pair_kernel, count, chans, height),
+            "lower",
+            (bf16(2 * count, coarse // 2, 4 * each), held, held),
+            [HBM] * 3,
+            (VMEM,) * 3,
+            scratch + [sems(depth + 2)],
+            cost=1_000_000_000,
+        )(fixed(feat), fixed(down_weight), fixed(bott_weight))
+        took = lax.ppermute(give, "row", [(i, i ^ 1) for i in range(count)])
         got = lax.all_to_all(lowered, ("row", "col"), split_axis=0, concat_axis=0, tiled=True)
-        blocks = [got.reshape(count, cols, coarse, 3 * each)]
-        sides = 2
+        shares = call(
+            bottleneck_pair_kernel,
+            "bottleneck",
+            bf16(2 * count, coarse, size),
+            [VMEM] * 3,
+            VMEM,
+            [pltpu.VMEM(((count + 2) * coarse, 12 * each), BF16)],
+            cost=2_000_000_000,
+        )(got.reshape(count, 2, coarse // 2, 4 * each), keep, took)
+        parts = lax.all_to_all(shares, ("row", "col"), split_axis=0, concat_axis=0, tiled=True)
     else:
+        lowered = call(
+            functools.partial(lower_kernel, count, chans, height),
+            "lower",
+            bf16(count, coarse, 3 * each),
+            [HBM] * 2,
+            VMEM,
+            scratch + [sems(depth)],
+            cost=1_000_000_000,
+        )(fixed(feat), fixed(down_weight))
         own = lax.all_to_all(lowered, "row", split_axis=0, concat_axis=0, tiled=True)
-        blocks = [lax.ppermute(own, "col", up_one), own, lax.ppermute(own, "col", down_one)]
-        sides = 3
-    shares = call(
-        functools.partial(bottleneck_kernel, cols == 2, sides),
-        "bottleneck",
-        bf16(count, coarse, top),
-        [VMEM] * (len(blocks) + 1),
-        VMEM,
-        [pltpu.VMEM(((count + 2) * coarse, 3 * each), BF16) for _ in range(sides)],
-        cost=2_000_000_000,
-    )(*blocks, bott_weight)
-    parts = lax.all_to_all(shares, "row", split_axis=0, concat_axis=0, tiled=True)
+        shares = call(
+            bottleneck_kernel,
+            "bottleneck",
+            bf16(count, coarse, top),
+            [VMEM] * 4,
+            VMEM,
+            [pltpu.VMEM(((count + 2) * coarse, 3 * each), BF16)] * 3,
+            cost=2_000_000_000,
+        )(lax.ppermute(own, "col", up_one), own, lax.ppermute(own, "col", down_one), bott_weight)
+        parts = lax.all_to_all(shares, "row", split_axis=0, concat_axis=0, tiled=True)
 
     side = bf16(depth + 2, chans, width)
     sides = 1 if cols == 2 else 2

time: 40.3 us -> 36.8 us (0.913)
  blocking collectives: 28.6 us -> 22.2 us
  starting transfers between devices: 0.92 us -> 3.72 us
    all_to_all x1, blocking collectives: 15.3 us -> 12.1 us  [body(): lax.all_to_all(lowered, ('row', 'col'), split_axis=0, concat_axis=0, tile...]
    all_to_all x1, blocking collectives: 13.2 us -> 10 us  [body(): lax.all_to_all(shares, ('row', 'col'), split_axis=0, concat_axis=0, tiled...]
    ppermute x0 -> x1, starting transfers between devices: none -> 3.03 us  [body(): took = lax.ppermute(give, 'row', [(i, i ^ 1) for i in range(count)])]
    ppermute x2, waiting for transfers between devices: 2.65 us -> 3.12 us  [body(): got.append(lax.ppermute(sent, ('row', 'col'), pairs))]
    ppermute x2, starting transfers between devices: 0.85 us -> 0.41 us  [body(): got.append(lax.ppermute(sent, ('row', 'col'), pairs))]
  transfers between devices with their start and end apart: 3 -> 4, of which waited for: 2 -> 2; matrix products, arithmetic and copies ran while one was open for 0% -> 0% of each run, Pallas kernels for 6% -> 6%
where the time goes in v3:
time: 36.8 us; the launch traced here: 36.6 us
  blocking collectives  22.2 us (60%)
  Pallas kernels  7.02 us (19%)
  starting transfers between devices  3.72 us (10%)
  waiting for transfers between devices  3.58 us (10%)
    all_to_all x1, blocking collectives, body(): lax.all_to_all(lowered, ('row', 'col'), split_axis=0, concat_axis=0, tile...  12.1 us
    all_to_all x1, blocking collectives, body(): lax.all_to_all(shares, ('row', 'col'), split_axis=0, concat_axis=0, tiled...  10 us
    ppermute x2, waiting for transfers between devices, body(): got.append(lax.ppermute(sent, ('row', 'col'), pairs))  3.12 us
    ppermute x1, starting transfers between devices, body(): took = lax.ppermute(give, 'row', [(i, i ^ 1) for i in range(count)])  3.03 us
    pallas_call x1, Pallas kernels, body(): call(functools.partial(lower_pair_kernel, count, chans, height), 'lower',...  2.14 us
    pallas_call x1, Pallas kernels, body(): call(functools.partial(interior_kernel, chans, height), 'interior', shape...  1.66 us
    pallas_call x1, Pallas kernels, body(): call(functools.partial(edge_kernel, chans, height), 'edge', shape, [VMEM]...  1.18 us
    pallas_call x1, Pallas kernels, body(): call(functools.partial(raise_kernel, chans, height), 'raise', (bf16(depth...  1.01 us
  transfers between devices with their start and end apart: 4, of which 2 were waited for; matrix products, arithmetic and copies ran while one was open for 0% of the time, Pallas kernels for 6%

profile of v3, /device:TPU:0, one launch (start us, length us, event | category | flops | bytes accessed | tf_op | source)
XLA Modules:
  0.0 36.6 jit_solution(13823950790919660016)
XLA Ops:
  0.0 2.1 %lower.1 = (bf16[32,8,128]{2,1,0:T(8,128)(2,1)S(1)}, bf16[3,3,3,32,128]{4,3,2,1,0:T(8,128)(2,1)S(1)}, bf16[3,3,3,32,128]{4,3,2,1,0:T(8,128)(2,1)S(1)}) custom-call(bf16[8,256,128]{2,1,0:T(8,128)(2,1)} %bitcast.11, bf16[4,4,4,32,512]{4,3,2,1,0:T(8,128)(2,1)} %down_hbm.1, bf16[3,3,3,32,512]{4,3,2,1,0:T(8,128)(2,1)} %bott_hbm.1), custom_call_target="tpu_custom_call" | custom-call | flops 1000000000 | bytes 10000000 | tf_op jit(solution)/shard_map/lower/pallas_call | solution.py:376
  2.2 3.0 %collective-permute-start = (bf16[3,3,3,32,128]{4,3,2,1,0:T(8,128)(2,1)S(1)}, bf16[3,3,3,32,128]{4,3,2,1,0:T(8,128)(2,1)S(1)}, u32[]{:S(2)}, u32[]{:S(2)}) collective-permute-start(bf16[3,3,3,32,128]{4,3,2,1,0:T(8,128)(2,1)S(1)} %get-tuple-element.13), channel_id=1, source_target_pairs={{0,2},{2,0},{4,6},{6,4},{8,10},{10,8},{12,14},{14,12},{16,18},{18,... | collective-permute-start | bytes 663560 | tf_op jit(solution)/shard_map/ppermute | solution.py:385
  5.2 12.1 %all_to_all.10 = bf16[32,8,128]{2,1,0:T(8,128)(2,1)S(1)} all-to-all(bf16[32,8,128]{2,1,0:T(8,128)(2,1)S(1)} %get-tuple-element.11), channel_id=1, replica_groups=mesh['row'=16,'col'=2] {'row','col'}, dimensions={0} | all-to-all | bytes 131072 | tf_op jit(solution)/shard_map/all_to_all | solution.py:386
  17.3 0.0 collective-permute-done.took
  17.3 0.0 copy-start
  17.3 0.0 copy-start.1
  17.3 0.4 %bottleneck.1 = bf16[32,16,128]{2,1,0:T(8,128)(2,1)S(1)} custom-call(bf16[16,2,8,128]{3,2,1,0:T(8,128)(2,1)S(1)} %bitcast.13, bf16[3,3,3,32,128]{4,3,2,1,0:T(8,128)(2,1)S(1)} %get-tuple-element.12.keep, bf16[3,3,3,32,128]{4,3,2,1,0:T(8,128)(2,1)S(1)} %collective-permute-done.took), custom_call_target="tpu_custom_call" | custom-call | flops 2000000000 | bytes 20000000 | tf_op jit(solution)/shard_map/bottleneck/pallas_call | solution.py:387
  17.8 0.0 copy-start.2
  17.8 10.0 %all_to_all.11.parts = bf16[32,16,128]{2,1,0:T(8,128)(2,1)S(1)} all-to-all(bf16[32,16,128]{2,1,0:T(8,128)(2,1)S(1)} %bottleneck.1), channel_id=1, replica_groups=mesh['row'=16,'col'=2] {'row','col'}, dimensions={0} | all-to-all | bytes 262144 | tf_op jit(solution)/shard_map/all_to_all | solution.py:396
  27.8 0.0 copy-done
  27.8 0.0 copy-done.1
  27.8 1.0 %raise.1 = (bf16[8,256,128]{2,1,0:T(8,128)(2,1)S(1)}, bf16[2,256,128]{2,1,0:T(8,128)(2,1)S(1)}, bf16[10,32,128]{2,1,0:T(8,128)(2,1)S(1)}) custom-call(bf16[32,16,128]{2,1,0:T(8,128)(2,1)S(1)} %all_to_all.11.parts, bf16[8,256,128]{2,1,0:T(8,128)(2,1)S(1)} %bitcast.12, bf16[4,4,4,32,512]{4,3,2,1,0:T(8,128)(2,1)S(1)} %copy-done), custom_call_target="tpu_custom_call" | custom-call | tf_op jit(solution)/shard_map/raise/pallas_call | solution.py:421
  28.8 0.3 collective-permute-start.1
  29.1 0.0 copy-done.2
  29.1 0.6 %band.1 = bf16[768,1024]{1,0:T(8,128)(2,1)S(1)} custom-call(bf16[3,3,3,32,32]{4,3,2,1,0:T(8,128)(2,1)S(1)} %copy-done.2, bf16[8,256,128]{2,1,0:T(8,128)(2,1)S(1)} %get-tuple-element.14.after.joined), custom_call_target="tpu_custom_call" | custom-call | flops 500000000 | bytes 5000000 | tf_op jit(solution)/shard_map/band/pallas_call | solution.py:435
  29.7 0.5 %collective-permute-done.1.rest_0_ = bf16[10,32,128]{2,1,0:T(8,128)(2,1)S(1)} collective-permute-done((bf16[10,32,128]{2,1,0:T(8,128)(2,1)S(1)}, bf16[10,32,128]{2,1,0:T(8,128)(2,1)S(1)}, u32[]{:S(2)}, u32[]{:S(2)}) %collective-permute-start.1) | collective-permute-done | bytes 81952 | tf_op jit(solution)/shard_map/ppermute | solution.py:430
  30.2 0.4 %collective-permute-start.2 = (bf16[288,128]{1,0:T(8,128)(2,1)S(1)}, bf16[288,128]{1,0:T(8,128)(2,1)S(1)}, u32[]{:S(2)}, u32[]{:S(2)}) collective-permute-start(bf16[288,128]{1,0:T(8,128)(2,1)S(1)} %pad_maximum_fusion), channel_id=1, source_target_pairs={{0,2},{1,3},{2,0},{3,1},{4,6},{5,7},{6,4},{7,5},{8,10},{9,11},{10,... | collective-permute-start | bytes 221192 | tf_op jit(solution)/shard_map/ppermute | solution.py:447
  30.6 0.0 collective-permute-start.3
  30.6 1.7 %interior.1.rest_1_ = bf16[8,256,128]{2,1,0:T(8,128)(2,1)} custom-call(bf16[768,1024]{1,0:T(8,128)(2,1)S(1)} %band.1, bf16[8,256,128]{2,1,0:T(8,128)(2,1)S(1)} %get-tuple-element.14.after.joined, bf16[10,32,128]{2,1,0:T(8,128)(2,1)S(1)} %collective-permute-done.1.rest_0_), custom_call_target="tpu_custom_call" | custom-call | flops 3000000000 | bytes 30000000 | tf_op jit(solution)/shard_map/interior/pallas_call | solution.py:450
  32.3 3.1 %collective-permute-done.2.near = bf16[288,128]{1,0:T(8,128)(2,1)S(1)} collective-permute-done((bf16[288,128]{1,0:T(8,128)(2,1)S(1)}, bf16[288,128]{1,0:T(8,128)(2,1)S(1)}, u32[]{:S(2)}, u32[]{:S(2)}) %collective-permute-start.2) | collective-permute-done | bytes 73760 | tf_op jit(solution)/shard_map/ppermute | solution.py:447
  35.4 0.0 collective-permute-done.3.far
  35.4 1.2 %edge.1 = bf16[8,256,128]{2,1,0:T(8,128)(2,1)} custom-call(bf16[768,1024]{1,0:T(8,128)(2,1)S(1)} %band.1, bf16[8,256,128]{2,1,0:T(8,128)(2,1)S(1)} %get-tuple-element.14.after.joined, bf16[288,128]{1,0:T(8,128)(2,1)S(1)} %collective-permute-done.2.near, bf16[288,128]{1,0:T(8,128)(2,1)S(1)} %collective-permute-done.3.far, ...), custom_call_target="tpu_custom_call", output_to_operand_aliasing={{}: (5, {})} | custom-call | flops 1000000000 | bytes 10000000 | tf_op jit(solution)/shard_map/edge/pallas_call | solution.py:464
  (4 shorter events, 0.0 us)
Async XLA Ops:
  2.2 15.2 %collective-permute-start = (bf16[3,3,3,32,128]{4,3,2,1,0:T(8,128)(2,1)S(1)}, bf16[3,3,3,32,128]{4,3,2,1,0:T(8,128)(2,1)S(1)}, u32[]{:S(2)}, u32[]{:S(2)}) collective-permute-start(bf16[3,3,3,32,128]{4,3,2,1,0:T(8,128)(2,1)S(1)} %get-tuple-element.13), channel_id=1, source_target_pairs={{0,2},{2,0},{4,6},{6,4},{8,10},{10,8},{12,14},{14,12},{16,18},{18,... | collective-permute-start | bytes 663560 | tf_op jit(solution)/shard_map/ppermute | solution.py:385
  17.3 10.5 %copy-start = (bf16[4,4,4,32,512]{4,3,2,1,0:T(8,128)(2,1)S(1)}, bf16[4,4,4,32,512]{4,3,2,1,0:T(8,128)(2,1)}, u32[]{:S(2)}) copy-start(bf16[4,4,4,32,512]{4,3,2,1,0:T(8,128)(2,1)} %up.1) | copy-start | bytes 6291460
  17.3 10.5 %copy-start.1 = (bf16[8,32,8,128]{3,2,1,0:T(8,128)(2,1)S(1)}, bf16[8,32,8,128]{3,2,1,0:T(8,128)(2,1)}, u32[]{:S(2)}) copy-start(bf16[8,32,8,128]{3,2,1,0:T(8,128)(2,1)} %param.5) | copy-start | bytes 1572868
  17.8 11.4 %copy-start.2 = (bf16[3,3,3,32,32]{4,3,2,1,0:T(8,128)(2,1)S(1)}, bf16[3,3,3,32,32]{4,3,2,1,0:T(8,128)(2,1)}, u32[]{:S(2)}) copy-start(bf16[3,3,3,32,32]{4,3,2,1,0:T(8,128)(2,1)} %dec.1) | copy-start | bytes 165892
  28.8 1.3 %collective-permute-start.1 = (bf16[10,32,128]{2,1,0:T(8,128)(2,1)S(1)}, bf16[10,32,128]{2,1,0:T(8,128)(2,1)S(1)}, u32[]{:S(2)}, u32[]{:S(2)}) collective-permute-start(bf16[10,32,128]{2,1,0:T(8,128)(2,1)S(1)} %get-tuple-element.16), channel_id=1, source_target_pairs={{0,1},{1,0},{2,3},{3,2},{4,5},{5,4},{6,7},{7,6},{8,9},{9,8},{10,11... | collective-permute-start | bytes 245768 | tf_op jit(solution)/shard_map/ppermute | solution.py:430
  30.2 5.2 %collective-permute-start.2 = (bf16[288,128]{1,0:T(8,128)(2,1)S(1)}, bf16[288,128]{1,0:T(8,128)(2,1)S(1)}, u32[]{:S(2)}, u32[]{:S(2)}) collective-permute-start(bf16[288,128]{1,0:T(8,128)(2,1)S(1)} %pad_maximum_fusion), channel_id=1, source_target_pairs={{0,2},{1,3},{2,0},{3,1},{4,6},{5,7},{6,4},{7,5},{8,10},{9,11},{10,... | collective-permute-start | bytes 221192 | tf_op jit(solution)/shard_map/ppermute | solution.py:447
  30.6 4.8 %collective-permute-start.3 = (bf16[288,128]{1,0:T(8,128)(2,1)S(1)}, bf16[288,128]{1,0:T(8,128)(2,1)S(1)}, u32[]{:S(2)}, u32[]{:S(2)}) collective-permute-start(bf16[288,128]{1,0:T(8,128)(2,1)S(1)} %pad_maximum_fusion.1), channel_id=1, source_target_pairs={{0,1},{1,0},{2,4},{3,5},{4,2},{5,3},{6,8},{7,9},{8,6},{9,7},{10,12... | collective-permute-start | bytes 221192 | tf_op jit(solution)/shard_map/ppermute | solution.py:447

commit v4 on v3

--- a/solution.py
+++ b/solution.py
@@ -6,6 +6,7 @@
 from jax.experimental import pallas as pl
 from jax.experimental.pallas import tpu as pltpu
 from jax.sharding import PartitionSpec as P
+
 
 F32, BF16 = jnp.float32, jnp.bfloat16
 NT = (((1,), (1,)), ((), ()))
@@ -83,12 +84,16 @@
 def lower_pair_kernel(count, chans, height, feat_hbm, down_hbm, bott_hbm, out, keep, give, feat, down, sems):
     loads = input_loads(feat_hbm, down_hbm, feat, down, sems)
     row, col = lax.axis_index("row"), lax.axis_index("col")
-    size = keep.shape[4]
+    taps, size = keep.shape
+    edge = (feat.shape[0] - 1) * (1 - row % 2)
     quarters = [
         pltpu.make_async_copy(
-            bott_hbm.at[:, :, :, :, pl.ds(quarter(owner, col, size), size)], held, sems.at[len(loads) + k]
-        )
-        for k, (owner, held) in enumerate(((row + 1, give), (row, keep)))
+            bott_hbm.at[:, pl.ds(quarter(row + 1, col, size), size)], give.at[:taps], sems.at[len(loads)]
+        ),
+        pltpu.make_async_copy(feat_hbm.at[edge], give.at[taps:], sems.at[len(loads) + 1]),
+        pltpu.make_async_copy(
+            bott_hbm.at[:, pl.ds(quarter(row, col, size), size)], keep, sems.at[len(loads) + 2]
+        ),
     ]
     for load in loads + quarters:
         load.start()
@@ -129,6 +134,7 @@
     group = lanes // 2
     coarse = 2 * half
     rows = depth * coarse
+    each = group // 2
     lane = iota((half, lanes), 1)
     blocks = []
     for d in range(depth):
@@ -150,7 +156,8 @@
         for c in range(3):
             for source in range(2):
                 for held in (keep, took):
-                    bands.append(jnp.concatenate([held[a, source - h + 1, c] for h in range(2)], axis=1))
+                    at = [((3 * a + source - h + 1) * 3 + c) * each for h in range(2)]
+                    bands.append(jnp.concatenate([held[k : k + each] for k in at], axis=1))
         term = dot(pad[a * coarse : a * coarse + rows], jnp.concatenate(bands, axis=0))
         total = term if total is None else total + term
     size = out.shape[2]
@@ -159,7 +166,7 @@
             out[2 * d + h] = total[d * coarse : (d + 1) * coarse, h * size : (h + 1) * size].astype(BF16)
 
 
-def raise_kernel(chans, height, parts, feat, up, joined, ends, *rest):
+def raise_kernel(chans, height, parts, feat, up, joined, first, second, *rest):
     sides, spread = rest[:-1], rest[-1]
     planes, rows, width = feat.shape
     coarse = width // 8
@@ -189,8 +196,11 @@
             joined[d, h * chans : (h + 1) * chans] = value.astype(BF16)
     odd = lax.axis_index("row") % 2
     near, far = (planes - 1) * (1 - odd), (planes - 1) * odd
-    ends[0] = joined[near]
-    ends[1] = joined[far]
+    if first.shape[0] == rows:
+        first[...] = joined[near]
+    else:
+        first[...] = jnp.where(odd == 1, raised[:per], raised[-per:]).astype(BF16)
+    second[...] = joined[far]
     if len(sides) == 1:
         starts = [pl.multiple_of((rows - chans) * (1 - lax.axis_index("col")), chans)]
     else:
@@ -278,26 +288,35 @@
         copy.wait()
 
 
-def edge_kernel(chans, height, band, joined, near, far, *rest):
+def nearby_kernel(chans, height, took, near, plane, corner, spread):
+    rows = plane.shape[0]
+    spread[...] = took[-rows:].astype(F32)
+    for h in range(height):
+        at = (h // 2) * chans
+        value = spread[pl.ds(h, chans, stride=height), :] + near[at : at + chans].astype(F32)
+        plane[h * chans : (h + 1) * chans] = value.astype(BF16)
+    corner[...] = plane[pl.ds(pl.multiple_of((rows - chans) * (1 - lax.axis_index("col")), chans), chans)]
+
+
+def edge_kernel(chans, height, band, joined, near, near_rows, far, far_rows, *rest):
     sides, (mid_hbm, out_hbm, field, spread, held, sems) = rest[:-6], rest[-6:]
-    planes, rows, width = joined.shape
+    planes, _, width = joined.shape
     for slot, d in ((1, 0), (2, 1), (3, planes - 2), (4, planes - 1)):
         fill(field, slot, chans, joined[d], [side[d] for side in sides])
     row, last = lax.axis_index("row"), lax.axis_size("row") - 1
 
-    def outer(slot, got):
-        borders = [got[rows + k * chans : rows + (k + 1) * chans] for k in range(len(sides))]
-        fill(field, slot, chans, got[:rows], borders)
+    def outer(slot, plane, corners):
+        fill(field, slot, chans, plane[...], [corners[k * chans : (k + 1) * chans] for k in range(len(sides))])
 
     @pl.when(row % 2 == 0)
     def _():
-        outer(0, far[...])
-        outer(5, near[...])
+        outer(0, far, far_rows)
+        outer(5, near, near_rows)
 
     @pl.when(row % 2 == 1)
     def _():
-        outer(0, near[...])
-        outer(5, far[...])
+        outer(0, near, near_rows)
+        outer(5, far, far_rows)
 
     @pl.when(row == 0)
     def _():
@@ -329,7 +348,7 @@
     return pltpu.with_memory_space_constraint(x, pltpu.MemorySpace.HBM)
 
 
-def call(kernel, name, shape, ins, out, scratch=(), aliases=None, cost=0, limit=24):
+def call(kernel, shape, ins, out, scratch=(), aliases=None, cost=0, limit=24):
     return pl.pallas_call(
         kernel,
         out_shape=shape,
@@ -337,7 +356,6 @@
         out_specs=out,
         scratch_shapes=list(scratch),
         input_output_aliases=aliases or {},
-        name=name,
         cost_estimate=pl.CostEstimate(flops=cost, bytes_accessed=cost // 100, transcendentals=0),
         compiler_params=pltpu.CompilerParams(vmem_limit_bytes=limit << 20),
     )
@@ -359,7 +377,7 @@
     return first, second
 
 
-def body(features, down_weight, bott_weight, up_weight, dec_weight):
+def level(features, down_weight, bott_weight, up_weight, dec_weight):
     depth, chans, height, width = features.shape
     count, cols = lax.axis_size("row"), lax.axis_size("col")
     top = down_weight.shape[4]
@@ -370,23 +388,22 @@
     scratch = [pltpu.VMEM(feat.shape, BF16), pltpu.VMEM(down_weight.shape, BF16)]
     up_one = [(i, i + 1) for i in range(cols - 1)]
     down_one = [(i + 1, i) for i in range(cols - 1)]
-    if cols == 2:
+    paired = cols == 2 and top // 4 == width
+    if paired:
         size = top // 4
-        held = bf16(3, 3, 3, each, size)
+        taps = bott_weight.shape[0] * bott_weight.shape[1] * bott_weight.shape[2] * each
         lowered, keep, give = call(
             functools.partial(lower_pair_kernel, count, chans, height),
-            "lower",
-            (bf16(2 * count, coarse // 2, 4 * each), held, held),
+            (bf16(2 * count, coarse // 2, 4 * each), bf16(taps, size), bf16(taps + rows, size)),
             [HBM] * 3,
             (VMEM,) * 3,
-            scratch + [sems(depth + 2)],
+            scratch + [sems(depth + 3)],
             cost=1_000_000_000,
-        )(fixed(feat), fixed(down_weight), fixed(bott_weight))
+        )(fixed(feat), fixed(down_weight), fixed(bott_weight.reshape(taps, top)))
         took = lax.ppermute(give, "row", [(i, i ^ 1) for i in range(count)])
         got = lax.all_to_all(lowered, ("row", "col"), split_axis=0, concat_axis=0, tiled=True)
         shares = call(
             bottleneck_pair_kernel,
-            "bottleneck",
             bf16(2 * count, coarse, size),
             [VMEM] * 3,
             VMEM,
@@ -397,7 +414,6 @@
     else:
         lowered = call(
             functools.partial(lower_kernel, count, chans, height),
-            "lower",
             bf16(count, coarse, 3 * each),
             [HBM] * 2,
             VMEM,
@@ -407,7 +423,6 @@
         own = lax.all_to_all(lowered, "row", split_axis=0, concat_axis=0, tiled=True)
         shares = call(
             bottleneck_kernel,
-            "bottleneck",
             bf16(count, coarse, top),
             [VMEM] * 4,
             VMEM,
@@ -418,14 +433,14 @@
 
     side = bf16(depth + 2, chans, width)
     sides = 1 if cols == 2 else 2
-    joined, ends, *sides = call(
+    joined, *ends = call(
         functools.partial(raise_kernel, chans, height),
-        "raise",
-        (bf16(depth, rows, width), bf16(2, rows, width)) + (side,) * sides,
+        (bf16(depth, rows, width), bf16(rows // 2 if paired else rows, width), bf16(rows, width)) + (side,) * sides,
         [VMEM] * 3,
-        (VMEM,) * (2 + sides),
+        (VMEM,) * (3 + sides),
         [pltpu.VMEM(feat.shape, F32)],
     )(parts, feat, up_weight)
+    ends, sides = ends[:2], ends[2:]
     if cols == 2:
         sides = [lax.ppermute(sides[0], "col", up_one + down_one)]
     else:
@@ -434,7 +449,6 @@
     span = rows + 2 * chans
     band = call(
         functools.partial(band_kernel, chans, height),
-        "band",
         bf16(3 * rows, -(-3 * span // 128) * 128),
         [VMEM, HBM],
         VMEM,
@@ -443,13 +457,24 @@
 
     got = []
     for k, pairs in enumerate(neighbour_swaps(count, cols)):
-        sent = jnp.concatenate([ends[k]] + [side[depth + k] for side in sides], axis=0)
-        got.append(lax.ppermute(sent, ("row", "col"), pairs))
+        alone = paired and k == 0
+        sent = ends[k] if alone else jnp.concatenate([ends[k]] + [side[depth + k] for side in sides], axis=0)
+        swapped = lax.ppermute(sent, ("row", "col"), pairs)
+        if alone:
+            plane, corner = call(
+                functools.partial(nearby_kernel, chans, height),
+                (bf16(rows, width), bf16(chans, width)),
+                [VMEM] * 2,
+                (VMEM,) * 2,
+                [pltpu.VMEM((rows, width), F32)],
+            )(took, swapped)
+            got += [plane, lax.ppermute(corner, "col", up_one + down_one)]
+        else:
+            got += [swapped[:rows], swapped[rows:]]
 
     shape = bf16(depth, rows, width)
     inner = call(
         functools.partial(interior_kernel, chans, height),
-        "interior",
         shape,
         [VMEM] * (2 + len(sides)),
         HBM,
@@ -463,9 +488,8 @@
     )(band, joined, *sides)
     decoded = call(
         functools.partial(edge_kernel, chans, height),
-        "edge",
         shape,
-        [VMEM] * (4 + len(sides)) + [HBM],
+        [VMEM] * (6 + len(sides)) + [HBM],
         HBM,
         [
             pltpu.VMEM((height + 2, 6 * chans, width), BF16),
@@ -473,7 +497,7 @@
             pltpu.VMEM((2, rows, width), BF16),
             sems(2),
         ],
-        aliases={4 + len(sides): 0},
+        aliases={6 + len(sides): 0},
         cost=1_000_000_000,
     )(band, joined, *got, *sides, inner)
     return decoded.reshape(depth, chans, height, width)
@@ -481,6 +505,4 @@
 
 def solution(mesh):
     placed = (P("row", None, "col", None), P(), P(None, None, None, "row", None), P(), P())
-    return jax.shard_map(
-        body, mesh=mesh, in_specs=placed, out_specs=P("row", None, "col", None), check_vma=False
-    )
+    return jax.shard_map(level, mesh=mesh, in_specs=placed, out_specs=P("row", None, "col", None), check_vma=False)

time: 36.8 us -> 38.6 us (1.049)
  the two profiles are of different devices: /device:TPU:0 before, /device:TPU:8 now
where the time goes in v4:
time: 38.6 us; the launch traced here: 38.4 us
  blocking collectives  21.2 us (55%)
  Pallas kernels  7.06 us (18%)
  waiting for transfers between devices  5.95 us (15%)
  starting transfers between devices  4 us (10%)
    all_to_all x1, blocking collectives, level(): lax.all_to_all(lowered, ('row', 'col'), split_axis=0, concat_axis=0, tile...  11.2 us
    all_to_all x1, blocking collectives, level(): lax.all_to_all(shares, ('row', 'col'), split_axis=0, concat_axis=0, tiled...  10.1 us
    ppermute x2, waiting for transfers between devices, level(): swapped = lax.ppermute(sent, ('row', 'col'), pairs)  5.94 us
    ppermute x2, starting transfers between devices, level(): swapped = lax.ppermute(sent, ('row', 'col'), pairs)  2.3 us
    pallas_call x1, Pallas kernels, level(): call(functools.partial(lower_pair_kernel, count, chans, height), (bf16(2...  2.16 us
    pallas_call x1, Pallas kernels, level(): call(functools.partial(interior_kernel, chans, height), shape, [VMEM] * (...  1.65 us
    ppermute x1, starting transfers between devices, level(): took = lax.ppermute(give, 'row', [(i, i ^ 1) for i in range(count)])  1.56 us
    pallas_call x1, Pallas kernels, level(): call(functools.partial(edge_kernel, chans, height), shape, [VMEM] * (6 +...  1.19 us
  transfers between devices with their start and end apart: 5, of which 2 were waited for; matrix products, arithmetic and copies ran while one was open for 0% of the time, Pallas kernels for 6%

profile of v4, /device:TPU:8, one launch (start us, length us, event | category | flops | bytes accessed | tf_op | source)
XLA Modules:
  0.0 38.4 jit_solution(1205335065103209331)
XLA Ops:
  0.0 2.2 %shard_map.55 = (bf16[32,8,128]{2,1,0:T(8,128)(2,1)S(1)}, bf16[864,128]{1,0:T(8,128)(2,1)S(1)}, bf16[1120,128]{1,0:T(8,128)(2,1)S(1)}) custom-call(bf16[8,256,128]{2,1,0:T(8,128)(2,1)} %bitcast.6, bf16[4,4,4,32,512]{4,3,2,1,0:T(8,128)(2,1)} %down_hbm.1, bf16[864,512]{1,0:T(8,128)(2,1)} %bitcast.9), custom_call_target="tpu_custom_call" | custom-call | flops 1000000000 | bytes 10000000 | tf_op jit(solution)/shard_map/pallas_call | solution.py:395
  2.2 1.6 %collective-permute-start = (bf16[1120,128]{1,0:T(8,128)(2,1)S(1)}, bf16[1120,128]{1,0:T(8,128)(2,1)S(1)}, u32[]{:S(2)}, u32[]{:S(2)}) collective-permute-start(bf16[1120,128]{1,0:T(8,128)(2,1)S(1)} %get-tuple-element.16), channel_id=1, source_target_pairs={{0,2},{2,0},{4,6},{6,4},{8,10},{10,8},{12,14},{14,12},{16,18},{18,... | collective-permute-start | bytes 860168 | tf_op jit(solution)/shard_map/ppermute | solution.py:403
  3.7 11.2 %all_to_all.10 = bf16[32,8,128]{2,1,0:T(8,128)(2,1)S(1)} all-to-all(bf16[32,8,128]{2,1,0:T(8,128)(2,1)S(1)} %get-tuple-element.14), channel_id=1, replica_groups=mesh['row'=16,'col'=2] {'row','col'}, dimensions={0} | all-to-all | bytes 131072 | tf_op jit(solution)/shard_map/all_to_all | solution.py:404
  14.9 0.0 collective-permute-done.took
  14.9 0.0 copy-start
  14.9 0.0 copy-start.1
  14.9 0.4 %shard_map.56 = bf16[32,16,128]{2,1,0:T(8,128)(2,1)S(1)} custom-call(bf16[16,2,8,128]{3,2,1,0:T(8,128)(2,1)S(1)} %bitcast.8, bf16[864,128]{1,0:T(8,128)(2,1)S(1)} %get-tuple-element.15.keep, bf16[1120,128]{1,0:T(8,128)(2,1)S(1)} %collective-permute-done.took), custom_call_target="tpu_custom_call" | custom-call | flops 2000000000 | bytes 20000000 | tf_op jit(solution)/shard_map/pallas_call | solution.py:405
  15.3 0.0 copy-start.2
  15.4 10.1 %all_to_all.11.parts = bf16[32,16,128]{2,1,0:T(8,128)(2,1)S(1)} all-to-all(bf16[32,16,128]{2,1,0:T(8,128)(2,1)S(1)} %shard_map.56), channel_id=1, replica_groups=mesh['row'=16,'col'=2] {'row','col'}, dimensions={0} | all-to-all | bytes 262144 | tf_op jit(solution)/shard_map/all_to_all | solution.py:413
  25.4 0.0 copy-done
  25.4 0.0 copy-done.1
  25.4 1.0 %shard_map.57 = (bf16[8,256,128]{2,1,0:T(8,128)(2,1)S(1)}, bf16[128,128]{1,0:T(8,128)(2,1)S(1)}, bf16[256,128]{1,0:T(8,128)(2,1)S(1)}, bf16[10,32,128]{2,1,0:T(8,128)(2,1)S(1)}) custom-call(bf16[32,16,128]{2,1,0:T(8,128)(2,1)S(1)} %all_to_all.11.parts, bf16[8,256,128]{2,1,0:T(8,128)(2,1)S(1)} %bitcast.7, bf16[4,4,4,32,512]{4,3,2,1,0:T(8,128)(2,1)S(1)} %copy-done), custom_call_target="tpu_custom_call" | custom-call | tf_op jit(solution)/shard_map/pallas_call | solution.py:436
  26.4 0.1 collective-permute-start.3
  26.5 0.6 %collective-permute-start.1 = (bf16[128,128]{1,0:T(8,128)(2,1)S(1)}, bf16[128,128]{1,0:T(8,128)(2,1)S(1)}, u32[]{:S(2)}, u32[]{:S(2)}) collective-permute-start(bf16[128,128]{1,0:T(8,128)(2,1)S(1)} %get-tuple-element.18), channel_id=1, source_target_pairs={{0,2},{1,3},{2,0},{3,1},{4,6},{5,7},{6,4},{7,5},{8,10},{9,11},{10,... | collective-permute-start | bytes 98312 | tf_op jit(solution)/shard_map/ppermute | solution.py:462
  27.1 0.0 copy-done.2
  27.1 0.6 %shard_map.58.band = bf16[768,1024]{1,0:T(8,128)(2,1)S(1)} custom-call(bf16[3,3,3,32,32]{4,3,2,1,0:T(8,128)(2,1)S(1)} %copy-done.2, bf16[8,256,128]{2,1,0:T(8,128)(2,1)S(1)} %get-tuple-element.17.after.joined), custom_call_target="tpu_custom_call" | custom-call | flops 500000000 | bytes 5000000 | tf_op jit(solution)/shard_map/pallas_call | solution.py:450
  27.7 2.8 %collective-permute-done.1.near = bf16[128,128]{1,0:T(8,128)(2,1)S(1)} collective-permute-done((bf16[128,128]{1,0:T(8,128)(2,1)S(1)}, bf16[128,128]{1,0:T(8,128)(2,1)S(1)}, u32[]{:S(2)}, u32[]{:S(2)}) %collective-permute-start.1) | collective-permute-done | bytes 32800 | tf_op jit(solution)/shard_map/ppermute | solution.py:462
  30.5 0.1 collective-permute-start.2
  30.6 0.0 collective-permute-done.3.rest_0_
  30.7 1.8 %collective-permute-start.4 = (bf16[288,128]{1,0:T(8,128)(2,1)S(1)}, bf16[288,128]{1,0:T(8,128)(2,1)S(1)}, u32[]{:S(2)}, u32[]{:S(2)}) collective-permute-start(bf16[288,128]{1,0:T(8,128)(2,1)S(1)} %pad_maximum_fusion), channel_id=1, source_target_pairs={{0,1},{1,0},{2,4},{3,5},{4,2},{5,3},{6,8},{7,9},{8,6},{9,7},{10,12... | collective-permute-start | bytes 221192 | tf_op jit(solution)/shard_map/ppermute | solution.py:462
  32.4 1.7 %shard_map.60.rest_1_ = bf16[8,256,128]{2,1,0:T(8,128)(2,1)} custom-call(bf16[768,1024]{1,0:T(8,128)(2,1)S(1)} %shard_map.58.band, bf16[8,256,128]{2,1,0:T(8,128)(2,1)S(1)} %get-tuple-element.17.after.joined, bf16[10,32,128]{2,1,0:T(8,128)(2,1)S(1)} %collective-permute-done.3.rest_0_), custom_call_target="tpu_custom_call" | custom-call | flops 3000000000 | bytes 30000000 | tf_op jit(solution)/shard_map/pallas_call | solution.py:476
  34.1 3.1 %collective-permute-done.4 = bf16[288,128]{1,0:T(8,128)(2,1)S(1)} collective-permute-done((bf16[288,128]{1,0:T(8,128)(2,1)S(1)}, bf16[288,128]{1,0:T(8,128)(2,1)S(1)}, u32[]{:S(2)}, u32[]{:S(2)}) %collective-permute-start.4) | collective-permute-done | bytes 73760 | tf_op jit(solution)/shard_map/ppermute | solution.py:462
  37.2 0.0 collective-permute-done.2.near_rows
  37.2 1.2 %shard_map.61 = bf16[8,256,128]{2,1,0:T(8,128)(2,1)} custom-call(bf16[768,1024]{1,0:T(8,128)(2,1)S(1)} %shard_map.58.band, bf16[8,256,128]{2,1,0:T(8,128)(2,1)S(1)} %get-tuple-element.17.after.joined, bf16[256,128]{1,0:T(8,128)(2,1)S(1)} %get-tuple-element.19.near, ...), custom_call_target="tpu_custom_call", output_to_operand_aliasing={{}: (7, {})} | custom-call | flops 1000000000 | bytes 10000000 | tf_op jit(solution)/shard_map/pallas_call | solution.py:489
  (5 shorter events, 0.1 us)
Async XLA Ops:
  2.2 12.7 %collective-permute-start = (bf16[1120,128]{1,0:T(8,128)(2,1)S(1)}, bf16[1120,128]{1,0:T(8,128)(2,1)S(1)}, u32[]{:S(2)}, u32[]{:S(2)}) collective-permute-start(bf16[1120,128]{1,0:T(8,128)(2,1)S(1)} %get-tuple-element.16), channel_id=1, source_target_pairs={{0,2},{2,0},{4,6},{6,4},{8,10},{10,8},{12,14},{14,12},{16,18},{18,... | collective-permute-start | bytes 860168 | tf_op jit(solution)/shard_map/ppermute | solution.py:403
  14.9 10.6 %copy-start = (bf16[4,4,4,32,512]{4,3,2,1,0:T(8,128)(2,1)S(1)}, bf16[4,4,4,32,512]{4,3,2,1,0:T(8,128)(2,1)}, u32[]{:S(2)}) copy-start(bf16[4,4,4,32,512]{4,3,2,1,0:T(8,128)(2,1)} %up.1) | copy-start | bytes 6291460
  14.9 10.6 %copy-start.1 = (bf16[8,32,8,128]{3,2,1,0:T(8,128)(2,1)S(1)}, bf16[8,32,8,128]{3,2,1,0:T(8,128)(2,1)}, u32[]{:S(2)}) copy-start(bf16[8,32,8,128]{3,2,1,0:T(8,128)(2,1)} %param.5) | copy-start | bytes 1572868
  15.3 11.7 %copy-start.2 = (bf16[3,3,3,32,32]{4,3,2,1,0:T(8,128)(2,1)S(1)}, bf16[3,3,3,32,32]{4,3,2,1,0:T(8,128)(2,1)}, u32[]{:S(2)}) copy-start(bf16[3,3,3,32,32]{4,3,2,1,0:T(8,128)(2,1)} %dec.1) | copy-start | bytes 165892
  26.4 4.2 %collective-permute-start.3 = (bf16[10,32,128]{2,1,0:T(8,128)(2,1)S(1)}, bf16[10,32,128]{2,1,0:T(8,128)(2,1)S(1)}, u32[]{:S(2)}, u32[]{:S(2)}) collective-permute-start(bf16[10,32,128]{2,1,0:T(8,128)(2,1)S(1)} %get-tuple-element.22), channel_id=1, source_target_pairs={{0,1},{1,0},{2,3},{3,2},{4,5},{5,4},{6,7},{7,6},{8,9},{9,8},{10,11... | collective-permute-start | bytes 245768 | tf_op jit(solution)/shard_map/ppermute | solution.py:445
  26.5 4.0 %collective-permute-start.1 = (bf16[128,128]{1,0:T(8,128)(2,1)S(1)}, bf16[128,128]{1,0:T(8,128)(2,1)S(1)}, u32[]{:S(2)}, u32[]{:S(2)}) collective-permute-start(bf16[128,128]{1,0:T(8,128)(2,1)S(1)} %get-tuple-element.18), channel_id=1, source_target_pairs={{0,2},{1,3},{2,0},{3,1},{4,6},{5,7},{6,4},{7,5},{8,10},{9,11},{10,... | collective-permute-start | bytes 98312 | tf_op jit(solution)/shard_map/ppermute | solution.py:462
  30.5 6.6 %collective-permute-start.2 = (bf16[32,128]{1,0:T(8,128)(2,1)S(1)}, bf16[32,128]{1,0:T(8,128)(2,1)S(1)}, u32[]{:S(2)}, u32[]{:S(2)}) collective-permute-start(bf16[32,128]{1,0:T(8,128)(2,1)S(1)} %get-tuple-element.20), channel_id=1, source_target_pairs={{0,1},{1,0},{2,3},{3,2},{4,5},{5,4},{6,7},{7,6},{8,9},{9,8},{10,11... | collective-permute-start | bytes 24584 | tf_op jit(solution)/shard_map/ppermute | solution.py:471
  30.7 6.5 %collective-permute-start.4 = (bf16[288,128]{1,0:T(8,128)(2,1)S(1)}, bf16[288,128]{1,0:T(8,128)(2,1)S(1)}, u32[]{:S(2)}, u32[]{:S(2)}) collective-permute-start(bf16[288,128]{1,0:T(8,128)(2,1)S(1)} %pad_maximum_fusion), channel_id=1, source_target_pairs={{0,1},{1,0},{2,4},{3,5},{4,2},{5,3},{6,8},{7,9},{8,6},{9,7},{10,12... | collective-permute-start | bytes 221192 | tf_op jit(solution)/shard_map/ppermute | solution.py:462

commit v5 on v4

--- a/solution.py
+++ b/solution.py
@@ -40,26 +40,25 @@
     shape = (4 * coarse, width)
     r, c = iota(shape, 0), iota(shape, 1)
     cols = ((r % coarse == c // 8) & (r // coarse == (c % 8) // 2)).astype(F32).astype(BF16)
-    for a in range(quarters):
-        loads[a].wait()
+    loads[0].wait()
     tables = [(dot(pick, feat[2 * a]) + dot(pick, feat[2 * a + 1])).astype(BF16) for a in range(quarters)]
     pooled = [(dot_nt(cols, table) * 0.125).astype(BF16) for table in tables]
     low = jnp.zeros((coarse, top), F32)
     for a in range(quarters):
-        loads[quarters + a].wait()
+        for load in loads[1 + 2 * a : 3 + 2 * a]:
+            load.wait()
         for c in range(4):
             low = low + dot(pooled[a][c * coarse : (c + 1) * coarse], down[a, :, c].reshape(-1, top))
     return silu(low)
 
 
 def input_loads(feat_hbm, down_hbm, feat, down, sems):
-    quarters = feat.shape[0] // 2
-    return [
-        pltpu.make_async_copy(feat_hbm.at[2 * a : 2 * a + 2], feat.at[2 * a : 2 * a + 2], sems.at[a])
-        for a in range(quarters)
-    ] + [
-        pltpu.make_async_copy(down_hbm.at[a], down.at[a], sems.at[quarters + a]) for a in range(quarters)
-    ]
+    taps, half = down.shape[0], down.shape[1] // 2
+    loads = [pltpu.make_async_copy(feat_hbm, feat, sems.at[0])]
+    for a in range(taps):
+        for part in (slice(0, half), slice(half, 2 * half)):
+            loads.append(pltpu.make_async_copy(down_hbm.at[a, part], down.at[a, part], sems.at[len(loads)]))
+    return loads
 
 
 def lower_kernel(count, chans, height, feat_hbm, down_hbm, out, feat, down, sems):
@@ -166,22 +165,55 @@
             out[2 * d + h] = total[d * coarse : (d + 1) * coarse, h * size : (h + 1) * size].astype(BF16)
 
 
-def raise_kernel(chans, height, parts, feat, up, joined, first, second, *rest):
-    sides, spread = rest[:-1], rest[-1]
+def join(chans, height, plane, raised, spread, store):
+    spread[...] = plane.astype(F32)
+    for h in range(height):
+        at = (h // 2) * chans
+        value = spread[pl.ds(h, chans, stride=height), :] + raised[at : at + chans].astype(F32)
+        store(h * chans, value.astype(BF16))
+
+
+def outer_kernel(chans, height, parts, feat, up, wide, first, second, spread):
     planes, rows, width = feat.shape
-    coarse = width // 8
-    groups = up.shape[4] // parts.shape[2]
+    coarse, top = width // 8, up.shape[4]
+    groups = top // parts.shape[2]
     sums = []
     for q in range(groups):
         total = parts[q].astype(F32)
         for k in range(q + groups, parts.shape[0], groups):
             total = total + parts[k].astype(F32)
         sums.append(total)
-    middle = silu(sums[0] if groups == 1 else jnp.concatenate(sums, axis=1)).astype(BF16)
-    shape = (4 * width, coarse)
-    r, c = iota(shape, 0), iota(shape, 1)
-    pick = (((r % width) // 8 == c) & ((r % 8) // 2 == r // width)).astype(F32).astype(BF16)
-    wide = dot(pick, middle).astype(BF16)
+    middle = silu(sums[0] if groups == 1 else jnp.concatenate(sums, axis=1))
+    spreading = jnp.concatenate([jnp.broadcast_to(middle[w : w + 1], (8, top)) for w in range(coarse)], axis=0)
+    which = iota(spreading.shape, 0) % 8 // 2
+    odd = lax.axis_index("row") % 2
+    last = up.shape[0] - 1
+    steps = (last * (1 - odd), last * odd)
+    raised = None
+    for c in range(4):
+        columns = jnp.where(which == c, spreading, 0.0).astype(BF16)
+        wide[c * width : (c + 1) * width] = columns
+        weight = jnp.concatenate([up[a, :, c].reshape(-1, top) for a in steps], axis=0)
+        term = dot_nt(weight, columns)
+        raised = term if raised is None else raised + term
+    per = raised.shape[0] // 2
+
+    def put(target):
+        def store(at, value):
+            target[at : at + chans] = value
+
+        return store
+
+    if first.shape[0] == rows:
+        join(chans, height, feat[(planes - 1) * (1 - odd)], raised[:per], spread.at[0], put(first))
+    else:
+        first[...] = raised[:per].astype(BF16)
+    join(chans, height, feat[(planes - 1) * odd], raised[per:], spread.at[1], put(second))
+
+
+def raise_kernel(chans, height, wide, feat, up, joined, *rest):
+    sides, spread = rest[:-1], rest[-1]
+    planes, rows, width = feat.shape
     raised = None
     for c in range(4):
         weight = up[:, :, c].reshape(-1, up.shape[4])
@@ -189,18 +221,13 @@
         raised = term if raised is None else raised + term
     per = chans * (height // 2)
     for d in range(planes):
-        spread[d] = feat[d].astype(F32)
-        for h in range(height):
-            start = (d // 2) * per + (h // 2) * chans
-            value = spread[d, pl.ds(h, chans, stride=height), :] + raised[start : start + chans]
-            joined[d, h * chans : (h + 1) * chans] = value.astype(BF16)
+
+        def store(at, value):
+            joined[d, at : at + chans] = value
+
+        join(chans, height, feat[d], raised[d // 2 * per : (d // 2 + 1) * per], spread.at[d], store)
     odd = lax.axis_index("row") % 2
     near, far = (planes - 1) * (1 - odd), (planes - 1) * odd
-    if first.shape[0] == rows:
-        first[...] = joined[near]
-    else:
-        first[...] = jnp.where(odd == 1, raised[:per], raised[-per:]).astype(BF16)
-    second[...] = joined[far]
     if len(sides) == 1:
         starts = [pl.multiple_of((rows - chans) * (1 - lax.axis_index("col")), chans)]
     else:
@@ -208,8 +235,9 @@
     for side, start in zip(sides, starts):
         for d in range(planes):
             side[d] = joined[d, pl.ds(start, chans)]
-        side[planes] = joined[near, pl.ds(start, chans)]
-        side[planes + 1] = joined[far, pl.ds(start, chans)]
+        if side.shape[0] > planes:
+            side[planes] = joined[near, pl.ds(start, chans)]
+            side[planes + 1] = joined[far, pl.ds(start, chans)]
 
 
 def band_kernel(chans, height, dec, after, out):
@@ -223,6 +251,14 @@
             row = h * step + c * chans
             moved = base if h == 0 else pltpu.roll(base, h * step, 1)
             out[row : row + chans] = moved.astype(BF16)
+
+
+def taps_of(chans, part):
+    width = part.shape[1]
+    lane = iota((chans, width), 1)
+    before = jnp.where(lane == 0, 0.0, pltpu.roll(part[:chans], 1, 1))
+    after = jnp.where(lane == width - 1, 0.0, pltpu.roll(part[2 * chans :], width - 1, 1))
+    return silu(part[chans : 2 * chans] + before + after)
 
 
 def decode_pair(chans, height, band, planes, spread, store):
@@ -239,14 +275,12 @@
         for h in range(first, last + 1):
             piece = part[(h - first) * step : (h - first + 1) * step]
             sums[h] = piece if sums[h] is None else sums[h] + piece
-    lane = iota((chans, width), 1)
     for e in range(2):
         for h in range(height):
-            part = sums[h][:, e * width : (e + 1) * width]
-            before = jnp.where(lane == 0, 0.0, pltpu.roll(part[:chans], 1, 1))
-            after = jnp.where(lane == width - 1, 0.0, pltpu.roll(part[2 * chans :], width - 1, 1))
-            spread[e, pl.ds(h, chans, stride=height), :] = silu(part[chans : 2 * chans] + before + after)
-        store(e, spread[e].astype(BF16))
+            value = taps_of(chans, sums[h][:, e * width : (e + 1) * width])
+            spread[e, pl.ds(h, chans, stride=height), :] = value
+        store(e)
+    return sums
 
 
 def fill(field, slot, chans, plane, borders):
@@ -264,49 +298,39 @@
 
 
 def interior_kernel(chans, height, band, joined, *rest):
-    sides, (out_hbm, field, spread, held, sems) = rest[:-5], rest[-5:]
+    sides, (out, field, spread) = rest[:-3], rest[-3:]
     planes = joined.shape[0]
     for d in range(planes):
         fill(field, d, chans, joined[d], [side[d] for side in sides])
-    copies = []
     for step in range(planes // 2 - 1):
-        views = [
-            lambda h, at=(2 * step + e) * chans: field[h, at : at + 3 * chans] for e in range(2)
-        ]
-
-        def store(e, value):
-            held[2 * step + e] = value
+        views = [lambda h, at=(2 * step + e) * chans: field[h, at : at + 3 * chans] for e in range(2)]
+
+        def store(e):
+            out[2 * step + e] = spread[step, e].astype(BF16)
 
         decode_pair(chans, height, band, views, spread.at[step], store)
-        copies.append(
-            pltpu.make_async_copy(
-                held.at[2 * step : 2 * step + 2], out_hbm.at[2 * step + 1 : 2 * step + 3], sems.at[step]
-            )
-        )
-        copies[-1].start()
-    for copy in copies:
-        copy.wait()
-
-
-def nearby_kernel(chans, height, took, near, plane, corner, spread):
+
+
+def nearby_kernel(chans, height, took, near, far, plane, corners, spread):
     rows = plane.shape[0]
-    spread[...] = took[-rows:].astype(F32)
-    for h in range(height):
-        at = (h // 2) * chans
-        value = spread[pl.ds(h, chans, stride=height), :] + near[at : at + chans].astype(F32)
-        plane[h * chans : (h + 1) * chans] = value.astype(BF16)
-    corner[...] = plane[pl.ds(pl.multiple_of((rows - chans) * (1 - lax.axis_index("col")), chans), chans)]
-
-
-def edge_kernel(chans, height, band, joined, near, near_rows, far, far_rows, *rest):
-    sides, (mid_hbm, out_hbm, field, spread, held, sems) = rest[:-6], rest[-6:]
+
+    def store(at, value):
+        plane[at : at + chans] = value
+
+    join(chans, height, took[-rows:], near, spread, store)
+    start = pl.multiple_of((rows - chans) * (1 - lax.axis_index("col")), chans)
+    corners[:chans] = plane[pl.ds(start, chans)]
+    corners[chans:] = far[pl.ds(start, chans)]
+
+
+def fill_edges(chans, joined, near, far, sides, near_rows, far_rows, field):
     planes, _, width = joined.shape
     for slot, d in ((1, 0), (2, 1), (3, planes - 2), (4, planes - 1)):
         fill(field, slot, chans, joined[d], [side[d] for side in sides])
     row, last = lax.axis_index("row"), lax.axis_size("row") - 1
 
     def outer(slot, plane, corners):
-        fill(field, slot, chans, plane[...], [corners[k * chans : (k + 1) * chans] for k in range(len(sides))])
+        fill(field, slot, chans, plane[...], corners)
 
     @pl.when(row % 2 == 0)
     def _():
@@ -320,22 +344,85 @@
 
     @pl.when(row == 0)
     def _():
-        field[:, :chans] = jnp.zeros((height + 2, chans, width), BF16)
+        field[:, :chans] = jnp.zeros((field.shape[0], chans, width), BF16)
 
     @pl.when(row == last)
     def _():
-        field[:, 5 * chans :] = jnp.zeros((height + 2, chans, width), BF16)
-
-    copies = [
-        pltpu.make_async_copy(held.at[e], out_hbm.at[d], sems.at[e]) for e, d in ((0, 0), (1, planes - 1))
-    ]
-
-    def store(e, value):
-        held[e] = value
-        copies[e].start()
-
-    views = [lambda h, at=3 * e * chans: field[h, at : at + 3 * chans] for e in range(2)]
-    decode_pair(chans, height, band, views, spread, store)
+        field[:, 5 * chans :] = jnp.zeros((field.shape[0], chans, width), BF16)
+
+
+def edge_views(chans, field):
+    return [lambda h, at=3 * e * chans: field[h, at : at + 3 * chans] for e in range(2)]
+
+
+def result_copies(inner, held, out_hbm, sems):
+    last = out_hbm.shape[0] - 1
+    pieces = ((inner, out_hbm.at[1:last]), (held.at[0], out_hbm.at[0]), (held.at[1], out_hbm.at[last]))
+    return [pltpu.make_async_copy(piece, place, sems.at[k]) for k, (piece, place) in enumerate(pieces)]
+
+
+def edge_kernel(chans, height, band, joined, near, near_rows, far, far_rows, *rest):
+    sides, (inner, out_hbm, field, spread, held, sems) = rest[:-6], rest[-6:]
+    copies = result_copies(inner, held, out_hbm, sems)
+    copies[0].start()
+    borders = [[got[k * chans : (k + 1) * chans] for k in range(len(sides))] for got in (near_rows, far_rows)]
+    fill_edges(chans, joined, near, far, sides, *borders, field)
+
+    def store(e):
+        held[e] = spread[e].astype(BF16)
+        copies[1 + e].start()
+
+    decode_pair(chans, height, band, edge_views(chans, field), spread, store)
+    for copy in copies:
+        copy.wait()
+
+
+def early_edge_kernel(chans, height, band, joined, near, far, side, values, partial, field):
+    none = [jnp.zeros((chans, joined.shape[2]), BF16)]
+    fill_edges(chans, joined, near, far, [side], none, none, field)
+    sums = decode_pair(chans, height, band, edge_views(chans, field), values, lambda e: None)
+    partial[...] = jnp.where(lax.axis_index("col") == 0, sums[-1], sums[0])
+
+
+def late_edge_kernel(chans, height, band, corners, values, partial, inner, out_hbm, window, spread, held, sems):
+    copies = result_copies(inner, held, out_hbm, sems)
+    copies[0].start()
+    row, last, col = lax.axis_index("row"), lax.axis_size("row") - 1, lax.axis_index("col")
+    step, width = 3 * chans, corners.shape[1]
+    tile = window.shape[0]
+    at_tile = pl.multiple_of((height + 2) * step // tile * tile * (1 - col), tile)
+    at_row = (height + 1) * step % tile * (1 - col)
+    window[...] = jnp.zeros(window.shape, BF16)
+
+    def put(tap, got):
+        window[pl.ds(pl.multiple_of(at_row + tap * chans, chans), chans), tap // 2 * width : (tap // 2 + 1) * width] = got
+
+    even = row % 2 == 0
+
+    @pl.when((row > 0) & even)
+    def _():
+        put(0, corners[chans:])
+
+    @pl.when((row > 0) & ~even)
+    def _():
+        put(0, corners[:chans])
+
+    @pl.when((row < last) & even)
+    def _():
+        put(2, corners[:chans])
+
+    @pl.when((row < last) & ~even)
+    def _():
+        put(2, corners[chans:])
+
+    edge = (height - 1) * (1 - col)
+    kernel = band[pl.ds(pl.multiple_of(edge * step, step), step), pl.ds(at_tile, tile)]
+    sums = partial[...] + dot(kernel, window[...])
+    for e in range(2):
+        spread[e] = values[e]
+        spread[e, pl.ds(edge, chans, stride=height), :] = taps_of(chans, sums[:, e * width : (e + 1) * width])
+        held[e] = spread[e].astype(BF16)
+        copies[1 + e].start()
     for copy in copies:
         copy.wait()
 
@@ -397,7 +484,7 @@
             (bf16(2 * count, coarse // 2, 4 * each), bf16(taps, size), bf16(taps + rows, size)),
             [HBM] * 3,
             (VMEM,) * 3,
-            scratch + [sems(depth + 3)],
+            scratch + [sems(depth + 4)],
             cost=1_000_000_000,
         )(fixed(feat), fixed(down_weight), fixed(bott_weight.reshape(taps, top)))
         took = lax.ppermute(give, "row", [(i, i ^ 1) for i in range(count)])
@@ -417,7 +504,7 @@
             bf16(count, coarse, 3 * each),
             [HBM] * 2,
             VMEM,
-            scratch + [sems(depth)],
+            scratch + [sems(depth + 1)],
             cost=1_000_000_000,
         )(fixed(feat), fixed(down_weight))
         own = lax.all_to_all(lowered, "row", split_axis=0, concat_axis=0, tiled=True)
@@ -431,16 +518,23 @@
         )(lax.ppermute(own, "col", up_one), own, lax.ppermute(own, "col", down_one), bott_weight)
         parts = lax.all_to_all(shares, "row", split_axis=0, concat_axis=0, tiled=True)
 
-    side = bf16(depth + 2, chans, width)
     sides = 1 if cols == 2 else 2
-    joined, *ends = call(
+    wide, *ends = call(
+        functools.partial(outer_kernel, chans, height),
+        (bf16(4 * width, top), bf16(rows // 2 if paired else rows, width), bf16(rows, width)),
+        [VMEM] * 3,
+        (VMEM,) * 3,
+        [pltpu.VMEM((2, rows, width), F32)],
+        cost=1_000_000_000,
+    )(parts, feat, up_weight)
+    joined, *sides = call(
         functools.partial(raise_kernel, chans, height),
-        (bf16(depth, rows, width), bf16(rows // 2 if paired else rows, width), bf16(rows, width)) + (side,) * sides,
+        (bf16(depth, rows, width),) + (bf16(depth + (0 if paired else 2), chans, width),) * sides,
         [VMEM] * 3,
-        (VMEM,) * (3 + sides),
+        (VMEM,) * (1 + sides),
         [pltpu.VMEM(feat.shape, F32)],
-    )(parts, feat, up_weight)
-    ends, sides = ends[:2], ends[2:]
+        cost=1_000_000_000,
+    )(wide, feat, up_weight)
     if cols == 2:
         sides = [lax.ppermute(sides[0], "col", up_one + down_one)]
     else:
@@ -455,51 +549,62 @@
         cost=500_000_000,
     )(dec_weight, joined)
 
-    got = []
+    swapped = []
     for k, pairs in enumerate(neighbour_swaps(count, cols)):
-        alone = paired and k == 0
-        sent = ends[k] if alone else jnp.concatenate([ends[k]] + [side[depth + k] for side in sides], axis=0)
-        swapped = lax.ppermute(sent, ("row", "col"), pairs)
-        if alone:
-            plane, corner = call(
-                functools.partial(nearby_kernel, chans, height),
-                (bf16(rows, width), bf16(chans, width)),
-                [VMEM] * 2,
-                (VMEM,) * 2,
-                [pltpu.VMEM((rows, width), F32)],
-            )(took, swapped)
-            got += [plane, lax.ppermute(corner, "col", up_one + down_one)]
-        else:
-            got += [swapped[:rows], swapped[rows:]]
+        sent = ends[k] if paired else jnp.concatenate([ends[k]] + [side[depth + k] for side in sides], axis=0)
+        swapped.append(lax.ppermute(sent, ("row", "col"), pairs))
+    if paired:
+        plane, corners = call(
+            functools.partial(nearby_kernel, chans, height),
+            (bf16(rows, width), bf16(2 * chans, width)),
+            [VMEM] * 3,
+            (VMEM,) * 2,
+            [pltpu.VMEM((rows, width), F32)],
+        )(took, *swapped)
+        corners = lax.ppermute(corners, "col", up_one + down_one)
+    else:
+        got = [part for plane in swapped for part in (plane[:rows], plane[rows:])]
 
     shape = bf16(depth, rows, width)
     inner = call(
         functools.partial(interior_kernel, chans, height),
-        shape,
+        bf16(depth - 2, rows, width),
         [VMEM] * (2 + len(sides)),
-        HBM,
+        VMEM,
         [
             pltpu.VMEM((height + 2, depth * chans, width), BF16),
             pltpu.VMEM((depth // 2 - 1, 2, rows, width), F32),
-            pltpu.VMEM((depth - 2, rows, width), BF16),
-            sems(depth // 2 - 1),
         ],
         cost=3_000_000_000,
     )(band, joined, *sides)
-    decoded = call(
-        functools.partial(edge_kernel, chans, height),
-        shape,
-        [VMEM] * (6 + len(sides)) + [HBM],
-        HBM,
-        [
-            pltpu.VMEM((height + 2, 6 * chans, width), BF16),
-            pltpu.VMEM((2, rows, width), F32),
-            pltpu.VMEM((2, rows, width), BF16),
-            sems(2),
-        ],
-        aliases={6 + len(sides): 0},
-        cost=1_000_000_000,
-    )(band, joined, *got, *sides, inner)
+    field = pltpu.VMEM((height + 2, 6 * chans, width), BF16)
+    spread, held = pltpu.VMEM((2, rows, width), F32), pltpu.VMEM((2, rows, width), BF16)
+    if paired:
+        values, partial = call(
+            functools.partial(early_edge_kernel, chans, height),
+            (jax.ShapeDtypeStruct((2, rows, width), F32), jax.ShapeDtypeStruct((3 * chans, 2 * width), F32)),
+            [VMEM] * 5,
+            (VMEM,) * 2,
+            [field],
+            cost=1_000_000_000,
+        )(band, joined, plane, swapped[1], sides[0])
+        decoded = call(
+            functools.partial(late_edge_kernel, chans, height),
+            shape,
+            [VMEM] * 5,
+            HBM,
+            [pltpu.VMEM((256, 2 * width), BF16), spread, held, sems(3)],
+            cost=1_000_000_000,
+        )(band, corners, values, partial, inner)
+    else:
+        decoded = call(
+            functools.partial(edge_kernel, chans, height),
+            shape,
+            [VMEM] * (7 + len(sides)),
+            HBM,
+            [field, spread, held, sems(3)],
+            cost=1_000_000_000,
+        )(band, joined, *got, *sides, inner)
     return decoded.reshape(depth, chans, height, width)
 
 

time: 38.6 us -> 36.3 us (0.940)
  the two profiles are of different devices: /device:TPU:8 before, /device:TPU:0 now
where the time goes in v5:
time: 36.3 us; the launch traced here: 36.1 us
  blocking collectives  22.2 us (61%)
  Pallas kernels  6.8 us (19%)
  starting transfers between devices  5.44 us (15%)
  waiting for transfers between devices  1.64 us (5%)
    all_to_all x1, blocking collectives, level(): lax.all_to_all(lowered, ('row', 'col'), split_axis=0, concat_axis=0, tile...  12.1 us
    all_to_all x1, blocking collectives, level(): lax.all_to_all(shares, ('row', 'col'), split_axis=0, concat_axis=0, tiled...  10 us
    ppermute x1, starting transfers between devices, level(): took = lax.ppermute(give, 'row', [(i, i ^ 1) for i in range(count)])  3.03 us
    pallas_call x1, Pallas kernels, level(): call(functools.partial(lower_pair_kernel, count, chans, height), (bf16(2...  2.06 us
    ppermute x2, starting transfers between devices, level(): swapped.append(lax.ppermute(sent, ('row', 'col'), pairs))  1.98 us
    ppermute x2, waiting for transfers between devices, level(): swapped.append(lax.ppermute(sent, ('row', 'col'), pairs))  1.63 us
    pallas_call x1, Pallas kernels, level(): call(functools.partial(late_edge_kernel, chans, height), shape, [VMEM] *...  0.98 us
    pallas_call x1, Pallas kernels, level(): call(functools.partial(interior_kernel, chans, height), bf16(depth - 2, r...  0.94 us
  transfers between devices with their start and end apart: 5, of which 1 were waited for; matrix products, arithmetic and copies ran while one was open for 0% of the time, Pallas kernels for 8%

profile of v5, /device:TPU:0, one launch (start us, length us, event | category | flops | bytes accessed | tf_op | source)
XLA Modules:
  0.0 36.1 jit_solution(9595624128803170580)
XLA Ops:
  0.0 2.1 %shard_map.55 = (bf16[32,8,128]{2,1,0:T(8,128)(2,1)S(1)}, bf16[864,128]{1,0:T(8,128)(2,1)S(1)}, bf16[1120,128]{1,0:T(8,128)(2,1)S(1)}) custom-call(bf16[8,256,128]{2,1,0:T(8,128)(2,1)} %bitcast.5, bf16[4,4,4,32,512]{4,3,2,1,0:T(8,128)(2,1)} %down_hbm.1, bf16[864,512]{1,0:T(8,128)(2,1)} %bitcast.8), custom_call_target="tpu_custom_call" | custom-call | flops 1000000000 | bytes 10000000 | tf_op jit(solution)/shard_map/pallas_call | solution.py:482
  2.1 3.0 %collective-permute-start = (bf16[1120,128]{1,0:T(8,128)(2,1)S(1)}, bf16[1120,128]{1,0:T(8,128)(2,1)S(1)}, u32[]{:S(2)}, u32[]{:S(2)}) collective-permute-start(bf16[1120,128]{1,0:T(8,128)(2,1)S(1)} %get-tuple-element.19), channel_id=1, source_target_pairs={{0,2},{2,0},{4,6},{6,4},{8,10},{10,8},{12,14},{14,12},{16,18},{18,... | collective-permute-start | bytes 860168 | tf_op jit(solution)/shard_map/ppermute | solution.py:490
  5.1 12.1 %all_to_all.10 = bf16[32,8,128]{2,1,0:T(8,128)(2,1)S(1)} all-to-all(bf16[32,8,128]{2,1,0:T(8,128)(2,1)S(1)} %get-tuple-element.17), channel_id=1, replica_groups=mesh['row'=16,'col'=2] {'row','col'}, dimensions={0} | all-to-all | bytes 131072 | tf_op jit(solution)/shard_map/all_to_all | solution.py:491
  17.2 0.0 collective-permute-done.took
  17.2 0.0 copy-start.1
  17.2 0.0 copy-start.2
  17.2 0.4 %shard_map.56 = bf16[32,16,128]{2,1,0:T(8,128)(2,1)S(1)} custom-call(bf16[16,2,8,128]{3,2,1,0:T(8,128)(2,1)S(1)} %bitcast.4, bf16[864,128]{1,0:T(8,128)(2,1)S(1)} %get-tuple-element.18.keep, bf16[1120,128]{1,0:T(8,128)(2,1)S(1)} %collective-permute-done.took), custom_call_target="tpu_custom_call" | custom-call | flops 2000000000 | bytes 20000000 | tf_op jit(solution)/shard_map/pallas_call | solution.py:492
  17.7 10.0 %all_to_all.11.parts = bf16[32,16,128]{2,1,0:T(8,128)(2,1)S(1)} all-to-all(bf16[32,16,128]{2,1,0:T(8,128)(2,1)S(1)} %shard_map.56), channel_id=1, replica_groups=mesh['row'=16,'col'=2] {'row','col'}, dimensions={0} | all-to-all | bytes 262144 | tf_op jit(solution)/shard_map/all_to_all | solution.py:500
  27.7 0.0 copy-done.1
  27.7 0.0 copy-done.2
  27.7 0.5 %shard_map.57 = (bf16[512,512]{1,0:T(8,128)(2,1)S(1)}, bf16[128,128]{1,0:T(8,128)(2,1)S(1)}, bf16[256,128]{1,0:T(8,128)(2,1)S(1)}) custom-call(bf16[32,16,128]{2,1,0:T(8,128)(2,1)S(1)} %all_to_all.11.parts, bf16[8,256,128]{2,1,0:T(8,128)(2,1)S(1)} %bitcast.6, bf16[4,4,4,32,512]{4,3,2,1,0:T(8,128)(2,1)S(1)} %copy-done.1), custom_call_target="tpu_custom_call" | custom-call | flops 1000000000 | bytes 10000000 | tf_op jit(solution)/shard_map/pallas_call | solution.py:522
  28.2 0.0 copy-start
  28.2 0.3 collective-permute-start.2
  28.5 0.8 %shard_map.58 = (bf16[8,256,128]{2,1,0:T(8,128)(2,1)S(1)}, bf16[8,32,128]{2,1,0:T(8,128)(2,1)S(1)}) custom-call(bf16[512,512]{1,0:T(8,128)(2,1)S(1)} %get-tuple-element.20.wide, bf16[8,256,128]{2,1,0:T(8,128)(2,1)S(1)} %bitcast.7, bf16[4,4,4,32,512]{4,3,2,1,0:T(8,128)(2,1)S(1)} %copy-done.1), custom_call_target="tpu_custom_call" | custom-call | flops 1000000000 | bytes 10000000 | tf_op jit(solution)/shard_map/pallas_call | solution.py:530
  29.3 0.4 collective-permute-start.4
  29.6 1.7 %collective-permute-start.1 = (bf16[128,128]{1,0:T(8,128)(2,1)S(1)}, bf16[128,128]{1,0:T(8,128)(2,1)S(1)}, u32[]{:S(2)}, u32[]{:S(2)}) collective-permute-start(bf16[128,128]{1,0:T(8,128)(2,1)S(1)} %get-tuple-element.22), channel_id=1, source_target_pairs={{0,2},{1,3},{2,0},{3,1},{4,6},{5,7},{6,4},{7,5},{8,10},{9,11},{10,... | collective-permute-start | bytes 98312 | tf_op jit(solution)/shard_map/ppermute | solution.py:555
  31.3 0.0 copy-done
  31.3 0.6 %shard_map.59.band = bf16[768,1024]{1,0:T(8,128)(2,1)S(1)} custom-call(bf16[3,3,3,32,32]{4,3,2,1,0:T(8,128)(2,1)S(1)} %copy-done, bf16[8,256,128]{2,1,0:T(8,128)(2,1)S(1)} %get-tuple-element.21.after.joined), custom_call_target="tpu_custom_call" | custom-call | flops 500000000 | bytes 5000000 | tf_op jit(solution)/shard_map/pallas_call | solution.py:544
  31.9 1.6 %collective-permute-done.1.near = bf16[128,128]{1,0:T(8,128)(2,1)S(1)} collective-permute-done((bf16[128,128]{1,0:T(8,128)(2,1)S(1)}, bf16[128,128]{1,0:T(8,128)(2,1)S(1)}, u32[]{:S(2)}, u32[]{:S(2)}) %collective-permute-start.1) | collective-permute-done | bytes 32800 | tf_op jit(solution)/shard_map/ppermute | solution.py:555
  33.6 0.0 collective-permute-done.2.far
  33.6 0.1 collective-permute-start.3
  33.7 0.0 collective-permute-done.4.side.rest_0_
  33.7 0.9 %shard_map.62.inner = bf16[6,256,128]{2,1,0:T(8,128)(2,1)S(1)} custom-call(bf16[768,1024]{1,0:T(8,128)(2,1)S(1)} %shard_map.59.band, bf16[8,256,128]{2,1,0:T(8,128)(2,1)S(1)} %get-tuple-element.21.after.joined, bf16[8,32,128]{2,1,0:T(8,128)(2,1)S(1)} %collective-permute-done.4.side.rest_0_), custom_call_target="tpu_custom_call" | custom-call | flops 3000000000 | bytes 30000000 | tf_op jit(solution)/shard_map/pallas_call | solution.py:569
  34.6 0.5 %shard_map.61 = (f32[2,256,128]{2,1,0:T(8,128)S(1)}, f32[96,256]{1,0:T(8,128)S(1)}) custom-call(bf16[768,1024]{1,0:T(8,128)(2,1)S(1)} %shard_map.59.band, bf16[8,256,128]{2,1,0:T(8,128)(2,1)S(1)} %get-tuple-element.21.after.joined, bf16[256,128]{1,0:T(8,128)(2,1)S(1)} %get-tuple-element.25.near, bf16[256,128]{1,0:T(8,128)(2,1)S(1)} %collective-permute-done.2.far, ...), custom_call_target="tpu_custom_call" | custom-call | flops 1000000000 | bytes 10000000 | tf_op jit(solution)/shard_map/pallas_call | solution.py:583
  35.2 0.0 collective-permute-done.3.corners
  35.2 1.0 %shard_map.63 = bf16[8,256,128]{2,1,0:T(8,128)(2,1)} custom-call(bf16[768,1024]{1,0:T(8,128)(2,1)S(1)} %shard_map.59.band, bf16[64,128]{1,0:T(8,128)(2,1)S(1)} %collective-permute-done.3.corners, f32[2,256,128]{2,1,0:T(8,128)S(1)} %get-tuple-element.27.values, f32[96,256]{1,0:T(8,128)S(1)} %get-tuple-element.28.partial, bf16[6,256,128]{2,1,0:T(8,128)(2,1)S(1)} %shard_map.62.inner), custom_call_target="tpu_custom_call" | custom-call | flops 1000000000 | bytes 10000000 | tf_op jit(solution)/shard_map/pallas_call | solution.py:591
  (1 shorter events, 0.0 us)
Async XLA Ops:
  2.1 15.2 %collective-permute-start = (bf16[1120,128]{1,0:T(8,128)(2,1)S(1)}, bf16[1120,128]{1,0:T(8,128)(2,1)S(1)}, u32[]{:S(2)}, u32[]{:S(2)}) collective-permute-start(bf16[1120,128]{1,0:T(8,128)(2,1)S(1)} %get-tuple-element.19), channel_id=1, source_target_pairs={{0,2},{2,0},{4,6},{6,4},{8,10},{10,8},{12,14},{14,12},{16,18},{18,... | collective-permute-start | bytes 860168 | tf_op jit(solution)/shard_map/ppermute | solution.py:490
  17.2 10.5 %copy-start.1 = (bf16[4,4,4,32,512]{4,3,2,1,0:T(8,128)(2,1)S(1)}, bf16[4,4,4,32,512]{4,3,2,1,0:T(8,128)(2,1)}, u32[]{:S(2)}) copy-start(bf16[4,4,4,32,512]{4,3,2,1,0:T(8,128)(2,1)} %up.3) | copy-start | bytes 6291460
  17.2 10.5 %copy-start.2 = (bf16[8,32,8,128]{3,2,1,0:T(8,128)(2,1)S(1)}, bf16[8,32,8,128]{3,2,1,0:T(8,128)(2,1)}, u32[]{:S(2)}) copy-start(bf16[8,32,8,128]{3,2,1,0:T(8,128)(2,1)} %param.5) | copy-start | bytes 1572868
  28.2 3.1 %copy-start = (bf16[3,3,3,32,32]{4,3,2,1,0:T(8,128)(2,1)S(1)}, bf16[3,3,3,32,32]{4,3,2,1,0:T(8,128)(2,1)}, u32[]{:S(2)}) copy-start(bf16[3,3,3,32,32]{4,3,2,1,0:T(8,128)(2,1)} %dec.1) | copy-start | bytes 165892
  28.2 5.3 %collective-permute-start.2 = (bf16[256,128]{1,0:T(8,128)(2,1)S(1)}, bf16[256,128]{1,0:T(8,128)(2,1)S(1)}, u32[]{:S(2)}, u32[]{:S(2)}) collective-permute-start(bf16[256,128]{1,0:T(8,128)(2,1)S(1)} %get-tuple-element.23), channel_id=1, source_target_pairs={{0,1},{1,0},{2,4},{3,5},{4,2},{5,3},{6,8},{7,9},{8,6},{9,7},{10,12... | collective-permute-start | bytes 196616 | tf_op jit(solution)/shard_map/ppermute | solution.py:555
  29.3 4.4 %collective-permute-start.4 = (bf16[8,32,128]{2,1,0:T(8,128)(2,1)S(1)}, bf16[8,32,128]{2,1,0:T(8,128)(2,1)S(1)}, u32[]{:S(2)}, u32[]{:S(2)}) collective-permute-start(bf16[8,32,128]{2,1,0:T(8,128)(2,1)S(1)} %get-tuple-element.26), channel_id=1, source_target_pairs={{0,1},{1,0},{2,3},{3,2},{4,5},{5,4},{6,7},{7,6},{8,9},{9,8},{10,11... | collective-permute-start | bytes 196616 | tf_op jit(solution)/shard_map/ppermute | solution.py:539
  29.6 3.9 %collective-permute-start.1 = (bf16[128,128]{1,0:T(8,128)(2,1)S(1)}, bf16[128,128]{1,0:T(8,128)(2,1)S(1)}, u32[]{:S(2)}, u32[]{:S(2)}) collective-permute-start(bf16[128,128]{1,0:T(8,128)(2,1)S(1)} %get-tuple-element.22), channel_id=1, source_target_pairs={{0,2},{1,3},{2,0},{3,1},{4,6},{5,7},{6,4},{7,5},{8,10},{9,11},{10,... | collective-permute-start | bytes 98312 | tf_op jit(solution)/shard_map/ppermute | solution.py:555
  33.6 1.6 %collective-permute-start.3 = (bf16[64,128]{1,0:T(8,128)(2,1)S(1)}, bf16[64,128]{1,0:T(8,128)(2,1)S(1)}, u32[]{:S(2)}, u32[]{:S(2)}) collective-permute-start(bf16[64,128]{1,0:T(8,128)(2,1)S(1)} %get-tuple-element.24), channel_id=1, source_target_pairs={{0,1},{1,0},{2,3},{3,2},{4,5},{5,4},{6,7},{7,6},{8,9},{9,8},{10,11... | collective-permute-start | bytes 49160 | tf_op jit(solution)/shard_map/ppermute | solution.py:564

commit v6 on v5

--- a/solution.py
+++ b/solution.py
@@ -22,6 +22,11 @@
 
 def dot_nt(a, b):
     return lax.dot_general(a, b, NT, preferred_element_type=F32)
+
+
+def tiled(piece, shape):
+    rows, lanes = (size // part for size, part in zip(shape, piece.shape))
+    return jnp.concatenate([jnp.concatenate([piece] * lanes, axis=1)] * rows, axis=0)
 
 
 def silu(v):
@@ -141,7 +146,7 @@
         blocks.append(jnp.where(lane < group, low, pltpu.roll(high, group, 1)))
         blocks.append(jnp.where(lane < group, pltpu.roll(low, group, 1), high))
     here = jnp.concatenate(blocks, axis=0)
-    place = iota((rows, lanes), 0) % coarse
+    place = tiled(iota((coarse, lanes), 0), (rows, lanes))
     before = jnp.where(place == 0, 0.0, pltpu.roll(here, 1, 0))
     after = jnp.where(place == coarse - 1, 0.0, pltpu.roll(here, rows - 1, 0))
     zero = jnp.zeros((coarse, 3 * lanes), BF16)
@@ -185,13 +190,15 @@
         sums.append(total)
     middle = silu(sums[0] if groups == 1 else jnp.concatenate(sums, axis=1))
     spreading = jnp.concatenate([jnp.broadcast_to(middle[w : w + 1], (8, top)) for w in range(coarse)], axis=0)
-    which = iota(spreading.shape, 0) % 8 // 2
+    spreading = spreading.astype(BF16)
+    which = iota((16, 128), 0) % 8 // 2
+    masks = [tiled((which == c).astype(F32).astype(BF16), spreading.shape) for c in range(4)]
     odd = lax.axis_index("row") % 2
     last = up.shape[0] - 1
     steps = (last * (1 - odd), last * odd)
     raised = None
     for c in range(4):
-        columns = jnp.where(which == c, spreading, 0.0).astype(BF16)
+        columns = spreading * masks[c]
         wide[c * width : (c + 1) * width] = columns
         weight = jnp.concatenate([up[a, :, c].reshape(-1, top) for a in steps], axis=0)
         term = dot_nt(weight, columns)

time: 36.3 us -> 36.3 us (level)
  no operation moved by 1% of the time
where the time goes in v6:
time: 36.3 us; the launch traced here: 36.1 us
  blocking collectives  22.2 us (61%)
  Pallas kernels  6.77 us (19%)
  starting transfers between devices  5.43 us (15%)
  waiting for transfers between devices  1.65 us (5%)
    all_to_all x1, blocking collectives, level(): lax.all_to_all(lowered, ('row', 'col'), split_axis=0, concat_axis=0, tile...  12.1 us
    all_to_all x1, blocking collectives, level(): lax.all_to_all(shares, ('row', 'col'), split_axis=0, concat_axis=0, tiled...  10 us
    ppermute x1, starting transfers between devices, level(): took = lax.ppermute(give, 'row', [(i, i ^ 1) for i in range(count)])  3.03 us
    pallas_call x1, Pallas kernels, level(): call(functools.partial(lower_pair_kernel, count, chans, height), (bf16(2...  2.06 us
    ppermute x2, starting transfers between devices, level(): swapped.append(lax.ppermute(sent, ('row', 'col'), pairs))  1.97 us
    ppermute x2, waiting for transfers between devices, level(): swapped.append(lax.ppermute(sent, ('row', 'col'), pairs))  1.64 us
    pallas_call x1, Pallas kernels, level(): call(functools.partial(late_edge_kernel, chans, height), shape, [VMEM] *...  0.98 us
    pallas_call x1, Pallas kernels, level(): call(functools.partial(interior_kernel, chans, height), bf16(depth - 2, r...  0.94 us
  transfers between devices with their start and end apart: 5, of which 1 were waited for; matrix products, arithmetic and copies ran while one was open for 0% of the time, Pallas kernels for 8%

profile of v6, /device:TPU:0, one launch (start us, length us, event | category | flops | bytes accessed | tf_op | source)
XLA Modules:
  0.0 36.1 jit_solution(14931601091299596763)
XLA Ops:
  0.0 2.1 %shard_map.55 = (bf16[32,8,128]{2,1,0:T(8,128)(2,1)S(1)}, bf16[864,128]{1,0:T(8,128)(2,1)S(1)}, bf16[1120,128]{1,0:T(8,128)(2,1)S(1)}) custom-call(bf16[8,256,128]{2,1,0:T(8,128)(2,1)} %bitcast.5, bf16[4,4,4,32,512]{4,3,2,1,0:T(8,128)(2,1)} %down_hbm.1, bf16[864,512]{1,0:T(8,128)(2,1)} %bitcast.8), custom_call_target="tpu_custom_call" | custom-call | flops 1000000000 | bytes 10000000 | tf_op jit(solution)/shard_map/pallas_call | solution.py:489
  2.1 3.0 %collective-permute-start = (bf16[1120,128]{1,0:T(8,128)(2,1)S(1)}, bf16[1120,128]{1,0:T(8,128)(2,1)S(1)}, u32[]{:S(2)}, u32[]{:S(2)}) collective-permute-start(bf16[1120,128]{1,0:T(8,128)(2,1)S(1)} %get-tuple-element.19), channel_id=1, source_target_pairs={{0,2},{2,0},{4,6},{6,4},{8,10},{10,8},{12,14},{14,12},{16,18},{18,... | collective-permute-start | bytes 860168 | tf_op jit(solution)/shard_map/ppermute | solution.py:497
  5.1 12.1 %all_to_all.10 = bf16[32,8,128]{2,1,0:T(8,128)(2,1)S(1)} all-to-all(bf16[32,8,128]{2,1,0:T(8,128)(2,1)S(1)} %get-tuple-element.17), channel_id=1, replica_groups=mesh['row'=16,'col'=2] {'row','col'}, dimensions={0} | all-to-all | bytes 131072 | tf_op jit(solution)/shard_map/all_to_all | solution.py:498
  17.2 0.0 collective-permute-done.took
  17.2 0.0 copy-start.1
  17.2 0.0 copy-start.2
  17.2 0.4 %shard_map.56 = bf16[32,16,128]{2,1,0:T(8,128)(2,1)S(1)} custom-call(bf16[16,2,8,128]{3,2,1,0:T(8,128)(2,1)S(1)} %bitcast.4, bf16[864,128]{1,0:T(8,128)(2,1)S(1)} %get-tuple-element.18.keep, bf16[1120,128]{1,0:T(8,128)(2,1)S(1)} %collective-permute-done.took), custom_call_target="tpu_custom_call" | custom-call | flops 2000000000 | bytes 20000000 | tf_op jit(solution)/shard_map/pallas_call | solution.py:499
  17.7 10.0 %all_to_all.11.parts = bf16[32,16,128]{2,1,0:T(8,128)(2,1)S(1)} all-to-all(bf16[32,16,128]{2,1,0:T(8,128)(2,1)S(1)} %shard_map.56), channel_id=1, replica_groups=mesh['row'=16,'col'=2] {'row','col'}, dimensions={0} | all-to-all | bytes 262144 | tf_op jit(solution)/shard_map/all_to_all | solution.py:507
  27.7 0.0 copy-done.1
  27.7 0.0 copy-done.2
  27.7 0.5 %shard_map.57 = (bf16[512,512]{1,0:T(8,128)(2,1)S(1)}, bf16[128,128]{1,0:T(8,128)(2,1)S(1)}, bf16[256,128]{1,0:T(8,128)(2,1)S(1)}) custom-call(bf16[32,16,128]{2,1,0:T(8,128)(2,1)S(1)} %all_to_all.11.parts, bf16[8,256,128]{2,1,0:T(8,128)(2,1)S(1)} %bitcast.6, bf16[4,4,4,32,512]{4,3,2,1,0:T(8,128)(2,1)S(1)} %copy-done.1), custom_call_target="tpu_custom_call" | custom-call | flops 1000000000 | bytes 10000000 | tf_op jit(solution)/shard_map/pallas_call | solution.py:529
  28.2 0.0 copy-start
  28.2 0.3 collective-permute-start.2
  28.5 0.8 %shard_map.58 = (bf16[8,256,128]{2,1,0:T(8,128)(2,1)S(1)}, bf16[8,32,128]{2,1,0:T(8,128)(2,1)S(1)}) custom-call(bf16[512,512]{1,0:T(8,128)(2,1)S(1)} %get-tuple-element.20.wide, bf16[8,256,128]{2,1,0:T(8,128)(2,1)S(1)} %bitcast.7, bf16[4,4,4,32,512]{4,3,2,1,0:T(8,128)(2,1)S(1)} %copy-done.1), custom_call_target="tpu_custom_call" | custom-call | flops 1000000000 | bytes 10000000 | tf_op jit(solution)/shard_map/pallas_call | solution.py:537
  29.2 0.4 collective-permute-start.4
  29.6 1.7 %collective-permute-start.1 = (bf16[128,128]{1,0:T(8,128)(2,1)S(1)}, bf16[128,128]{1,0:T(8,128)(2,1)S(1)}, u32[]{:S(2)}, u32[]{:S(2)}) collective-permute-start(bf16[128,128]{1,0:T(8,128)(2,1)S(1)} %get-tuple-element.22), channel_id=1, source_target_pairs={{0,2},{1,3},{2,0},{3,1},{4,6},{5,7},{6,4},{7,5},{8,10},{9,11},{10,... | collective-permute-start | bytes 98312 | tf_op jit(solution)/shard_map/ppermute | solution.py:562
  31.3 0.0 copy-done
  31.3 0.6 %shard_map.59.band = bf16[768,1024]{1,0:T(8,128)(2,1)S(1)} custom-call(bf16[3,3,3,32,32]{4,3,2,1,0:T(8,128)(2,1)S(1)} %copy-done, bf16[8,256,128]{2,1,0:T(8,128)(2,1)S(1)} %get-tuple-element.21.after.joined), custom_call_target="tpu_custom_call" | custom-call | flops 500000000 | bytes 5000000 | tf_op jit(solution)/shard_map/pallas_call | solution.py:551
  31.9 1.6 %collective-permute-done.1.near = bf16[128,128]{1,0:T(8,128)(2,1)S(1)} collective-permute-done((bf16[128,128]{1,0:T(8,128)(2,1)S(1)}, bf16[128,128]{1,0:T(8,128)(2,1)S(1)}, u32[]{:S(2)}, u32[]{:S(2)}) %collective-permute-start.1) | collective-permute-done | bytes 32800 | tf_op jit(solution)/shard_map/ppermute | solution.py:562
  33.5 0.0 collective-permute-done.2.far
  33.6 0.1 collective-permute-start.3
  33.6 0.0 collective-permute-done.4.side.rest_0_
  33.7 0.9 %shard_map.62.inner = bf16[6,256,128]{2,1,0:T(8,128)(2,1)S(1)} custom-call(bf16[768,1024]{1,0:T(8,128)(2,1)S(1)} %shard_map.59.band, bf16[8,256,128]{2,1,0:T(8,128)(2,1)S(1)} %get-tuple-element.21.after.joined, bf16[8,32,128]{2,1,0:T(8,128)(2,1)S(1)} %collective-permute-done.4.side.rest_0_), custom_call_target="tpu_custom_call" | custom-call | flops 3000000000 | bytes 30000000 | tf_op jit(solution)/shard_map/pallas_call | solution.py:576
  34.6 0.5 %shard_map.61 = (f32[2,256,128]{2,1,0:T(8,128)S(1)}, f32[96,256]{1,0:T(8,128)S(1)}) custom-call(bf16[768,1024]{1,0:T(8,128)(2,1)S(1)} %shard_map.59.band, bf16[8,256,128]{2,1,0:T(8,128)(2,1)S(1)} %get-tuple-element.21.after.joined, bf16[256,128]{1,0:T(8,128)(2,1)S(1)} %get-tuple-element.25.near, bf16[256,128]{1,0:T(8,128)(2,1)S(1)} %collective-permute-done.2.far, ...), custom_call_target="tpu_custom_call" | custom-call | flops 1000000000 | bytes 10000000 | tf_op jit(solution)/shard_map/pallas_call | solution.py:590
  35.1 0.0 collective-permute-done.3.corners
  35.1 1.0 %shard_map.63 = bf16[8,256,128]{2,1,0:T(8,128)(2,1)} custom-call(bf16[768,1024]{1,0:T(8,128)(2,1)S(1)} %shard_map.59.band, bf16[64,128]{1,0:T(8,128)(2,1)S(1)} %collective-permute-done.3.corners, f32[2,256,128]{2,1,0:T(8,128)S(1)} %get-tuple-element.27.values, f32[96,256]{1,0:T(8,128)S(1)} %get-tuple-element.28.partial, bf16[6,256,128]{2,1,0:T(8,128)(2,1)S(1)} %shard_map.62.inner), custom_call_target="tpu_custom_call" | custom-call | flops 1000000000 | bytes 10000000 | tf_op jit(solution)/shard_map/pallas_call | solution.py:598
  (1 shorter events, 0.0 us)
Async XLA Ops:
  2.1 15.2 %collective-permute-start = (bf16[1120,128]{1,0:T(8,128)(2,1)S(1)}, bf16[1120,128]{1,0:T(8,128)(2,1)S(1)}, u32[]{:S(2)}, u32[]{:S(2)}) collective-permute-start(bf16[1120,128]{1,0:T(8,128)(2,1)S(1)} %get-tuple-element.19), channel_id=1, source_target_pairs={{0,2},{2,0},{4,6},{6,4},{8,10},{10,8},{12,14},{14,12},{16,18},{18,... | collective-permute-start | bytes 860168 | tf_op jit(solution)/shard_map/ppermute | solution.py:497
  17.2 10.5 %copy-start.1 = (bf16[4,4,4,32,512]{4,3,2,1,0:T(8,128)(2,1)S(1)}, bf16[4,4,4,32,512]{4,3,2,1,0:T(8,128)(2,1)}, u32[]{:S(2)}) copy-start(bf16[4,4,4,32,512]{4,3,2,1,0:T(8,128)(2,1)} %up.3) | copy-start | bytes 6291460
  17.2 10.5 %copy-start.2 = (bf16[8,32,8,128]{3,2,1,0:T(8,128)(2,1)S(1)}, bf16[8,32,8,128]{3,2,1,0:T(8,128)(2,1)}, u32[]{:S(2)}) copy-start(bf16[8,32,8,128]{3,2,1,0:T(8,128)(2,1)} %param.5) | copy-start | bytes 1572868
  28.2 3.1 %copy-start = (bf16[3,3,3,32,32]{4,3,2,1,0:T(8,128)(2,1)S(1)}, bf16[3,3,3,32,32]{4,3,2,1,0:T(8,128)(2,1)}, u32[]{:S(2)}) copy-start(bf16[3,3,3,32,32]{4,3,2,1,0:T(8,128)(2,1)} %dec.1) | copy-start | bytes 165892
  28.2 5.3 %collective-permute-start.2 = (bf16[256,128]{1,0:T(8,128)(2,1)S(1)}, bf16[256,128]{1,0:T(8,128)(2,1)S(1)}, u32[]{:S(2)}, u32[]{:S(2)}) collective-permute-start(bf16[256,128]{1,0:T(8,128)(2,1)S(1)} %get-tuple-element.23), channel_id=1, source_target_pairs={{0,1},{1,0},{2,4},{3,5},{4,2},{5,3},{6,8},{7,9},{8,6},{9,7},{10,12... | collective-permute-start | bytes 196616 | tf_op jit(solution)/shard_map/ppermute | solution.py:562
  29.2 4.4 %collective-permute-start.4 = (bf16[8,32,128]{2,1,0:T(8,128)(2,1)S(1)}, bf16[8,32,128]{2,1,0:T(8,128)(2,1)S(1)}, u32[]{:S(2)}, u32[]{:S(2)}) collective-permute-start(bf16[8,32,128]{2,1,0:T(8,128)(2,1)S(1)} %get-tuple-element.26), channel_id=1, source_target_pairs={{0,1},{1,0},{2,3},{3,2},{4,5},{5,4},{6,7},{7,6},{8,9},{9,8},{10,11... | collective-permute-start | bytes 196616 | tf_op jit(solution)/shard_map/ppermute | solution.py:546
  29.6 3.9 %collective-permute-start.1 = (bf16[128,128]{1,0:T(8,128)(2,1)S(1)}, bf16[128,128]{1,0:T(8,128)(2,1)S(1)}, u32[]{:S(2)}, u32[]{:S(2)}) collective-permute-start(bf16[128,128]{1,0:T(8,128)(2,1)S(1)} %get-tuple-element.22), channel_id=1, source_target_pairs={{0,2},{1,3},{2,0},{3,1},{4,6},{5,7},{6,4},{7,5},{8,10},{9,11},{10,... | collective-permute-start | bytes 98312 | tf_op jit(solution)/shard_map/ppermute | solution.py:562
  33.6 1.6 %collective-permute-start.3 = (bf16[64,128]{1,0:T(8,128)(2,1)S(1)}, bf16[64,128]{1,0:T(8,128)(2,1)S(1)}, u32[]{:S(2)}, u32[]{:S(2)}) collective-permute-start(bf16[64,128]{1,0:T(8,128)(2,1)S(1)} %get-tuple-element.24), channel_id=1, source_target_pairs={{0,1},{1,0},{2,3},{3,2},{4,5},{5,4},{6,7},{7,6},{8,9},{9,8},{10,11... | collective-permute-start | bytes 49160 | tf_op jit(solution)/shard_map/ppermute | solution.py:571

commit v7 on v6

--- a/solution.py
+++ b/solution.py
@@ -384,16 +384,21 @@
         copy.wait()
 
 
-def early_edge_kernel(chans, height, band, joined, near, far, side, values, partial, field):
+def early_edge_kernel(chans, height, band, joined, near, far, side, inner, values, partial, out_hbm, field, sems):
+    copy = pltpu.make_async_copy(inner, out_hbm.at[1 : out_hbm.shape[0] - 1], sems.at[0])
+    copy.start()
     none = [jnp.zeros((chans, joined.shape[2]), BF16)]
     fill_edges(chans, joined, near, far, [side], none, none, field)
     sums = decode_pair(chans, height, band, edge_views(chans, field), values, lambda e: None)
     partial[...] = jnp.where(lax.axis_index("col") == 0, sums[-1], sums[0])
-
-
-def late_edge_kernel(chans, height, band, corners, values, partial, inner, out_hbm, window, spread, held, sems):
-    copies = result_copies(inner, held, out_hbm, sems)
-    copies[0].start()
+    copy.wait()
+
+
+def late_edge_kernel(chans, height, band, corners, values, partial, mid_hbm, out_hbm, window, spread, held, sems):
+    copies = [
+        pltpu.make_async_copy(held.at[e], out_hbm.at[d], sems.at[e])
+        for e, d in ((0, 0), (1, out_hbm.shape[0] - 1))
+    ]
     row, last, col = lax.axis_index("row"), lax.axis_size("row") - 1, lax.axis_index("col")
     step, width = 3 * chans, corners.shape[1]
     tile = window.shape[0]
@@ -429,7 +434,7 @@
         spread[e] = values[e]
         spread[e, pl.ds(edge, chans, stride=height), :] = taps_of(chans, sums[:, e * width : (e + 1) * width])
         held[e] = spread[e].astype(BF16)
-        copies[1 + e].start()
+        copies[e].start()
     for copy in copies:
         copy.wait()
 
@@ -587,20 +592,21 @@
     field = pltpu.VMEM((height + 2, 6 * chans, width), BF16)
     spread, held = pltpu.VMEM((2, rows, width), F32), pltpu.VMEM((2, rows, width), BF16)
     if paired:
-        values, partial = call(
+        values, partial, inner = call(
             functools.partial(early_edge_kernel, chans, height),
-            (jax.ShapeDtypeStruct((2, rows, width), F32), jax.ShapeDtypeStruct((3 * chans, 2 * width), F32)),
-            [VMEM] * 5,
-            (VMEM,) * 2,
-            [field],
+            (jax.ShapeDtypeStruct((2, rows, width), F32), jax.ShapeDtypeStruct((3 * chans, 2 * width), F32), shape),
+            [VMEM] * 6,
+            (VMEM, VMEM, HBM),
+            [field, sems(1)],
             cost=1_000_000_000,
-        )(band, joined, plane, swapped[1], sides[0])
+        )(band, joined, plane, swapped[1], sides[0], inner)
         decoded = call(
             functools.partial(late_edge_kernel, chans, height),
             shape,
-            [VMEM] * 5,
+            [VMEM] * 4 + [HBM],
             HBM,
-            [pltpu.VMEM((256, 2 * width), BF16), spread, held, sems(3)],
+            [pltpu.VMEM((256, 2 * width), BF16), spread, held, sems(2)],
+            aliases={4: 0},
             cost=1_000_000_000,
         )(band, corners, values, partial, inner)
     else:

time: 36.3 us -> 36.5 us (level)
  no operation moved by 1% of the time
where the time goes in v7:
time: 36.5 us; the launch traced here: 36.4 us
  blocking collectives  22.2 us (61%)
  Pallas kernels  7.01 us (19%)
  starting transfers between devices  5.43 us (15%)
  waiting for transfers between devices  1.65 us (5%)
    all_to_all x1, blocking collectives, level(): lax.all_to_all(lowered, ('row', 'col'), split_axis=0, concat_axis=0, tile...  12.1 us
    all_to_all x1, blocking collectives, level(): lax.all_to_all(shares, ('row', 'col'), split_axis=0, concat_axis=0, tiled...  10 us
    ppermute x1, starting transfers between devices, level(): took = lax.ppermute(give, 'row', [(i, i ^ 1) for i in range(count)])  3.03 us
    pallas_call x1, Pallas kernels, level(): call(functools.partial(lower_pair_kernel, count, chans, height), (bf16(2...  2.06 us
    ppermute x2, starting transfers between devices, level(): swapped.append(lax.ppermute(sent, ('row', 'col'), pairs))  1.97 us
    ppermute x2, waiting for transfers between devices, level(): swapped.append(lax.ppermute(sent, ('row', 'col'), pairs))  1.64 us
    pallas_call x1, Pallas kernels, level(): call(functools.partial(late_edge_kernel, chans, height), shape, [VMEM] *...  0.97 us
    pallas_call x1, Pallas kernels, level(): call(functools.partial(interior_kernel, chans, height), bf16(depth - 2, r...  0.94 us
  transfers between devices with their start and end apart: 5, of which 1 were waited for; matrix products, arithmetic and copies ran while one was open for 0% of the time, Pallas kernels for 8%

profile of v7, /device:TPU:0, one launch (start us, length us, event | category | flops | bytes accessed | tf_op | source)
XLA Modules:
  0.0 36.4 jit_solution(11222939365599408633)
XLA Ops:
  0.0 2.1 %shard_map.55 = (bf16[32,8,128]{2,1,0:T(8,128)(2,1)S(1)}, bf16[864,128]{1,0:T(8,128)(2,1)S(1)}, bf16[1120,128]{1,0:T(8,128)(2,1)S(1)}) custom-call(bf16[8,256,128]{2,1,0:T(8,128)(2,1)} %bitcast.5, bf16[4,4,4,32,512]{4,3,2,1,0:T(8,128)(2,1)} %down_hbm.1, bf16[864,512]{1,0:T(8,128)(2,1)} %bitcast.8), custom_call_target="tpu_custom_call" | custom-call | flops 1000000000 | bytes 10000000 | tf_op jit(solution)/shard_map/pallas_call | solution.py:494
  2.1 3.0 %collective-permute-start = (bf16[1120,128]{1,0:T(8,128)(2,1)S(1)}, bf16[1120,128]{1,0:T(8,128)(2,1)S(1)}, u32[]{:S(2)}, u32[]{:S(2)}) collective-permute-start(bf16[1120,128]{1,0:T(8,128)(2,1)S(1)} %get-tuple-element.20), channel_id=1, source_target_pairs={{0,2},{2,0},{4,6},{6,4},{8,10},{10,8},{12,14},{14,12},{16,18},{18,... | collective-permute-start | bytes 860168 | tf_op jit(solution)/shard_map/ppermute | solution.py:502
  5.1 12.1 %all_to_all.10 = bf16[32,8,128]{2,1,0:T(8,128)(2,1)S(1)} all-to-all(bf16[32,8,128]{2,1,0:T(8,128)(2,1)S(1)} %get-tuple-element.18), channel_id=1, replica_groups=mesh['row'=16,'col'=2] {'row','col'}, dimensions={0} | all-to-all | bytes 131072 | tf_op jit(solution)/shard_map/all_to_all | solution.py:503
  17.2 0.0 collective-permute-done.took
  17.2 0.0 copy-start.1
  17.2 0.0 copy-start.2
  17.2 0.4 %shard_map.56 = bf16[32,16,128]{2,1,0:T(8,128)(2,1)S(1)} custom-call(bf16[16,2,8,128]{3,2,1,0:T(8,128)(2,1)S(1)} %bitcast.4, bf16[864,128]{1,0:T(8,128)(2,1)S(1)} %get-tuple-element.19.keep, bf16[1120,128]{1,0:T(8,128)(2,1)S(1)} %collective-permute-done.took), custom_call_target="tpu_custom_call" | custom-call | flops 2000000000 | bytes 20000000 | tf_op jit(solution)/shard_map/pallas_call | solution.py:504
  17.7 10.0 %all_to_all.11.parts = bf16[32,16,128]{2,1,0:T(8,128)(2,1)S(1)} all-to-all(bf16[32,16,128]{2,1,0:T(8,128)(2,1)S(1)} %shard_map.56), channel_id=1, replica_groups=mesh['row'=16,'col'=2] {'row','col'}, dimensions={0} | all-to-all | bytes 262144 | tf_op jit(solution)/shard_map/all_to_all | solution.py:512
  27.7 0.0 copy-done.1
  27.7 0.0 copy-done.2
  27.7 0.5 %shard_map.57 = (bf16[512,512]{1,0:T(8,128)(2,1)S(1)}, bf16[128,128]{1,0:T(8,128)(2,1)S(1)}, bf16[256,128]{1,0:T(8,128)(2,1)S(1)}) custom-call(bf16[32,16,128]{2,1,0:T(8,128)(2,1)S(1)} %all_to_all.11.parts, bf16[8,256,128]{2,1,0:T(8,128)(2,1)S(1)} %bitcast.6, bf16[4,4,4,32,512]{4,3,2,1,0:T(8,128)(2,1)S(1)} %copy-done.1), custom_call_target="tpu_custom_call" | custom-call | flops 1000000000 | bytes 10000000 | tf_op jit(solution)/shard_map/pallas_call | solution.py:534
  28.2 0.0 copy-start
  28.2 0.3 collective-permute-start.2
  28.5 0.8 %shard_map.58 = (bf16[8,256,128]{2,1,0:T(8,128)(2,1)S(1)}, bf16[8,32,128]{2,1,0:T(8,128)(2,1)S(1)}) custom-call(bf16[512,512]{1,0:T(8,128)(2,1)S(1)} %get-tuple-element.21.wide, bf16[8,256,128]{2,1,0:T(8,128)(2,1)S(1)} %bitcast.7, bf16[4,4,4,32,512]{4,3,2,1,0:T(8,128)(2,1)S(1)} %copy-done.1), custom_call_target="tpu_custom_call" | custom-call | flops 1000000000 | bytes 10000000 | tf_op jit(solution)/shard_map/pallas_call | solution.py:542
  29.2 0.4 collective-permute-start.4
  29.6 1.7 %collective-permute-start.1 = (bf16[128,128]{1,0:T(8,128)(2,1)S(1)}, bf16[128,128]{1,0:T(8,128)(2,1)S(1)}, u32[]{:S(2)}, u32[]{:S(2)}) collective-permute-start(bf16[128,128]{1,0:T(8,128)(2,1)S(1)} %get-tuple-element.23), channel_id=1, source_target_pairs={{0,2},{1,3},{2,0},{3,1},{4,6},{5,7},{6,4},{7,5},{8,10},{9,11},{10,... | collective-permute-start | bytes 98312 | tf_op jit(solution)/shard_map/ppermute | solution.py:567
  31.3 0.0 copy-done
  31.3 0.6 %shard_map.59.band = bf16[768,1024]{1,0:T(8,128)(2,1)S(1)} custom-call(bf16[3,3,3,32,32]{4,3,2,1,0:T(8,128)(2,1)S(1)} %copy-done, bf16[8,256,128]{2,1,0:T(8,128)(2,1)S(1)} %get-tuple-element.22.after.joined), custom_call_target="tpu_custom_call" | custom-call | flops 500000000 | bytes 5000000 | tf_op jit(solution)/shard_map/pallas_call | solution.py:556
  31.9 1.6 %collective-permute-done.1.near = bf16[128,128]{1,0:T(8,128)(2,1)S(1)} collective-permute-done((bf16[128,128]{1,0:T(8,128)(2,1)S(1)}, bf16[128,128]{1,0:T(8,128)(2,1)S(1)}, u32[]{:S(2)}, u32[]{:S(2)}) %collective-permute-start.1) | collective-permute-done | bytes 32800 | tf_op jit(solution)/shard_map/ppermute | solution.py:567
  33.5 0.0 collective-permute-done.2.far
  33.6 0.1 collective-permute-start.3
  33.6 0.0 collective-permute-done.4.rest_0_.side
  33.7 0.9 %shard_map.61.inner = bf16[6,256,128]{2,1,0:T(8,128)(2,1)S(1)} custom-call(bf16[768,1024]{1,0:T(8,128)(2,1)S(1)} %shard_map.59.band, bf16[8,256,128]{2,1,0:T(8,128)(2,1)S(1)} %get-tuple-element.22.after.joined, bf16[8,32,128]{2,1,0:T(8,128)(2,1)S(1)} %collective-permute-done.4.rest_0_.side), custom_call_target="tpu_custom_call" | custom-call | flops 3000000000 | bytes 30000000 | tf_op jit(solution)/shard_map/pallas_call | solution.py:581
  34.6 0.8 %shard_map.62 = (f32[2,256,128]{2,1,0:T(8,128)S(1)}, f32[96,256]{1,0:T(8,128)S(1)}, bf16[8,256,128]{2,1,0:T(8,128)(2,1)}) custom-call(bf16[768,1024]{1,0:T(8,128)(2,1)S(1)} %shard_map.59.band, bf16[8,256,128]{2,1,0:T(8,128)(2,1)S(1)} %get-tuple-element.22.after.joined, bf16[256,128]{1,0:T(8,128)(2,1)S(1)} %get-tuple-element.26.near, ...), custom_call_target="tpu_custom_call" | custom-call | flops 1000000000 | bytes 10000000 | tf_op jit(solution)/shard_map/pallas_call | solution.py:595
  35.4 0.0 collective-permute-done.3.corners
  35.4 1.0 %shard_map.63 = bf16[8,256,128]{2,1,0:T(8,128)(2,1)} custom-call(bf16[768,1024]{1,0:T(8,128)(2,1)S(1)} %shard_map.59.band, bf16[64,128]{1,0:T(8,128)(2,1)S(1)} %collective-permute-done.3.corners, f32[2,256,128]{2,1,0:T(8,128)S(1)} %get-tuple-element.28.values, f32[96,256]{1,0:T(8,128)S(1)} %get-tuple-element.29.partial, ...), custom_call_target="tpu_custom_call", output_to_operand_aliasing={{}: (4, {})} | custom-call | flops 1000000000 | bytes 10000000 | tf_op jit(solution)/shard_map/pallas_call | solution.py:603
  (1 shorter events, 0.0 us)
Async XLA Ops:
  2.1 15.2 %collective-permute-start = (bf16[1120,128]{1,0:T(8,128)(2,1)S(1)}, bf16[1120,128]{1,0:T(8,128)(2,1)S(1)}, u32[]{:S(2)}, u32[]{:S(2)}) collective-permute-start(bf16[1120,128]{1,0:T(8,128)(2,1)S(1)} %get-tuple-element.20), channel_id=1, source_target_pairs={{0,2},{2,0},{4,6},{6,4},{8,10},{10,8},{12,14},{14,12},{16,18},{18,... | collective-permute-start | bytes 860168 | tf_op jit(solution)/shard_map/ppermute | solution.py:502
  17.2 10.5 %copy-start.1 = (bf16[4,4,4,32,512]{4,3,2,1,0:T(8,128)(2,1)S(1)}, bf16[4,4,4,32,512]{4,3,2,1,0:T(8,128)(2,1)}, u32[]{:S(2)}) copy-start(bf16[4,4,4,32,512]{4,3,2,1,0:T(8,128)(2,1)} %up.3) | copy-start | bytes 6291460
  17.2 10.5 %copy-start.2 = (bf16[8,32,8,128]{3,2,1,0:T(8,128)(2,1)S(1)}, bf16[8,32,8,128]{3,2,1,0:T(8,128)(2,1)}, u32[]{:S(2)}) copy-start(bf16[8,32,8,128]{3,2,1,0:T(8,128)(2,1)} %param.5) | copy-start | bytes 1572868
  28.2 3.1 %copy-start = (bf16[3,3,3,32,32]{4,3,2,1,0:T(8,128)(2,1)S(1)}, bf16[3,3,3,32,32]{4,3,2,1,0:T(8,128)(2,1)}, u32[]{:S(2)}) copy-start(bf16[3,3,3,32,32]{4,3,2,1,0:T(8,128)(2,1)} %dec.1) | copy-start | bytes 165892
  28.2 5.3 %collective-permute-start.2 = (bf16[256,128]{1,0:T(8,128)(2,1)S(1)}, bf16[256,128]{1,0:T(8,128)(2,1)S(1)}, u32[]{:S(2)}, u32[]{:S(2)}) collective-permute-start(bf16[256,128]{1,0:T(8,128)(2,1)S(1)} %get-tuple-element.24), channel_id=1, source_target_pairs={{0,1},{1,0},{2,4},{3,5},{4,2},{5,3},{6,8},{7,9},{8,6},{9,7},{10,12... | collective-permute-start | bytes 196616 | tf_op jit(solution)/shard_map/ppermute | solution.py:567
  29.2 4.4 %collective-permute-start.4 = (bf16[8,32,128]{2,1,0:T(8,128)(2,1)S(1)}, bf16[8,32,128]{2,1,0:T(8,128)(2,1)S(1)}, u32[]{:S(2)}, u32[]{:S(2)}) collective-permute-start(bf16[8,32,128]{2,1,0:T(8,128)(2,1)S(1)} %get-tuple-element.27), channel_id=1, source_target_pairs={{0,1},{1,0},{2,3},{3,2},{4,5},{5,4},{6,7},{7,6},{8,9},{9,8},{10,11... | collective-permute-start | bytes 196616 | tf_op jit(solution)/shard_map/ppermute | solution.py:551
  29.6 3.9 %collective-permute-start.1 = (bf16[128,128]{1,0:T(8,128)(2,1)S(1)}, bf16[128,128]{1,0:T(8,128)(2,1)S(1)}, u32[]{:S(2)}, u32[]{:S(2)}) collective-permute-start(bf16[128,128]{1,0:T(8,128)(2,1)S(1)} %get-tuple-element.23), channel_id=1, source_target_pairs={{0,2},{1,3},{2,0},{3,1},{4,6},{5,7},{6,4},{7,5},{8,10},{9,11},{10,... | collective-permute-start | bytes 98312 | tf_op jit(solution)/shard_map/ppermute | solution.py:567
  33.6 1.8 %collective-permute-start.3 = (bf16[64,128]{1,0:T(8,128)(2,1)S(1)}, bf16[64,128]{1,0:T(8,128)(2,1)S(1)}, u32[]{:S(2)}, u32[]{:S(2)}) collective-permute-start(bf16[64,128]{1,0:T(8,128)(2,1)S(1)} %get-tuple-element.25), channel_id=1, source_target_pairs={{0,1},{1,0},{2,3},{3,2},{4,5},{5,4},{6,7},{7,6},{8,9},{9,8},{10,11... | collective-permute-start | bytes 49160 | tf_op jit(solution)/shard_map/ppermute | solution.py:576
